TPU v7x, 32 devices: a whole 2x2x4 slice. The times are simulated.
32 devices in a mesh: dp: 8 (over z, x), tensor: 4 (over y, core).
Axes of the slice: x: 2, y: 2, z: 4, core: 2. Of those that a mesh axis runs over, the one named last changes fastest.
Arguments:
- tokens: bfloat16 [16384, 1024], P('dp'), may hold values from -6 to 6
- segments: int32 [16, 1024], P('dp'), may hold values from 0 to 7, never falling along the last dimension, each value on 1 to 512 neighbouring positions
- w_qkv: bfloat16 [1024, 3, 1024], P(None, None, 'tensor'), may hold values from -0.1875 to 0.1875
- head_bias: float32 [2, 1024], P(None, 'tensor'), may hold values from -3 to 3
- w_out: bfloat16 [1024, 1024], P('tensor'), may hold values from -0.75 to 0.75
- w_in: bfloat16 [1024, 4096], P(None, 'tensor'), may hold values from -0.1875 to 0.1875
- unit_bias: float32 [4096], P('tensor'), may hold values from -3 to 3
- w_down: bfloat16 [4096, 1024], P('tensor'), may hold values from -0.09375 to 0.09375
- vectors: float32 [6, 1024], replicated, may hold values from 0.5 to 1.5
- cotangent: bfloat16 [16384, 1024], P('dp'), may hold values from -6 to 6
- err_qkv: float32 [8, 1024, 3, 1024], P('dp', None, None, 'tensor'), may hold values from -80 to 80
- err_out: float32 [8, 1024, 1024], P('dp', 'tensor'), may hold values from -80 to 80
- err_in: float32 [8, 1024, 4096], P('dp', None, 'tensor'), may hold values from -80 to 80
- err_down: float32 [8, 4096, 1024], P('dp', 'tensor'), may hold values from -80 to 80
- basis_qkv: float32 [8, 3, 1024], P(None, None, 'tensor'), may hold values from -6 to 6
- basis_out: float32 [32, 1024], P('tensor'), may hold values from -6 to 6
- basis_in: float32 [8, 4096], P(None, 'tensor'), may hold values from -6 to 6
- basis_down: float32 [32, 1024], P('tensor'), may hold values from -6 to 6
- mom_qkv: float32 [1024, 3, 1024], P(None, None, 'tensor'), may hold values from -5 to 5
- mom_head_bias: float32 [2, 1024], P(None, 'tensor'), may hold values from -10 to 10
- mom_out: float32 [1024, 1024], P('tensor'), may hold values from -5 to 5
- mom_in: float32 [1024, 4096], P(None, 'tensor'), may hold values from -5 to 5
- mom_unit_bias: float32 [4096], P('tensor'), may hold values from -10 to 10
- mom_down: float32 [4096, 1024], P('tensor'), may hold values from -5 to 5
- mom_vectors: float32 [6, 1024], replicated, may hold values from -28 to 28
Outputs:
- layer_out: bfloat16 [16384, 1024], P(('dp', 'tensor'))
- grad_tokens: float32 [16384, 1024], P(('dp', 'tensor'))
- grad_w_qkv: float32 [1024, 3, 1024], P(None, None, 'tensor')
- grad_head_bias: float32 [2, 1024], P(None, 'tensor')
- grad_w_out: float32 [1024, 1024], P('tensor')
- grad_w_in: float32 [1024, 4096], P(None, 'tensor')
- grad_unit_bias: float32 [4096], P('tensor')
- grad_w_down: float32 [4096, 1024], P('tensor')
- grad_vectors: float32 [6, 1024], replicated
- new_err_qkv: float32 [8, 1024, 3, 1024], P('dp', None, None, 'tensor')
- new_err_out: float32 [8, 1024, 1024], P('dp', 'tensor')
- new_err_in: float32 [8, 1024, 4096], P('dp', None, 'tensor')
- new_err_down: float32 [8, 4096, 1024], P('dp', 'tensor')
- new_basis_qkv: float32 [8, 3, 1024], P(None, None, 'tensor')
- new_basis_out: float32 [32, 1024], P('tensor')
- new_basis_in: float32 [8, 4096], P(None, 'tensor')
- new_basis_down: float32 [32, 1024], P('tensor')
- new_mom_qkv: float32 [1024, 3, 1024], P(None, None, 'tensor')
- new_mom_head_bias: float32 [2, 1024], P(None, 'tensor')
- new_mom_out: float32 [1024, 1024], P('tensor')
- new_mom_in: float32 [1024, 4096], P(None, 'tensor')
- new_mom_unit_bias: float32 [4096], P('tensor')
- new_mom_down: float32 [4096, 1024], P('tensor')
- new_mom_vectors: float32 [6, 1024], replicated
- new_w_qkv: float32 [1024, 3, 1024], P(None, None, 'tensor')
- new_head_bias: float32 [2, 1024], P(None, 'tensor')
- new_w_out: float32 [1024, 1024], P('tensor')
- new_w_in: float32 [1024, 4096], P(None, 'tensor')
- new_unit_bias: float32 [4096], P('tensor')
- new_w_down: float32 [4096, 1024], P('tensor')
- new_vectors: float32 [6, 1024], replicated
Inputs may be any that keep to these rules, and one draw needn't show every extreme that they name: `segments`: along a sequence the numbers never fall; each of its 8 documents holds 1 to 512 tokens, and one of them exactly 512.
All inputs are finite; a program needn't handle non-finite values.
Results may differ from a plain program's by a relative error of at most 0.02.
Values may be sent and summed in bfloat16 or wider, within the bound.
A program may use at most 256 MiB of HBM per device.

v0:
```python
from functools import partial
import math

import jax
import jax.numpy as jnp
from jax import lax
from jax.sharding import PartitionSpec as P

DH = 64


PRECISE = lax.Precision.HIGHEST
EPS_NORM = 1e-05
EPS_BASIS = 1e-08
MASKED = -1000000000.0


def norm_forward(values, gain, shift):
    row_mean = jnp.mean(values, axis=-1, keepdims=True)
    centred = values - row_mean
    variance = jnp.mean(centred * centred, axis=-1, keepdims=True)
    inverse = lax.rsqrt(variance + EPS_NORM)
    normed = centred * inverse
    return (normed * gain + shift, normed, inverse)


def norm_backward(grad_norm, normed, inverse, gain):
    scaled_grad = grad_norm * gain
    grad_mean = jnp.mean(scaled_grad, axis=-1, keepdims=True)
    along_norm = jnp.mean(scaled_grad * normed, axis=-1, keepdims=True)
    return inverse * (scaled_grad - grad_mean - normed * along_norm)


def times_trans(left_side, right_side):
    return lax.dot_general(
        left_side, right_side, (((1,), (1,)), ((), ())), preferred_element_type=jnp.float32
    )


def trans_times(left_side, right_side):
    return lax.dot_general(
        left_side, right_side, (((0,), (0,)), ((), ())), preferred_element_type=jnp.float32
    )


def left_of(matrix, factor):
    return lax.dot_general(
        matrix,
        factor,
        (((1,), (1,)), ((), ())),
        precision=PRECISE,
        preferred_element_type=jnp.float32,
    )


def right_of(basis, matrix):
    return lax.dot_general(
        basis,
        matrix,
        (((0,), (0,)), ((), ())),
        precision=PRECISE,
        preferred_element_type=jnp.float32,
    )


def orthonormal(factor):
    columns = []
    for position in range(factor.shape[-1]):
        column = factor[..., position]
        for earlier in columns:
            column = column - jnp.sum(earlier * column, axis=-1, keepdims=True) * earlier
        column = column / (jnp.sqrt(jnp.sum(column * column, axis=-1, keepdims=True)) + EPS_BASIS)
        columns.append(column)
    return jnp.stack(columns, axis=-1)


def masked_scores(queries, key_heads, seg_ids):
    scores = jnp.einsum("qhd,khd->hqk", queries, key_heads, preferred_element_type=jnp.float32)
    same_doc = seg_ids[:, None] == seg_ids[None, :]
    return jnp.where(same_doc[None], scores, MASKED)


def attend_forward(inputs_of):
    queries, key_heads, value_heads, seg_ids = inputs_of
    scores = masked_scores(queries, key_heads, seg_ids)
    highest = jnp.max(scores, axis=-1, keepdims=True)
    powers = jnp.exp(scores - highest)
    denominator = jnp.sum(powers, axis=-1, keepdims=True)
    weights = (powers / denominator).astype(jnp.bfloat16)
    mixed_heads = jnp.einsum(
        "hqk,khd->qhd", weights, value_heads, preferred_element_type=jnp.float32
    )
    return (mixed_heads.astype(jnp.bfloat16), highest[..., 0] + jnp.log(denominator[..., 0]))


def attend_backward(inputs_of):
    queries, key_heads, value_heads, seg_ids, grad_mixed, log_total = inputs_of
    scores = masked_scores(queries, key_heads, seg_ids)
    probability = jnp.exp(scores - log_total[..., None])
    grad_probs = jnp.einsum(
        "qhd,khd->hqk", grad_mixed, value_heads, preferred_element_type=jnp.float32
    )
    centre = jnp.sum(probability * grad_probs, axis=-1, keepdims=True)
    grad_scores = (probability * (grad_probs - centre)).astype(jnp.bfloat16)
    grad_query = jnp.einsum(
        "hqk,khd->qhd", grad_scores, key_heads, preferred_element_type=jnp.float32
    )
    grad_key = jnp.einsum("hqk,qhd->khd", grad_scores, queries, preferred_element_type=jnp.float32)
    grad_value = jnp.einsum(
        "hqk,qhd->khd",
        probability.astype(jnp.bfloat16),
        grad_mixed,
        preferred_element_type=jnp.float32,
    )
    return (
        grad_query.astype(jnp.bfloat16),
        grad_key.astype(jnp.bfloat16),
        grad_value.astype(jnp.bfloat16),
    )


def local(
    tokens,
    segments,
    w_qkv,
    head_bias,
    w_out,
    w_in,
    unit_bias,
    w_down,
    vectors,
    cotangent,
    err_qkv,
    err_out,
    err_in,
    err_down,
    basis_qkv,
    basis_out,
    basis_in,
    basis_down,
    mom_qkv,
    mom_head_bias,
    mom_out,
    mom_in,
    mom_unit_bias,
    mom_down,
    mom_vectors,
):
    token_count, model_width = tokens.shape
    seq_count, length = segments.shape
    head_slab = w_qkv.shape[2]
    head_count = head_slab // DH
    unit_slab = w_in.shape[1]
    rank_size = basis_in.shape[0]
    tensor_size = lax.axis_size("tensor")
    replicas = lax.axis_size("dp")
    share_rows = token_count // tensor_size
    tensor_place = lax.axis_index("tensor")
    row_start = tensor_place * share_rows
    head_scale = 1.0 / math.sqrt(DH)

    def own_rows(values):
        return lax.dynamic_slice_in_dim(values, row_start, share_rows, 0)

    flat_qkv = w_qkv.reshape(model_width, 3 * head_slab)
    projected = jnp.dot(tokens, flat_qkv, preferred_element_type=jnp.float32).reshape(
        token_count, 3, head_slab
    )
    head_shape = (seq_count, length, head_count, DH)
    queries = (
        ((projected[:, 0] + head_bias[0]) * head_scale).astype(jnp.bfloat16).reshape(head_shape)
    )
    key_heads = projected[:, 1].astype(jnp.bfloat16).reshape(head_shape)
    value_heads = (projected[:, 2] + head_bias[1]).astype(jnp.bfloat16).reshape(head_shape)
    mixed_heads, log_total = lax.map(attend_forward, (queries, key_heads, value_heads, segments))
    mixed_flat = mixed_heads.reshape(token_count, head_slab)
    attn_out = (
        lax.psum(jnp.dot(mixed_flat, w_out, preferred_element_type=jnp.float32), "tensor")
        + vectors[0]
    )
    first_norm, first_normed, first_inverse = norm_forward(
        tokens.astype(jnp.float32) + attn_out, vectors[2], vectors[3]
    )
    first_low = first_norm.astype(jnp.bfloat16)
    hidden = jnp.dot(first_low, w_in, preferred_element_type=jnp.float32) + unit_bias
    active, gelu_back = jax.vjp(partial(jax.nn.gelu, approximate=False), hidden)
    active_low = active.astype(jnp.bfloat16)
    grad_out_share = own_rows(cotangent).astype(jnp.float32)
    summed_input = (
        first_norm
        + lax.psum(jnp.dot(active_low, w_down, preferred_element_type=jnp.float32), "tensor")
        + vectors[1]
    )
    second_norm, second_normed, second_inverse = norm_forward(summed_input, vectors[4], vectors[5])
    layer_out = own_rows(second_norm).astype(jnp.bfloat16)
    grad_sum = norm_backward(
        cotangent.astype(jnp.float32), second_normed, second_inverse, vectors[4]
    )
    grad_branch = grad_sum.astype(jnp.bfloat16)
    second_share = own_rows(second_normed)
    grad_w_down = trans_times(active_low, grad_branch)
    grad_active = times_trans(grad_branch, w_down)
    grad_hidden = gelu_back(grad_active)[0].astype(jnp.bfloat16)
    grad_w_in = trans_times(first_low, grad_hidden)
    grad_units = jnp.sum(grad_hidden.astype(jnp.float32), axis=0)
    grad_first = lax.psum(times_trans(grad_hidden, w_in), "tensor") + grad_sum
    grad_h1 = norm_backward(grad_first, first_normed, first_inverse, vectors[2])
    grad_attn = grad_h1.astype(jnp.bfloat16)
    grad_first_share = own_rows(grad_first)
    first_normed_share = own_rows(first_normed)
    grad_h1_share = own_rows(grad_h1)
    grad_w_out = trans_times(mixed_flat, grad_attn)
    grad_mixed = times_trans(grad_attn, w_out).astype(jnp.bfloat16).reshape(head_shape)
    grad_query, grad_key, grad_value = lax.map(
        attend_backward, (queries, key_heads, value_heads, segments, grad_mixed, log_total)
    )
    grad_query = (
        grad_query.reshape(token_count, head_slab).astype(jnp.float32) * head_scale
    ).astype(jnp.bfloat16)
    grad_key = grad_key.reshape(token_count, head_slab)
    grad_value = grad_value.reshape(token_count, head_slab)
    grad_projected = jnp.stack([grad_query, grad_key, grad_value], axis=1).reshape(
        token_count, 3 * head_slab
    )
    grad_w_qkv = trans_times(tokens, grad_projected)
    grad_heads = jnp.stack(
        [
            jnp.sum(grad_query.astype(jnp.float32), axis=0),
            jnp.sum(grad_value.astype(jnp.float32), axis=0),
        ]
    )
    grad_tokens = (
        lax.psum_scatter(
            times_trans(grad_projected, flat_qkv).astype(jnp.bfloat16),
            "tensor",
            scatter_dimension=0,
            tiled=True,
        ).astype(jnp.float32)
        + grad_h1_share
    )
    local_vectors = jnp.stack(
        [
            jnp.sum(own_rows(grad_attn).astype(jnp.float32), axis=0),
            jnp.sum(own_rows(grad_branch).astype(jnp.float32), axis=0),
            jnp.sum(grad_first_share * first_normed_share, axis=0),
            jnp.sum(grad_first_share, axis=0),
            jnp.sum(grad_out_share * second_share, axis=0),
            jnp.sum(grad_out_share, axis=0),
        ]
    )
    zero_index = jnp.zeros((), jnp.int32)
    head_full = lax.dynamic_update_slice(
        jnp.zeros((2, head_slab * tensor_size), jnp.float32),
        grad_heads,
        (zero_index, tensor_place * head_slab),
    )
    unit_full = lax.dynamic_update_slice(
        jnp.zeros((unit_slab * tensor_size,), jnp.float32), grad_units, (tensor_place * unit_slab,)
    )
    vector_sum, head_sum, unit_sum = lax.psum(
        (local_vectors, head_full, unit_full), ("dp", "tensor")
    )
    grad_vectors = vector_sum / replicas
    grad_head_bias = (
        lax.dynamic_slice_in_dim(head_sum, tensor_place * head_slab, head_slab, 1) / replicas
    )
    grad_unit_bias = (
        lax.dynamic_slice_in_dim(unit_sum, tensor_place * unit_slab, unit_slab, 0) / replicas
    )
    combined_qkv = grad_w_qkv + err_qkv[0].reshape(model_width, 3 * head_slab)
    combined_out = grad_w_out + err_out[0]
    combined_in = grad_w_in + err_in[0]
    combined_down = grad_w_down + err_down[0]
    left_qkv, left_out, left_in, left_down = (
        lax.psum(
            left_of(combined_qkv, basis_qkv.reshape(rank_size, 3 * head_slab)).astype(jnp.bfloat16),
            "dp",
        ).astype(jnp.float32),
        lax.psum(left_of(combined_out, basis_out).astype(jnp.bfloat16), "dp").astype(jnp.float32),
        lax.psum(left_of(combined_in, basis_in).astype(jnp.bfloat16), "dp").astype(jnp.float32),
        lax.psum(left_of(combined_down, basis_down).astype(jnp.bfloat16), "dp").astype(jnp.float32),
    )
    ortho_qkv = orthonormal(left_qkv / replicas)
    ortho_out = orthonormal(left_out / replicas)
    ortho_in = orthonormal(left_in / replicas)
    ortho_down = orthonormal(left_down / replicas)
    right_qkv, right_out, right_in, right_down = (
        lax.psum(right_of(ortho_qkv, combined_qkv).astype(jnp.bfloat16), "dp").astype(jnp.float32),
        lax.psum(right_of(ortho_out, combined_out).astype(jnp.bfloat16), "dp").astype(jnp.float32),
        lax.psum(right_of(ortho_in, combined_in).astype(jnp.bfloat16), "dp").astype(jnp.float32),
        lax.psum(right_of(ortho_down, combined_down).astype(jnp.bfloat16), "dp").astype(
            jnp.float32
        ),
    )
    right_qkv = right_qkv / replicas
    right_out = right_out / replicas
    right_in = right_in / replicas
    right_down = right_down / replicas
    rank_qkv = jnp.dot(ortho_qkv, right_qkv, precision=PRECISE)
    rank_out = jnp.dot(ortho_out, right_out, precision=PRECISE)
    rank_in = jnp.dot(ortho_in, right_in, precision=PRECISE)
    rank_down = jnp.dot(ortho_down, right_down, precision=PRECISE)
    reduced_qkv = rank_qkv.reshape(model_width, 3, head_slab)
    new_err_qkv = (combined_qkv - rank_qkv).reshape(1, model_width, 3, head_slab)
    new_err_out = (combined_out - rank_out)[None]
    new_err_in = (combined_in - rank_in)[None]
    new_err_down = (combined_down - rank_down)[None]
    new_basis_qkv = right_qkv.reshape(rank_size, 3, head_slab)
    step_rate = 0.3 * math.sqrt(replicas / token_count)
    new_mom_qkv = 0.9 * mom_qkv + reduced_qkv
    new_mom_head_bias = 0.9 * mom_head_bias + grad_head_bias
    new_mom_out = 0.9 * mom_out + rank_out
    new_mom_in = 0.9 * mom_in + rank_in
    new_mom_unit_bias = 0.9 * mom_unit_bias + grad_unit_bias
    new_mom_down = 0.9 * mom_down + rank_down
    new_mom_vectors = 0.9 * mom_vectors + grad_vectors
    new_w_qkv = w_qkv.astype(jnp.float32) - step_rate * new_mom_qkv
    new_head_bias = head_bias - step_rate * new_mom_head_bias
    new_w_out = w_out.astype(jnp.float32) - step_rate * new_mom_out
    new_w_in = w_in.astype(jnp.float32) - step_rate * new_mom_in
    new_unit_bias = unit_bias - step_rate * new_mom_unit_bias
    new_w_down = w_down.astype(jnp.float32) - step_rate * new_mom_down
    new_vectors = vectors - step_rate * new_mom_vectors
    return (
        layer_out,
        grad_tokens,
        reduced_qkv,
        grad_head_bias,
        rank_out,
        rank_in,
        grad_unit_bias,
        rank_down,
        grad_vectors,
        new_err_qkv,
        new_err_out,
        new_err_in,
        new_err_down,
        new_basis_qkv,
        right_out,
        right_in,
        right_down,
        new_mom_qkv,
        new_mom_head_bias,
        new_mom_out,
        new_mom_in,
        new_mom_unit_bias,
        new_mom_down,
        new_mom_vectors,
        new_w_qkv,
        new_head_bias,
        new_w_out,
        new_w_in,
        new_unit_bias,
        new_w_down,
        new_vectors,
    )


def solution(mesh):
    in_specs = (
        P("dp", None),
        P("dp", None),
        P(None, None, "tensor"),
        P(None, "tensor"),
        P("tensor", None),
        P(None, "tensor"),
        P("tensor"),
        P("tensor", None),
        P(),
        P("dp", None),
        P("dp", None, None, "tensor"),
        P("dp", "tensor", None),
        P("dp", None, "tensor"),
        P("dp", "tensor", None),
        P(None, None, "tensor"),
        P("tensor", None),
        P(None, "tensor"),
        P("tensor", None),
        P(None, None, "tensor"),
        P(None, "tensor"),
        P("tensor", None),
        P(None, "tensor"),
        P("tensor"),
        P("tensor", None),
        P(),
    )
    out_specs = (
        P(("dp", "tensor"), None),
        P(("dp", "tensor"), None),
        P(None, None, "tensor"),
        P(None, "tensor"),
        P("tensor", None),
        P(None, "tensor"),
        P("tensor"),
        P("tensor", None),
        P(),
        P("dp", None, None, "tensor"),
        P("dp", "tensor", None),
        P("dp", None, "tensor"),
        P("dp", "tensor", None),
        P(None, None, "tensor"),
        P("tensor", None),
        P(None, "tensor"),
        P("tensor", None),
        P(None, None, "tensor"),
        P(None, "tensor"),
        P("tensor", None),
        P(None, "tensor"),
        P("tensor"),
        P("tensor", None),
        P(),
        P(None, None, "tensor"),
        P(None, "tensor"),
        P("tensor", None),
        P(None, "tensor"),
        P("tensor"),
        P("tensor", None),
        P(),
    )
    return jax.shard_map(local, mesh=mesh, in_specs=in_specs, out_specs=out_specs, check_vma=False)
```

profile of v0, /device:TPU:0, one launch (start us, length us, event | category | flops | bytes accessed | tf_op | source)
XLA Modules:
  0.0 1268.2 jit_solution(10177957480828531079)
XLA Ops:
  9.0 5.3 fusion.62
  21.6 5.1 reshape.517
  44.9 51.5 %while.26 = (s32[]{:T(128)}, bf16[2,1024,4,64]{1,3,2,0:T(8,128)(2,1)}, f32[2,4,1024]{2,1,0:T(4,128)S(1)}, bf16[2,1024,4,64]{1,3,2,0:T(8,128)(2,1)}, s32[2,1024]{...) while((s32[]{:T(128)}, ...), condition=%wide.region_3.4_spmd, body=%wide.region_0.3_spmd.sunk | while | flops 1112797184 | bytes 56768612 | solution.py:175
  45.8 7.3 select_reduce_fusion.2
  53.1 8.8 fusion.154
  61.8 8.9 fusion.155
  71.4 7.3 select_reduce_fusion.2
  78.7 8.8 fusion.154
  87.5 8.9 fusion.155
  100.7 5.6 fusion.87
  106.4 155.6 %all-reduce.7.cloned.1.call-done = f32[2048,1024]{1,0:T(8,128)} async-done(((f32[2048,1024]{1,0:T(8,128)}), f32[2048,1024]{1,0:T(8,128)}) %all-reduce.7.cloned.1.call-update) | async-done | bytes 8388624 | tf_op jit(solution)/shard_map/psum | solution.py:178
  262.0 5.9 fusion.64
  274.1 24.4 %multiply_convert_fusion.1 = (bf16[2048,1024]{1,0:T(8,128)(2,1)S(1)}, f32[2048,1024]{1,0:T(8,128)}, f32[2048,1024]{1,0:T(8,128)}) fusion(f32[1024]{0:T(1024)S(1)} %copy-done.65, bf16[1024,1024]{1,0:T(8,128)(2,1)S(1)} %copy-done.37, f32[2048,1024]{1,0:T(8,128)S(1)} %subtract_multiply_fusion.3, f32[1024]{0:T(1024)S(1)} %bitcast.353, f32[1024]{0:T(1024)S(1)} %bitcast.281), kind=kOutput, calls=%fused_computation.74 | convolution fusion | flops 4439670784 | bytes 31469568 | tf_op jit(solution)/shard_map/dot_general | solution.py:185
  300.6 6.6 fusion.88
  307.3 153.1 %all-reduce.9.cloned.1.call-done = f32[2048,1024]{1,0:T(8,128)} async-done(((f32[2048,1024]{1,0:T(8,128)}), f32[2048,1024]{1,0:T(8,128)}) %all-reduce.9.cloned.1.call-update) | async-done | bytes 8388624 | tf_op jit(solution)/shard_map/psum | solution.py:191
  460.4 6.7 fusion.78
  475.8 13.2 %convert_reduce_fusion = (f32[1024]{0:T(1024)S(1)}, bf16[2048,1024]{1,0:T(8,128)(2,1)S(1)}) fusion(f32[2048,1024]{1,0:T(8,128)} %get-tuple-element.569, f32[2048,1024]{1,0:T(8,128)} %get-tuple-element.620, f32[1024]{0:T(1024)S(1)} %copy-done.65, bf16[2048,1024]{1,0:T(8,128)(2,1)S(1)} %fusion.74, bf16[1024,1024]{1,0:T(8,128)(2,1)S(1)} %copy-done.39), kind=kOutput, calls=%fused_computation.64 | convolution fusion | flops 4330617856 | bytes 27271168 | tf_op jit(solution)/shard_map/dot_general | solution.py:35
  491.0 6.9 fusion.89
  507.6 9.5 bitcast_add_fusion
  534.4 116.7 %all-reduce.11.cloned.1.call-done = f32[2048,1024]{1,0:T(8,128)} async-done(((f32[2048,1024]{1,0:T(8,128)}), f32[2048,1024]{1,0:T(8,128)}) %all-reduce.11.cloned.1.call-update) | async-done | bytes 8388624 | tf_op jit(solution)/shard_map/psum | solution.py:206
  651.1 11.4 multiply_reduce_fusion.5
  662.6 9.5 fusion.76
  685.4 95.2 %while.27 = (s32[]{:T(128)}, bf16[2,1024,4,64]{1,3,2,0:T(8,128)(2,1)}, bf16[2,1024,4,64]{1,3,2,0:T(8,128)(2,1)}, bf16[2,1024,4,64]{1,3,2,0:T(8,128)(2,1)}, bf16[...) while((s32[]{:T(128)}, ...), condition=%wide.region_17.18_spmd, body=%wide.region_15.17_spmd.sunk | while | flops 2736517120 | bytes 219284944 | solution.py:214
  686.6 9.5 fusion.164
  696.1 8.9 fusion.167
  705.0 14.7 %multiply_reduce_fusion.152 = (f32[4,1024]{1,0:T(4,128)S(1)}, f32[4,1024,1024]{1,2,0:T(8,128)}) fusion(f32[4,1024,1024]{1,2,0:T(8,128)} %fusion.164, f32[4,1024]{1,0:T(4,128)S(1)} %dynamic-slice_bitcast_fusion.2, pred[1024,1024]{0,1:T(8,128)(4,1)} %copy-done.2, bf16[2,1024,4,64]{1,3,2,0:T(8,128)(2,1)} %get-tuple-element.793, s32[]{:T(128)S(6)} %copy.165, ...), kind=kOutput, calls=%fused_computation.22.clone.1 | convolution fusion | flops 553644032 | bytes 35685376 | tf_op jit(solution)/shard_map/while/body/eval_jaxpr/qhd,khd->hqk/dot_general | solution.py:100
  719.7 8.2 multiply_convert_fusion.5
  734.0 9.5 fusion.164
  743.5 8.9 fusion.167
  752.4 14.7 %multiply_reduce_fusion.152 = (f32[4,1024]{1,0:T(4,128)S(1)}, f32[4,1024,1024]{1,2,0:T(8,128)}) fusion(f32[4,1024,1024]{1,2,0:T(8,128)} %fusion.164, f32[4,1024]{1,0:T(4,128)S(1)} %dynamic-slice_bitcast_fusion.2, pred[1024,1024]{0,1:T(8,128)(4,1)} %copy-done.2, bf16[2,1024,4,64]{1,3,2,0:T(8,128)(2,1)} %get-tuple-element.793, s32[]{:T(128)S(6)} %copy.165, ...), kind=kOutput, calls=%fused_computation.22.clone.1 | convolution fusion | flops 553644032 | bytes 35685376 | tf_op jit(solution)/shard_map/while/body/eval_jaxpr/qhd,khd->hqk/dot_general | solution.py:100
  767.1 8.2 multiply_convert_fusion.5
  808.4 7.1 bitcast_convert_fusion
  820.4 7.5 bitcast_add_fusion.2
  829.6 37.9 %all-reduce.2 = (bf16[1024,8]{0,1:T(8,128)(2,1)S(1)}, bf16[256,8]{0,1:T(8,128)(2,1)S(1)}, bf16[1024,8]{0,1:T(8,128)(2,1)S(1)}, bf16[1024,8]{0,1:T(8,128)(2,1)S(1)}) all-reduce(bf16[1024,8]{0,1:T(8,128)(2,1)S(1)} %convolution_convert_fusion.8, ...), channel_id=1, replica_groups=mesh['dp'=8,'tensor'=4] {'dp'}, use_global_device_ids=true, to_apply=%region_19.20 | all-reduce | flops 26624 | bytes 106496 | tf_op jit(solution)/shard_map/psum | solution.py:275
  880.9 6.3 multiply_reduce_fusion.120
  913.5 5.2 multiply_reduce_fusion.85
  923.2 6.4 multiply_reduce_fusion.84
  968.7 6.2 multiply_reduce_fusion.48
  1003.7 5.0 multiply_reduce_fusion.13
  1013.1 6.3 multiply_reduce_fusion.12
  1045.2 17.5 %subtract_divide_fusion.21 = (f32[256,1]{0,1:T(1,128)S(1)}, f32[256,1]{0,1:T(1,128)S(1)}, f32[256,1]{0,1:T(1,128)S(1)}, f32[256,1]{0,1:T(1,128)S(1)}, f32[256,1]...) fusion(f32[256,1]{0,1:T(1,128)S(1)} %get-tuple-element.613, f32[]{:T(128)S(6)} %add.371, ...), kind=kLoop, calls=%fused_computation.402 | loop fusion | flops 16128 | bytes 15500 | tf_op jit(solution)/shard_map/div | solution.py:72
  1062.7 18.2 %subtract_divide_fusion.14 = (f32[1024,1]{0,1:T(1,128)S(1)}, f32[1024,1]{0,1:T(1,128)S(1)}, f32[1024,1]{0,1:T(1,128)S(1)}, f32[1024,1]{0,1:T(1,128)S(1)}, f32[10...) fusion(f32[1024,1]{0,1:T(1,128)S(1)} %get-tuple-element.599, f32[]{:T(128)S(6)} %add.361, ...), kind=kLoop, calls=%fused_computation.300 | loop fusion | flops 64512 | bytes 61580 | tf_op jit(solution)/shard_map/div | solution.py:72
  1081.0 17.4 %subtract_divide_fusion.7 = (f32[1024,1]{0,1:T(1,128)S(1)}, f32[1024,1]{0,1:T(1,128)S(1)}, f32[1024,1]{0,1:T(1,128)S(1)}, f32[1024,1]{0,1:T(1,128)S(1)}, f32[102...) fusion(f32[1024,1]{0,1:T(1,128)S(1)} %get-tuple-element.591, f32[]{:T(128)S(6)} %add.380, ...), kind=kLoop, calls=%fused_computation.230 | loop fusion | flops 64512 | bytes 61580 | tf_op jit(solution)/shard_map/div | solution.py:72
  1098.4 17.5 %subtract_divide_fusion = (f32[1024,1]{0,1:T(1,128)S(1)}, f32[1024,1]{0,1:T(1,128)S(1)}, f32[1024,1]{0,1:T(1,128)S(1)}, f32[1024,1]{0,1:T(1,128)S(1)}, f32[1024,...) fusion(f32[1024,1]{0,1:T(1,128)S(1)} %get-tuple-element.583, f32[]{:T(128)S(6)} %add.390, ...), kind=kLoop, calls=%fused_computation.159 | loop fusion | flops 64512 | bytes 61580 | tf_op jit(solution)/shard_map/div | solution.py:72
  1127.0 33.7 %all-reduce.1 = (bf16[8,768]{1,0:T(8,128)(2,1)S(1)}, bf16[8,1024]{1,0:T(8,128)(2,1)S(1)}, bf16[8,1024]{1,0:T(8,128)(2,1)S(1)}, bf16[8,1024]{1,0:T(8,128)(2,1)S(1)}) all-reduce(bf16[8,768]{1,0:T(8,128)(2,1)S(1)} %convolution_convert_fusion.9, ...), channel_id=1, replica_groups=mesh['dp'=8,'tensor'=4] {'dp'}, use_global_device_ids=true, to_apply=%region_56.57 | all-reduce | flops 30720 | bytes 122880 | tf_op jit(solution)/shard_map/psum | solution.py:288
  1177.1 37.7 %all-reduce = (f32[2,1024]{1,0:T(2,128)S(1)}, f32[4096]{0:T(1024)S(1)}, f32[6,1024]{1,0:T(8,128)S(1)}) all-reduce(f32[2,1024]{1,0:T(2,128)S(1)} %constant_dynamic-update-slice_fusion.3, f32[4096]{0:T(1024)S(1)} %copy-done.56, f32[6,1024]{1,0:T(8,128)S(1)} %stack.44), channel_id=1, replica_groups=mesh['dp'=8,'tensor'=4] {'dp','tensor'}, use_global_device_ids=true, to_apply=%region_59.60 | all-reduce | flops 12288 | bytes 98304 | tf_op jit(solution)/shard_map/psum | solution.py:260
  1233.9 12.2 multiply_subtract_fusion.1
  1246.1 11.5 multiply_subtract_fusion
  (360 shorter events, 308.8 us)
Async XLA Ops:
  7.2 511.8 %copy-start = (f32[8,1024]{1,0:T(8,128)S(1)}, f32[8,1024]{1,0:T(8,128)}, u32[]{:S(2)}) copy-start(f32[8,1024]{1,0:T(8,128)} %param.46) | copy-start | bytes 98308
  7.2 254.8 %all-reduce.7.cloned.1.call-start = ((), (), s32[]{:S(2)}) async-start(), calls=%async_computation.1 | async-start | bytes 16777216 | tf_op jit(solution)/shard_map/psum | solution.py:178
  31.4 13.5 %copy-start.44 = (s32[2,1024]{1,0:T(2,128)S(1)}, s32[2,1024]{1,0:T(2,128)}, u32[]{:S(2)}) copy-start(s32[2,1024]{1,0:T(2,128)} %param.30) | copy-start | bytes 24580
  106.3 354.1 %all-reduce.9.cloned.1.call-start = ((), (), s32[]{:S(2)}) async-start(), calls=%async_computation.2 | async-start | bytes 16777216 | tf_op jit(solution)/shard_map/psum | solution.py:191
  274.0 24.5 %copy-start.3 = (f32[2048,1024]{1,0:T(8,128)}, f32[2048,1024]{1,0:T(8,128)S(1)}, u32[]{:S(2)}) copy-start(f32[2048,1024]{1,0:T(8,128)S(1)} %subtract_multiply_fusion.3) | copy-start | bytes 25165828
  274.1 26.4 %copy-start.38 = (bf16[1024,1024]{1,0:T(8,128)(2,1)S(1)}, bf16[1024,1024]{1,0:T(8,128)(2,1)}, u32[]{:S(2)}) copy-start(bf16[1024,1024]{1,0:T(8,128)(2,1)} %param.36) | copy-start | bytes 6291460
  307.2 343.9 %all-reduce.11.cloned.1.call-start = ((), (), s32[]{:S(2)}) async-start(), calls=%async_computation.3 | async-start | bytes 16777216 | tf_op jit(solution)/shard_map/psum | solution.py:206
  475.8 13.2 %copy-start.17 = (bf16[2048,1024]{1,0:T(8,128)(2,1)}, bf16[2048,1024]{1,0:T(8,128)(2,1)S(1)}, u32[]{:S(2)}) copy-start(bf16[2048,1024]{1,0:T(8,128)(2,1)S(1)} %fusion.74) | copy-start | bytes 12582916
  498.0 759.6 %reduce-scatter.2.cloned.1.call-start = ((), (), s32[]{:S(2)}) async-start(), calls=%async_computation.4 | async-start | bytes 5242880 | tf_op jit(solution)/shard_map/reduce_scatter | solution.py:233
  503.1 20.1 %slice-start.4 = ((s8[8388608]{0:T(1024)(128)(4,1)}), s8[4194304]{0:T(1024)(128)(4,1)S(1)}, s32[]{:S(2)}) async-start(s8[8388608]{0:T(1024)(128)(4,1)} %bitcast.240), calls=%async_computation.9 | async-start | bytes 8388608
  507.6 15.6 %slice-start.5 = ((s8[8388608]{0:T(1024)(128)(4,1)}), s8[4194304]{0:T(1024)(128)(4,1)S(1)}, s32[]{:S(2)}) async-start(s8[8388608]{0:T(1024)(128)(4,1)} %bitcast.240), calls=%async_computation.10 | async-start | bytes 8388608
  507.6 15.6 %copy-start.69 = (f32[1,1024,1024]{2,1,0:T(8,128)S(1)}, f32[1,1024,1024]{2,1,0:T(8,128)}, u32[]{:S(2)}) copy-start(f32[1,1024,1024]{2,1,0:T(8,128)} %param.41) | copy-start | bytes 12582916
  507.6 15.6 %copy-start.71 = (bf16[2048,1024]{1,0:T(8,128)(2,1)S(1)}, bf16[2048,1024]{1,0:T(8,128)(2,1)}, u32[]{:S(2)}) copy-start(bf16[2048,1024]{1,0:T(8,128)(2,1)} %copy-done.70) | copy-start | bytes 12582916
  534.4 128.2 %copy-start.52 = (f32[2048]{0:T(1024)S(1)}, f32[2048]{0:T(1024)}, u32[]{:S(2)}) copy-start(f32[2048]{0:T(1024)} %copy-done.51) | copy-start | bytes 24580
  662.6 11.5 copy-start.35
  674.1 11.3 copy-start.6
  674.1 11.3 copy-start.43
  674.1 11.3 copy-start.45
  696.1 23.6 %slice-start = ((s8[16777216]{0:T(1024)(128)(4,1)}), s8[4194304]{0:T(1024)(128)(4,1)S(1)}, s32[]{:S(2)}) async-start(s8[16777216]{0:T(1024)(128)(4,1)} %bitcast.238), calls=%async_computation.5 | async-start | bytes 8388608 | tf_op jit(solution)/shard_map/while
  696.1 23.6 %slice-start.1 = ((s8[16777216]{0:T(1024)(128)(4,1)}), s8[4194304]{0:T(1024)(128)(4,1)S(1)}, s32[]{:S(2)}) async-start(s8[16777216]{0:T(1024)(128)(4,1)} %bitcast.238), calls=%async_computation.6 | async-start | bytes 8388608 | tf_op jit(solution)/shard_map/while
  705.0 14.7 %slice-start.2 = ((s8[16777216]{0:T(1024)(128)(4,1)}), s8[4194304]{0:T(1024)(128)(4,1)S(1)}, s32[]{:S(2)}) async-start(s8[16777216]{0:T(1024)(128)(4,1)} %bitcast.238), calls=%async_computation.7 | async-start | bytes 8388608 | tf_op jit(solution)/shard_map/while
  705.0 14.7 %slice-start.3 = ((s8[16777216]{0:T(1024)(128)(4,1)}), s8[4194304]{0:T(1024)(128)(4,1)S(1)}, s32[]{:S(2)}) async-start(s8[16777216]{0:T(1024)(128)(4,1)} %bitcast.238), calls=%async_computation.8 | async-start | bytes 8388608 | tf_op jit(solution)/shard_map/while
  743.5 23.6 %slice-start = ((s8[16777216]{0:T(1024)(128)(4,1)}), s8[4194304]{0:T(1024)(128)(4,1)S(1)}, s32[]{:S(2)}) async-start(s8[16777216]{0:T(1024)(128)(4,1)} %bitcast.238), calls=%async_computation.5 | async-start | bytes 8388608 | tf_op jit(solution)/shard_map/while
  743.5 23.6 %slice-start.1 = ((s8[16777216]{0:T(1024)(128)(4,1)}), s8[4194304]{0:T(1024)(128)(4,1)S(1)}, s32[]{:S(2)}) async-start(s8[16777216]{0:T(1024)(128)(4,1)} %bitcast.238), calls=%async_computation.6 | async-start | bytes 8388608 | tf_op jit(solution)/shard_map/while
  752.4 14.7 %slice-start.2 = ((s8[16777216]{0:T(1024)(128)(4,1)}), s8[4194304]{0:T(1024)(128)(4,1)S(1)}, s32[]{:S(2)}) async-start(s8[16777216]{0:T(1024)(128)(4,1)} %bitcast.238), calls=%async_computation.7 | async-start | bytes 8388608 | tf_op jit(solution)/shard_map/while
  752.4 14.7 %slice-start.3 = ((s8[16777216]{0:T(1024)(128)(4,1)}), s8[4194304]{0:T(1024)(128)(4,1)S(1)}, s32[]{:S(2)}) async-start(s8[16777216]{0:T(1024)(128)(4,1)} %bitcast.238), calls=%async_computation.8 | async-start | bytes 8388608 | tf_op jit(solution)/shard_map/while
  808.4 11.0 copy-start.58
  1165.3 11.7 copy-start.61
  1165.3 11.7 copy-start.62
  1165.3 11.8 copy-start.56
  1165.3 49.6 %copy-start.64 = (f32[2,256]{1,0:T(2,128)S(1)}, f32[2,256]{1,0:T(2,128)}, u32[]{:S(2)}) copy-start(f32[2,256]{1,0:T(2,128)} %param.32) | copy-start | bytes 6148
  1165.3 49.6 %copy-start.68 = (f32[2,256]{1,0:T(2,128)S(1)}, f32[2,256]{1,0:T(2,128)}, u32[]{:S(2)}) copy-start(f32[2,256]{1,0:T(2,128)} %param.48) | copy-start | bytes 6148
  1165.3 50.2 %copy-start.66 = (f32[1024]{0:T(1024)S(1)}, f32[1024]{0:T(1024)}, u32[]{:S(2)}) copy-start(f32[1024]{0:T(1024)} %param.35) | copy-start | bytes 12292
  1165.3 50.2 %copy-start.67 = (f32[1024]{0:T(1024)S(1)}, f32[1024]{0:T(1024)}, u32[]{:S(2)}) copy-start(f32[1024]{0:T(1024)} %param.51) | copy-start | bytes 12292
  1165.3 51.5 %copy-start.50 = (f32[6,1024]{1,0:T(8,128)S(1)}, f32[6,1024]{1,0:T(8,128)}, u32[]{:S(2)}) copy-start(f32[6,1024]{1,0:T(8,128)} %param.37) | copy-start | bytes 73732
  1165.4 51.5 %copy-start.59 = (f32[6,1024]{1,0:T(8,128)S(1)}, f32[6,1024]{1,0:T(8,128)}, u32[]{:S(2)}) copy-start(f32[6,1024]{1,0:T(8,128)} %param.53) | copy-start | bytes 73732
  1171.4 59.2 %copy-start.19 = (f32[1024,3,256]{2,0,1:T(8,128)}, f32[1024,3,256]{2,0,1:T(8,128)S(1)}, u32[]{:S(2)}) copy-start(f32[1024,3,256]{2,0,1:T(8,128)S(1)} %copy.125) | copy-start | bytes 9437188
  1214.9 13.7 %copy-start.21 = (f32[256,1024]{1,0:T(8,128)S(1)}, f32[256,1024]{1,0:T(8,128)}, u32[]{:S(2)}) copy-start(f32[256,1024]{1,0:T(8,128)} %copy-done.20) | copy-start | bytes 3145732
  1214.9 13.7 %copy-start.36 = (bf16[256,1024]{1,0:T(8,128)(2,1)S(1)}, bf16[256,1024]{1,0:T(8,128)(2,1)}, u32[]{:S(2)}) copy-start(bf16[256,1024]{1,0:T(8,128)(2,1)} %param.33) | copy-start | bytes 1572868
  1214.9 13.7 %copy-start.41 = (f32[256,1024]{1,0:T(8,128)S(1)}, f32[256,1024]{1,0:T(8,128)}, u32[]{:S(2)}) copy-start(f32[256,1024]{1,0:T(8,128)} %param.49) | copy-start | bytes 3145732
  1216.7 13.8 %copy-start.24 = (bf16[1024,3,256]{2,0,1:T(8,128)(2,1)S(1)}, bf16[1024,3,256]{2,0,1:T(8,128)(2,1)}, u32[]{:S(2)}) copy-start(bf16[1024,3,256]{2,0,1:T(8,128)(2,1)} %param.31) | copy-start | bytes 4718596
  1216.7 13.8 %copy-start.33 = (f32[1024,3,256]{2,0,1:T(8,128)S(1)}, f32[1024,3,256]{2,0,1:T(8,128)}, u32[]{:S(2)}) copy-start(f32[1024,3,256]{2,0,1:T(8,128)} %param.47) | copy-start | bytes 9437188
  1216.7 17.2 %copy-start.48 = (f32[8,1024]{1,0:T(8,128)}, f32[8,1024]{1,0:T(8,128)S(1)}, u32[]{:S(2)}) copy-start(f32[8,1024]{1,0:T(8,128)S(1)} %convert_multiply_fusion.6) | copy-start | bytes 98308
  1216.8 17.1 %copy-start.46 = (f32[8,1024]{1,0:T(8,128)}, f32[8,1024]{1,0:T(8,128)S(1)}, u32[]{:S(2)}) copy-start(f32[8,1024]{1,0:T(8,128)S(1)} %convert_multiply_fusion.4) | copy-start | bytes 98308
  1216.8 17.1 %copy-start.47 = (f32[8,1024]{1,0:T(8,128)}, f32[8,1024]{1,0:T(8,128)S(1)}, u32[]{:S(2)}) copy-start(f32[8,1024]{1,0:T(8,128)S(1)} %convert_multiply_fusion.2) | copy-start | bytes 98308
  1218.5 10.0 copy-start.31
  1233.9 12.2 copy-start.40
  1246.1 15.1 %copy-start.1 = (f32[8,1024]{1,0:T(8,128)S(1)}, f32[8,1024]{1,0:T(8,128)}, u32[]{:S(2)}) copy-start(f32[8,1024]{1,0:T(8,128)} %param.46) | copy-start | bytes 98308
  (46 other events, 234.9 us)
Sparse Core Ops, SparseCore 0:
  106.4 155.5 all-reduce.6
  307.4 152.9 all-reduce.8
  498.1 152.9 all-reduce.10
  1034.8 40.9 reduce-scatter.1
where the time goes:
time: 1280 us; the launch traced here: 1270 us
  waiting for transfers between devices  425 us (33%)
  other arithmetic  359 us (28%)
  matrix products  242 us (19%)
  blocking collectives  109 us (9%)
  local copies, waits for them, and re-layouts  94.7 us (7%)
  between operations  37 us (3%)
    psum x1, waiting for transfers between devices, local(): lax.psum(jnp.dot(mixed_flat, w_out, preferred_element_type=jnp.float32),...  156 us
    psum x1, waiting for transfers between devices, local(): lax.psum(jnp.dot(active_low, w_down, preferred_element_type=jnp.float32),...  153 us
    reduce_sum x40, other arithmetic, orthonormal(): jnp.sum(earlier * column, axis=-1, keepdims=True) * earlier  122 us
    psum x1, waiting for transfers between devices, local(): grad_first = lax.psum(times_trans(grad_hidden, w_in), 'tensor') + grad_sum  117 us
    div x4, other arithmetic, orthonormal(): column / (jnp.sqrt(jnp.sum(column * column, axis=-1, keepdims=True)) + EP...  70.6 us
    psum x1, blocking collectives, local(): lax.psum(left_of(combined_qkv, basis_qkv.reshape(rank_size, 3 * head_slab...  37.9 us
    psum x1, blocking collectives, local(): lax.psum((local_vectors, head_full, unit_full), ('dp', 'tensor'))  37.7 us
    reduce_sum x20, other arithmetic, orthonormal(): jnp.sum(column * column, axis=-1, keepdims=True)  33.8 us
  transfers between devices with their start and end apart: 4, of which 3 were waited for; matrix products, arithmetic and copies ran while one was open for 14% of the time, Pallas kernels for 0%

commit v1 on v0

--- a/solution.py
+++ b/solution.py
@@ -4,9 +4,13 @@
 import jax
 import jax.numpy as jnp
 from jax import lax
+from jax.experimental import pallas as pl
+from jax.experimental.pallas import tpu as pltpu
 from jax.sharding import PartitionSpec as P
 
 DH = 64
+LANES = 128
+MESH = pl.DeviceIdType.MESH
 
 
 PRECISE = lax.Precision.HIGHEST
@@ -43,35 +47,487 @@
     )
 
 
-def left_of(matrix, factor):
+def split_bf16(values):
+    high = values.astype(jnp.bfloat16)
+    low = (values - high.astype(jnp.float32)).astype(jnp.bfloat16)
+    return high, low
+
+
+def dot_nt(left_side, right_side):
     return lax.dot_general(
-        matrix,
-        factor,
-        (((1,), (1,)), ((), ())),
-        precision=PRECISE,
-        preferred_element_type=jnp.float32,
-    )
-
-
-def right_of(basis, matrix):
+        left_side, right_side, (((1,), (1,)), ((), ())), preferred_element_type=jnp.float32
+    )
+
+
+def dot_nn(left_side, right_side):
     return lax.dot_general(
-        basis,
-        matrix,
-        (((0,), (0,)), ((), ())),
-        precision=PRECISE,
-        preferred_element_type=jnp.float32,
-    )
-
-
-def orthonormal(factor):
-    columns = []
-    for position in range(factor.shape[-1]):
-        column = factor[..., position]
-        for earlier in columns:
-            column = column - jnp.sum(earlier * column, axis=-1, keepdims=True) * earlier
-        column = column / (jnp.sqrt(jnp.sum(column * column, axis=-1, keepdims=True)) + EPS_BASIS)
-        columns.append(column)
-    return jnp.stack(columns, axis=-1)
+        left_side, right_side, (((1,), (0,)), ((), ())), preferred_element_type=jnp.float32
+    )
+
+
+def dot_tn(left_side, right_side):
+    return lax.dot_general(
+        left_side, right_side, (((0,), (0,)), ((), ())), preferred_element_type=jnp.float32
+    )
+
+
+def left_factor(factor, matrix):
+    rank_size = factor.shape[0]
+    factor_high, factor_low = split_bf16(factor)
+    matrix_high, matrix_low = split_bf16(matrix)
+    both = dot_nt(jnp.concatenate([factor_high, factor_low], axis=0), matrix_high)
+    return both[:rank_size] + both[rank_size:] + dot_nt(factor_high, matrix_low)
+
+
+def right_factor(basis_rows, matrix):
+    rank_size = basis_rows.shape[0]
+    basis_high, basis_low = split_bf16(basis_rows)
+    matrix_high, matrix_low = split_bf16(matrix)
+    both = dot_nn(jnp.concatenate([basis_high, basis_low], axis=0), matrix_high)
+    return both[:rank_size] + both[rank_size:] + dot_nn(basis_high, matrix_low)
+
+
+def lefts_kernel(qkv_ref, out_ref, in_ref, down_ref, fq_ref, fo_ref, fi_ref, fd_ref,
+                 lq_ref, lo_ref, li_ref, ld_ref):
+    lq_ref[...] = (
+        left_factor(fq_ref[0], qkv_ref[0])
+        + left_factor(fq_ref[1], qkv_ref[1])
+        + left_factor(fq_ref[2], qkv_ref[2])
+    )
+    li_ref[...] = left_factor(fi_ref[...], in_ref[...])
+    ld_ref[...] = left_factor(fd_ref[...], down_ref[...])
+
+    @pl.when(pl.program_id(0) == 0)
+    def _():
+        lo_ref[...] = left_factor(fo_ref[...], out_ref[...])
+
+
+def lefts_of(matrices, factors):
+    steps = 4
+    qkv, out, inw, down = matrices
+    rank_size = factors[1].shape[0]
+
+    def whole(array):
+        return pl.BlockSpec(array.shape, lambda i: (0,) * array.ndim)
+
+    def rows(array):
+        return pl.BlockSpec((array.shape[0] // steps, array.shape[1]), lambda i: (i, 0))
+
+    def lanes(size):
+        return pl.BlockSpec((rank_size, size // steps), lambda i: (0, i))
+
+    return pl.pallas_call(
+        lefts_kernel,
+        grid=(steps,),
+        in_specs=[
+            pl.BlockSpec((3, qkv.shape[1] // steps, qkv.shape[2]), lambda i: (0, i, 0)),
+            whole(out),
+            rows(inw),
+            rows(down),
+        ]
+        + [whole(factor) for factor in factors],
+        out_specs=[
+            lanes(qkv.shape[1]),
+            pl.BlockSpec((rank_size, out.shape[0]), lambda i: (0, 0)),
+            lanes(inw.shape[0]),
+            lanes(down.shape[0]),
+        ],
+        out_shape=[
+            jax.ShapeDtypeStruct((rank_size, size), jnp.float32)
+            for size in (qkv.shape[1], out.shape[0], inw.shape[0], down.shape[0])
+        ],
+        compiler_params=pltpu.CompilerParams(vmem_limit_bytes=40 << 20),
+        name="left_factors",
+    )(qkv, out, inw, down, *factors)
+
+
+def rights_kernel(qkv_ref, out_ref, in_ref, down_ref, bq_ref, bo_ref, bi_ref, bd_ref,
+                  rq_ref, ro_ref, ri_ref, rd_ref):
+    first = pl.program_id(0) == 0
+
+    @pl.when(first)
+    def _():
+        ro_ref[...] = right_factor(bo_ref[...], out_ref[...])
+        rq_ref[...] = jnp.zeros_like(rq_ref)
+        ri_ref[...] = jnp.zeros_like(ri_ref)
+        rd_ref[...] = jnp.zeros_like(rd_ref)
+
+    for part in range(3):
+        rq_ref[part] += right_factor(bq_ref[...], qkv_ref[part])
+    ri_ref[...] += right_factor(bi_ref[...], in_ref[...])
+    rd_ref[...] += right_factor(bd_ref[...], down_ref[...])
+
+
+def rights_of(matrices, bases):
+    steps = 4
+    qkv, out, inw, down = matrices
+    rank_size = bases[0].shape[0]
+
+    def whole(shape):
+        return pl.BlockSpec(shape, lambda i: (0,) * len(shape))
+
+    def rows(array):
+        return pl.BlockSpec((array.shape[0] // steps, array.shape[1]), lambda i: (i, 0))
+
+    def lanes(array):
+        return pl.BlockSpec((rank_size, array.shape[1] // steps), lambda i: (0, i))
+
+    shapes = [(3, rank_size, qkv.shape[2])] + [(rank_size, one.shape[1]) for one in (out, inw, down)]
+    return pl.pallas_call(
+        rights_kernel,
+        grid=(steps,),
+        in_specs=[
+            pl.BlockSpec((3, qkv.shape[1] // steps, qkv.shape[2]), lambda i: (0, i, 0)),
+            whole(out.shape),
+            rows(inw),
+            rows(down),
+            lanes(bases[0]),
+            whole(bases[1].shape),
+            lanes(bases[2]),
+            lanes(bases[3]),
+        ],
+        out_specs=[whole(shape) for shape in shapes],
+        out_shape=[jax.ShapeDtypeStruct(shape, jnp.float32) for shape in shapes],
+        compiler_params=pltpu.CompilerParams(vmem_limit_bytes=40 << 20),
+        name="right_factors",
+    )(qkv, out, inw, down, *bases)
+
+
+def peer_ids(replicas, place):
+    dp_place = lax.axis_index("dp")
+    tensor_place = lax.axis_index("tensor")
+    return dp_place, tensor_place
+
+
+def greet(replicas, tensor_size):
+    dp_place = lax.axis_index("dp")
+    tensor_place = lax.axis_index("tensor")
+    barrier = pltpu.get_barrier_semaphore()
+
+    def greet_dp(step, carry):
+        pl.semaphore_signal(
+            barrier,
+            inc=1,
+            device_id=(lax.rem(dp_place + step, replicas), tensor_place),
+            device_id_type=MESH,
+        )
+        return carry
+
+    def greet_tensor(step, carry):
+        pl.semaphore_signal(
+            barrier,
+            inc=1,
+            device_id=(dp_place, lax.rem(tensor_place + step, tensor_size)),
+            device_id_type=MESH,
+        )
+        return carry
+
+    lax.fori_loop(1, replicas, greet_dp, 0)
+    if tensor_size > 1:
+        lax.fori_loop(1, tensor_size, greet_tensor, 0)
+    pl.semaphore_wait(barrier, replicas - 1 + tensor_size - 1)
+
+
+def dp_sum(replicas, mine, wire, arrived, total, send_one, recv_one, send_two, recv_two):
+    dp_place = lax.axis_index("dp")
+    tensor_place = lax.axis_index("tensor")
+
+    def scatter_to(step):
+        peer = lax.rem(dp_place + step, replicas)
+        return pltpu.make_async_remote_copy(
+            src_ref=wire.at[peer],
+            dst_ref=arrived.at[dp_place],
+            send_sem=send_one.at[step],
+            recv_sem=recv_one.at[dp_place],
+            device_id=(peer, tensor_place),
+            device_id_type=MESH,
+        )
+
+    def scatter_from(step):
+        peer = lax.rem(dp_place + step, replicas)
+        return pltpu.make_async_remote_copy(
+            src_ref=wire.at[peer],
+            dst_ref=arrived.at[peer],
+            send_sem=send_one.at[step],
+            recv_sem=recv_one.at[peer],
+            device_id=(peer, tensor_place),
+            device_id_type=MESH,
+        )
+
+    def gather_to(step):
+        peer = lax.rem(dp_place + step, replicas)
+        return pltpu.make_async_remote_copy(
+            src_ref=total.at[dp_place],
+            dst_ref=total.at[dp_place],
+            send_sem=send_two.at[step],
+            recv_sem=recv_two.at[dp_place],
+            device_id=(peer, tensor_place),
+            device_id_type=MESH,
+        )
+
+    def gather_from(step):
+        peer = lax.rem(dp_place + step, replicas)
+        return pltpu.make_async_remote_copy(
+            src_ref=total.at[dp_place],
+            dst_ref=total.at[peer],
+            send_sem=send_two.at[step],
+            recv_sem=recv_two.at[peer],
+            device_id=(peer, tensor_place),
+            device_id_type=MESH,
+        )
+
+    def start_scatter(step, carry):
+        scatter_to(step).start()
+        return carry
+
+    def add_arrived(step, carry):
+        scatter_from(step).wait_recv()
+        peer = lax.rem(dp_place + step, replicas)
+        return carry + arrived[peer].astype(jnp.float32)
+
+    def start_gather(step, carry):
+        gather_to(step).start()
+        return carry
+
+    def finish(step, carry):
+        scatter_to(step).wait_send()
+        gather_to(step).wait_send()
+        gather_from(step).wait_recv()
+        return carry
+
+    wire[...] = mine[...].astype(wire.dtype)
+    lax.fori_loop(1, replicas, start_scatter, 0)
+    total[dp_place] = lax.fori_loop(1, replicas, add_arrived, mine[dp_place])
+    lax.fori_loop(1, replicas, start_gather, 0)
+    lax.fori_loop(1, replicas, finish, 0)
+
+
+def place_tiles(target, offset, values):
+    per_chunk = target.shape[2] // LANES
+    for tile in range(values.shape[1] // LANES):
+        spot = offset + tile
+        target[spot // per_chunk, :, pl.ds(spot % per_chunk * LANES, LANES)] = values[
+            :, tile * LANES : (tile + 1) * LANES
+        ]
+    return offset + values.shape[1] // LANES
+
+
+def take_tiles(source, offset, size):
+    per_chunk = source.shape[2] // LANES
+    pieces = []
+    for tile in range(size // LANES):
+        spot = offset + tile
+        pieces.append(source[spot // per_chunk, :, pl.ds(spot % per_chunk * LANES, LANES)])
+    return jnp.concatenate(pieces, axis=1) if len(pieces) > 1 else pieces[0]
+
+
+def orthonormal_rows(rows):
+    rank_size = rows.shape[0]
+    row_number = lax.broadcasted_iota(jnp.int32, (rank_size, 1), 0)
+    for position in range(rank_size):
+        row = rows[position : position + 1]
+        length = jnp.sqrt(jnp.sum(row * row, axis=1, keepdims=True)) + EPS_BASIS
+        unit = row / length
+        along = jnp.sum(rows * unit, axis=1, keepdims=True)
+        later = jnp.where(row_number > position, along, 0.0)
+        rows = jnp.where(row_number == position, unit, rows - later * unit)
+    return rows
+
+
+def basis_kernel(replicas, tensor_size, lq_ref, lo_ref, li_ref, ld_ref, small_ref,
+                 bq_ref, bo_ref, bi_ref, bd_ref, sum_ref,
+                 mine, wire, arrived, total, small_slots,
+                 send_one, recv_one, send_two, recv_two, send_three, recv_three):
+    dp_place = lax.axis_index("dp")
+    tensor_place = lax.axis_index("tensor")
+    mine[...] = jnp.zeros_like(mine)
+    greet(replicas, tensor_size)
+    lefts = (lq_ref, lo_ref, li_ref, ld_ref)
+    offset = 0
+    for ref in lefts + (small_ref,):
+        offset = place_tiles(mine, offset, ref[...])
+    dp_sum(replicas, mine, wire, arrived, total, send_one, recv_one, send_two, recv_two)
+
+    def slot_copy(step, slot):
+        peer = lax.rem(tensor_place + step, tensor_size)
+        return pltpu.make_async_remote_copy(
+            src_ref=small_slots.at[tensor_place],
+            dst_ref=small_slots.at[slot],
+            send_sem=send_three.at[step],
+            recv_sem=recv_three.at[slot],
+            device_id=(dp_place, peer),
+            device_id_type=MESH,
+        )
+
+    def start(step, carry):
+        slot_copy(step, tensor_place).start()
+        return carry
+
+    small_at = sum(ref.shape[1] for ref in lefts) // LANES
+    own_small = take_tiles(total, small_at, small_ref.shape[1])
+    small_slots[tensor_place] = own_small
+    lax.fori_loop(1, tensor_size, start, 0)
+    offset = 0
+    for ref, basis_ref in zip(lefts, (bq_ref, bo_ref, bi_ref, bd_ref)):
+        rows = take_tiles(total, offset, ref.shape[1]) * (1.0 / replicas)
+        basis_ref[...] = orthonormal_rows(rows)
+        offset += ref.shape[1] // LANES
+
+    def collect(step, carry):
+        peer = lax.rem(tensor_place + step, tensor_size)
+        slot_copy(step, peer).wait_recv()
+        slot_copy(step, tensor_place).wait_send()
+        return carry + small_slots[peer]
+
+    everyone = lax.fori_loop(1, tensor_size, collect, own_small)
+    row_number = lax.broadcasted_iota(jnp.int32, everyone.shape, 0)
+    sum_ref[...] = jnp.where(row_number < 6, everyone, own_small) * (1.0 / replicas)
+
+
+def bases_of(lefts, small, replicas, tensor_size):
+    rank_size = small.shape[0]
+    lanes = sum(left.shape[1] for left in lefts) + small.shape[1]
+    width = -(-lanes // (LANES * replicas)) * LANES
+    shapes = [left.shape for left in lefts] + [small.shape]
+    vmem = pl.BlockSpec(memory_space=pltpu.VMEM)
+    return pl.pallas_call(
+        partial(basis_kernel, replicas, tensor_size),
+        in_specs=[vmem] * 5,
+        out_specs=[vmem] * 5,
+        out_shape=[jax.ShapeDtypeStruct(shape, jnp.float32) for shape in shapes],
+        scratch_shapes=[
+            pltpu.VMEM((replicas, rank_size, width), jnp.float32),
+            pltpu.VMEM((replicas, rank_size, width), jnp.bfloat16),
+            pltpu.VMEM((replicas, rank_size, width), jnp.bfloat16),
+            pltpu.VMEM((replicas, rank_size, width), jnp.float32),
+            pltpu.VMEM((tensor_size,) + small.shape, jnp.float32),
+            pltpu.SemaphoreType.DMA((replicas,)),
+            pltpu.SemaphoreType.DMA((replicas,)),
+            pltpu.SemaphoreType.DMA((replicas,)),
+            pltpu.SemaphoreType.DMA((replicas,)),
+            pltpu.SemaphoreType.DMA((tensor_size,)),
+            pltpu.SemaphoreType.DMA((tensor_size,)),
+        ],
+        compiler_params=pltpu.CompilerParams(collective_id=1, has_side_effects=True),
+        name="bases",
+    )(*lefts, small)
+
+
+def right_sum_kernel(replicas, rq_ref, ro_ref, ri_ref, rd_ref, sq_ref, so_ref, si_ref, sd_ref,
+                     mine, wire, arrived, total, send_one, recv_one, send_two, recv_two):
+    mine[...] = jnp.zeros_like(mine)
+    greet(replicas, 1)
+    offset = 0
+    for part in range(3):
+        offset = place_tiles(mine, offset, rq_ref[part])
+    for ref in (ro_ref, ri_ref, rd_ref):
+        offset = place_tiles(mine, offset, ref[...])
+    dp_sum(replicas, mine, wire, arrived, total, send_one, recv_one, send_two, recv_two)
+    offset = 0
+    for part in range(3):
+        sq_ref[part] = take_tiles(total, offset, sq_ref.shape[2]) * (1.0 / replicas)
+        offset += sq_ref.shape[2] // LANES
+    for ref in (so_ref, si_ref, sd_ref):
+        ref[...] = take_tiles(total, offset, ref.shape[1]) * (1.0 / replicas)
+        offset += ref.shape[1] // LANES
+
+
+def right_sums(rights, replicas):
+    rank_size = rights[1].shape[0]
+    lanes = 3 * rights[0].shape[2] + sum(right.shape[1] for right in rights[1:])
+    width = -(-lanes // (LANES * replicas)) * LANES
+    vmem = pl.BlockSpec(memory_space=pltpu.VMEM)
+    return pl.pallas_call(
+        partial(right_sum_kernel, replicas),
+        in_specs=[vmem] * 4,
+        out_specs=[vmem] * 4,
+        out_shape=[jax.ShapeDtypeStruct(right.shape, jnp.float32) for right in rights],
+        scratch_shapes=[
+            pltpu.VMEM((replicas, rank_size, width), jnp.float32),
+            pltpu.VMEM((replicas, rank_size, width), jnp.bfloat16),
+            pltpu.VMEM((replicas, rank_size, width), jnp.bfloat16),
+            pltpu.VMEM((replicas, rank_size, width), jnp.float32),
+            pltpu.SemaphoreType.DMA((replicas,)),
+            pltpu.SemaphoreType.DMA((replicas,)),
+            pltpu.SemaphoreType.DMA((replicas,)),
+            pltpu.SemaphoreType.DMA((replicas,)),
+        ],
+        compiler_params=pltpu.CompilerParams(collective_id=2, has_side_effects=True),
+        name="right_sums",
+    )(*rights)
+
+
+def outer_of(basis_rows, right):
+    basis_high, basis_low = split_bf16(basis_rows)
+    right_high, right_low = split_bf16(right)
+    return dot_tn(
+        jnp.concatenate([basis_high, basis_low, basis_high], axis=0),
+        jnp.concatenate([right_high, right_high, right_low], axis=0),
+    )
+
+
+def update_kernel(step_rate, out_steps, *refs):
+    (mq, mo, mi, md, oq, oo, oi, od, wq, wo, wi, wd, bq, bo, bi, bd, rq, ro, ri, rd,
+     gq, go, gi, gd, eq, eo, ei, ed, nq, no, ni, nd, vq, vo, vi, vd) = refs
+    step = pl.program_id(0)
+
+    def one(matrix, old, weight, rank, grad_ref, err_ref, mom_ref, new_ref, place):
+        moment = 0.9 * old + rank
+        grad_ref[place] = rank
+        err_ref[place] = matrix - rank
+        mom_ref[place] = moment
+        new_ref[place] = weight.astype(jnp.float32) - step_rate * moment
+
+    def lanes_of(ref, rows):
+        return ref[:, pl.ds(pl.multiple_of(step * rows, LANES), rows)]
+
+    rows = mq.shape[1]
+    for part in range(3):
+        rank = outer_of(lanes_of(bq, rows), rq[part])
+        one(mq[part], oq[part], wq[part], rank, gq, eq, nq, vq, part)
+    rank = outer_of(lanes_of(bi, mi.shape[0]), ri[...])
+    one(mi[...], oi[...], wi[...], rank, gi, ei, ni, vi, slice(None))
+    rank = outer_of(lanes_of(bd, md.shape[0]), rd[...])
+    one(md[...], od[...], wd[...], rank, gd, ed, nd, vd, slice(None))
+
+    @pl.when(step < out_steps)
+    def _():
+        rank = outer_of(lanes_of(bo, mo.shape[0]), ro[...])
+        one(mo[...], oo[...], wo[...], rank, go, eo, no, vo, slice(None))
+
+
+def update(matrices, momenta, weights, bases, rights, step_rate):
+    qkv, out, inw, down = matrices
+    rows = LANES
+    steps = inw.shape[0] // rows
+    down_rows = down.shape[0] // steps
+    if down_rows < LANES:
+        steps = down.shape[0] // LANES
+        rows, down_rows = inw.shape[0] // steps, LANES
+    out_steps = out.shape[0] // LANES
+
+    def whole(array):
+        return pl.BlockSpec(array.shape, lambda i: (0,) * array.ndim)
+
+    def specs():
+        return [
+            pl.BlockSpec((3, rows, qkv.shape[2]), lambda i: (0, i, 0)),
+            pl.BlockSpec((LANES, out.shape[1]), lambda i: (jnp.minimum(i, out_steps - 1), 0)),
+            pl.BlockSpec((rows, inw.shape[1]), lambda i: (i, 0)),
+            pl.BlockSpec((down_rows, down.shape[1]), lambda i: (i, 0)),
+        ]
+
+    shapes = [jax.ShapeDtypeStruct(one.shape, jnp.float32) for one in matrices]
+    outputs = pl.pallas_call(
+        partial(update_kernel, step_rate, out_steps),
+        grid=(steps,),
+        in_specs=specs() * 3 + [whole(one) for one in bases] + [whole(one) for one in rights],
+        out_specs=specs() * 4,
+        out_shape=shapes * 4,
+        compiler_params=pltpu.CompilerParams(vmem_limit_bytes=48 << 20),
+        name="update",
+    )(*matrices, *momenta, *weights, *bases, *rights)
+    return outputs[0:4], outputs[4:8], outputs[8:12], outputs[12:16]
 
 
 def masked_scores(queries, key_heads, seg_ids):
@@ -151,7 +607,6 @@
     head_slab = w_qkv.shape[2]
     head_count = head_slab // DH
     unit_slab = w_in.shape[1]
-    rank_size = basis_in.shape[0]
     tensor_size = lax.axis_size("tensor")
     replicas = lax.axis_size("dp")
     share_rows = token_count // tensor_size
@@ -248,78 +703,55 @@
             jnp.sum(grad_out_share, axis=0),
         ]
     )
-    zero_index = jnp.zeros((), jnp.int32)
-    head_full = lax.dynamic_update_slice(
-        jnp.zeros((2, head_slab * tensor_size), jnp.float32),
-        grad_heads,
-        (zero_index, tensor_place * head_slab),
-    )
-    unit_full = lax.dynamic_update_slice(
-        jnp.zeros((unit_slab * tensor_size,), jnp.float32), grad_units, (tensor_place * unit_slab,)
-    )
-    vector_sum, head_sum, unit_sum = lax.psum(
-        (local_vectors, head_full, unit_full), ("dp", "tensor")
-    )
-    grad_vectors = vector_sum / replicas
-    grad_head_bias = (
-        lax.dynamic_slice_in_dim(head_sum, tensor_place * head_slab, head_slab, 1) / replicas
-    )
-    grad_unit_bias = (
-        lax.dynamic_slice_in_dim(unit_sum, tensor_place * unit_slab, unit_slab, 0) / replicas
-    )
-    combined_qkv = grad_w_qkv + err_qkv[0].reshape(model_width, 3 * head_slab)
+    small = jnp.concatenate(
+        [
+            local_vectors,
+            jnp.pad(grad_units, (0, model_width - unit_slab))[None],
+            jnp.pad(grad_heads.reshape(1, 2 * head_slab), ((0, 0), (0, model_width - 2 * head_slab))),
+        ],
+        axis=0,
+    )
+    planes = (1, 0, 2)
+    combined_qkv = grad_w_qkv.reshape(model_width, 3, head_slab).transpose(planes) + err_qkv[
+        0
+    ].transpose(planes)
     combined_out = grad_w_out + err_out[0]
     combined_in = grad_w_in + err_in[0]
     combined_down = grad_w_down + err_down[0]
-    left_qkv, left_out, left_in, left_down = (
-        lax.psum(
-            left_of(combined_qkv, basis_qkv.reshape(rank_size, 3 * head_slab)).astype(jnp.bfloat16),
-            "dp",
-        ).astype(jnp.float32),
-        lax.psum(left_of(combined_out, basis_out).astype(jnp.bfloat16), "dp").astype(jnp.float32),
-        lax.psum(left_of(combined_in, basis_in).astype(jnp.bfloat16), "dp").astype(jnp.float32),
-        lax.psum(left_of(combined_down, basis_down).astype(jnp.bfloat16), "dp").astype(jnp.float32),
-    )
-    ortho_qkv = orthonormal(left_qkv / replicas)
-    ortho_out = orthonormal(left_out / replicas)
-    ortho_in = orthonormal(left_in / replicas)
-    ortho_down = orthonormal(left_down / replicas)
-    right_qkv, right_out, right_in, right_down = (
-        lax.psum(right_of(ortho_qkv, combined_qkv).astype(jnp.bfloat16), "dp").astype(jnp.float32),
-        lax.psum(right_of(ortho_out, combined_out).astype(jnp.bfloat16), "dp").astype(jnp.float32),
-        lax.psum(right_of(ortho_in, combined_in).astype(jnp.bfloat16), "dp").astype(jnp.float32),
-        lax.psum(right_of(ortho_down, combined_down).astype(jnp.bfloat16), "dp").astype(
-            jnp.float32
-        ),
-    )
-    right_qkv = right_qkv / replicas
-    right_out = right_out / replicas
-    right_in = right_in / replicas
-    right_down = right_down / replicas
-    rank_qkv = jnp.dot(ortho_qkv, right_qkv, precision=PRECISE)
-    rank_out = jnp.dot(ortho_out, right_out, precision=PRECISE)
-    rank_in = jnp.dot(ortho_in, right_in, precision=PRECISE)
-    rank_down = jnp.dot(ortho_down, right_down, precision=PRECISE)
-    reduced_qkv = rank_qkv.reshape(model_width, 3, head_slab)
-    new_err_qkv = (combined_qkv - rank_qkv).reshape(1, model_width, 3, head_slab)
-    new_err_out = (combined_out - rank_out)[None]
-    new_err_in = (combined_in - rank_in)[None]
-    new_err_down = (combined_down - rank_down)[None]
-    new_basis_qkv = right_qkv.reshape(rank_size, 3, head_slab)
+    matrices = (combined_qkv, combined_out, combined_in, combined_down)
+    lefts = lefts_of(matrices, (basis_qkv.transpose(planes), basis_out, basis_in, basis_down))
+    *bases, small_sum = bases_of(lefts, small, replicas, tensor_size)
+    rights = right_sums(rights_of(matrices, bases), replicas)
     step_rate = 0.3 * math.sqrt(replicas / token_count)
-    new_mom_qkv = 0.9 * mom_qkv + reduced_qkv
+    grads, errors, moments, news = update(
+        matrices,
+        (mom_qkv.transpose(planes), mom_out, mom_in, mom_down),
+        (w_qkv.transpose(planes), w_out, w_in, w_down),
+        bases,
+        rights,
+        step_rate,
+    )
+    reduced_qkv, rank_out, rank_in, rank_down = (grads[0].transpose(planes),) + tuple(grads[1:])
+    new_err_qkv, new_err_out, new_err_in, new_err_down = (
+        errors[0].transpose(planes)[None],
+        errors[1][None],
+        errors[2][None],
+        errors[3][None],
+    )
+    new_mom_qkv, new_mom_out, new_mom_in, new_mom_down = (moments[0].transpose(planes),) + tuple(
+        moments[1:]
+    )
+    new_w_qkv, new_w_out, new_w_in, new_w_down = (news[0].transpose(planes),) + tuple(news[1:])
+    right_qkv, right_out, right_in, right_down = rights
+    new_basis_qkv = right_qkv.transpose(planes)
+    grad_vectors = small_sum[:6]
+    grad_unit_bias = small_sum[6, :unit_slab]
+    grad_head_bias = small_sum[7, : 2 * head_slab].reshape(2, head_slab)
     new_mom_head_bias = 0.9 * mom_head_bias + grad_head_bias
-    new_mom_out = 0.9 * mom_out + rank_out
-    new_mom_in = 0.9 * mom_in + rank_in
     new_mom_unit_bias = 0.9 * mom_unit_bias + grad_unit_bias
-    new_mom_down = 0.9 * mom_down + rank_down
     new_mom_vectors = 0.9 * mom_vectors + grad_vectors
-    new_w_qkv = w_qkv.astype(jnp.float32) - step_rate * new_mom_qkv
     new_head_bias = head_bias - step_rate * new_mom_head_bias
-    new_w_out = w_out.astype(jnp.float32) - step_rate * new_mom_out
-    new_w_in = w_in.astype(jnp.float32) - step_rate * new_mom_in
     new_unit_bias = unit_bias - step_rate * new_mom_unit_bias
-    new_w_down = w_down.astype(jnp.float32) - step_rate * new_mom_down
     new_vectors = vectors - step_rate * new_mom_vectors
     return (
         layer_out,

time: 1280 us -> 978 us (0.76)
  other arithmetic: 359 us -> 105 us
  blocking collectives: 109 us -> 0 us
  Pallas kernels: 0 us -> 64 us
  waiting for transfers between devices: 425 us -> 461 us
  matrix products: 242 us -> 210 us
  between operations: 37 us -> 15 us
  local copies, waits for them, and re-layouts: 94.7 us -> 114 us
    reduce_sum x60 -> x1, other arithmetic: 156 us -> 1.45 us  [local(): jnp.sum(grad_value.astype(jnp.float32), axis=0)]
    psum x3 -> x0, blocking collectives: 109 us -> none  [the longest x1 37.9 us: local(): lax.psum(left_of(combined_qkv, basis_qkv.reshape(rank_size, 3 * head_slab...]
    div x12 -> x0, other arithmetic: 71.3 us -> none  [the longest x4 70.6 us: orthonormal(): column / (jnp.sqrt(jnp.sum(column * column, axis=-1, keepdims=True)) + EP...]
    pallas_call x0 -> x5, Pallas kernels: none -> 64 us  [the longest x1 27.3 us: update(): pl.pallas_call(partial(update_kernel, step_rate, out_steps), grid=(steps,...]
    dot_general x12 -> x0, matrix products: 37.9 us -> none  [the longest x4 11.4 us: left_of(): lax.dot_general(matrix, factor, (((1,), (1,)), ((), ())), precision=PRECI...]
    psum x1, waiting for transfers between devices: 117 us -> 153 us  [local(): grad_first = lax.psum(times_trans(grad_hidden, w_in), 'tensor') + grad_sum]
    sub x4 -> x0, other arithmetic: 29 us -> none  [the longest x1 12.2 us: local(): new_w_in = w_in.astype(jnp.float32) - step_rate * new_mom_in]
    unnamed x139 -> x177, local copies, waits for them, and re-layouts: 33.3 us -> 42.3 us
  transfers between devices with their start and end apart: 4 -> 4, of which waited for: 3 -> 3; matrix products, arithmetic and copies ran while one was open for 14% -> 5% of each run, Pallas kernels for 0% -> 0%
where the time goes in v1:
time: 978 us; the launch traced here: 970 us
  waiting for transfers between devices  461 us (47%)
  matrix products  210 us (21%)
  local copies, waits for them, and re-layouts  114 us (12%)
  other arithmetic  105 us (11%)
  Pallas kernels  64 us (7%)
  between operations  15 us (2%)
    psum x1, waiting for transfers between devices, local(): lax.psum(jnp.dot(mixed_flat, w_out, preferred_element_type=jnp.float32),...  155 us
    psum x1, waiting for transfers between devices, local(): lax.psum(jnp.dot(active_low, w_down, preferred_element_type=jnp.float32),...  153 us
    psum x1, waiting for transfers between devices, local(): grad_first = lax.psum(times_trans(grad_hidden, w_in), 'tensor') + grad_sum  153 us
    unnamed x177, local copies, waits for them, and re-layouts  42.3 us
    dot_general x4, matrix products, masked_scores(): jnp.einsum('qhd,khd->hqk', queries, key_heads, preferred_element_type=jnp...  35.2 us
    dot_general x2, matrix products, attend_backward(): jnp.einsum('qhd,khd->hqk', grad_mixed, value_heads, preferred_element_typ...  30.3 us
    dot_general x4, matrix products, times_trans(): lax.dot_general(left_side, right_side, (((1,), (1,)), ((), ())), preferre...  29.9 us
    dot_general x4, matrix products, trans_times(): lax.dot_general(left_side, right_side, (((0,), (0,)), ((), ())), preferre...  29.9 us
  transfers between devices with their start and end apart: 4, of which 3 were waited for; matrix products, arithmetic and copies ran while one was open for 5% of the time, Pallas kernels for 0%

profile of v1, /device:TPU:0, one launch (start us, length us, event | category | flops | bytes accessed | tf_op | source)
XLA Modules:
  0.0 970.5 jit_solution(6933260766387637286)
XLA Ops:
  9.0 5.3 fusion.62
  21.6 5.1 reshape.257
  26.6 4.8 copy.100
  34.3 4.0 squeeze.49
  45.8 53.5 %while.26 = (s32[]{:T(128)}, bf16[2,1024,4,64]{1,3,2,0:T(8,128)(2,1)}, f32[2,4,1024]{2,1,0:T(4,128)S(1)}, bf16[2,1024,4,64]{1,3,2,0:T(8,128)(2,1)}, s32[2,1024]{...) while((s32[]{:T(128)}, ...), condition=%wide.region_3.4_spmd, body=%wide.region_0.3_spmd.sunk | while | flops 1112797184 | bytes 56768612 | solution.py:630
  46.7 8.3 select_reduce_fusion.2
  55.0 8.8 fusion.121
  63.7 8.9 fusion.122
  73.3 8.3 select_reduce_fusion.2
  81.6 8.8 fusion.121
  90.4 8.9 fusion.122
  102.3 4.6 fusion.79
  107.6 155.0 %all-reduce.5.cloned.1.call-done = f32[2048,1024]{1,0:T(8,128)} async-done(((f32[2048,1024]{1,0:T(8,128)}), f32[2048,1024]{1,0:T(8,128)}) %all-reduce.5.cloned.1.call-update) | async-done | bytes 8388624 | tf_op jit(solution)/shard_map/psum | solution.py:633
  262.6 5.9 fusion.65
  274.4 24.6 %multiply_convert_fusion.1 = (bf16[2048,1024]{1,0:T(8,128)(2,1)S(1)}, f32[2048,1024]{1,0:T(8,128)}, f32[2048,1024]{1,0:T(8,128)}) fusion(f32[1024]{0:T(1024)S(1)} %copy-done.81, bf16[1024,1024]{1,0:T(8,128)(2,1)S(1)} %copy-done.61, f32[2048,1024]{1,0:T(8,128)S(1)} %subtract_multiply_fusion.3, f32[1024]{0:T(1024)S(1)} %bitcast.224, f32[1024]{0:T(1024)S(1)} %bitcast.219), kind=kOutput, calls=%fused_computation.74 | convolution fusion | flops 4439670784 | bytes 31469568 | tf_op jit(solution)/shard_map/dot_general | solution.py:640
  301.0 6.6 fusion.80
  307.7 153.1 %all-reduce.7.cloned.1.call-done = f32[2048,1024]{1,0:T(8,128)} async-done(((f32[2048,1024]{1,0:T(8,128)}), f32[2048,1024]{1,0:T(8,128)}) %all-reduce.7.cloned.1.call-update) | async-done | bytes 8388624 | tf_op jit(solution)/shard_map/psum | solution.py:646
  460.9 6.9 fusion.75
  476.5 13.8 %convert_reduce_fusion = (f32[1024]{0:T(1024)}, bf16[2048,1024]{1,0:T(8,128)(2,1)S(1)}) fusion(f32[2048,1024]{1,0:T(8,128)} %get-tuple-element.305, f32[2048,1024]{1,0:T(8,128)} %get-tuple-element.321, f32[1024]{0:T(1024)S(1)} %copy-done.81, bf16[2048,1024]{1,0:T(8,128)(2,1)S(1)} %fusion.72, bf16[1024,1024]{1,0:T(8,128)(2,1)S(1)} %copy-done.63), kind=kOutput, calls=%fused_computation.64 | convolution fusion | flops 4330617856 | bytes 27271168 | tf_op jit(solution)/shard_map/dot_general | solution.py:39
  492.3 6.9 fusion.81
  499.3 153.1 %all-reduce.9.cloned.1.call-done = f32[2048,1024]{1,0:T(8,128)} async-done(((f32[2048,1024]{1,0:T(8,128)}), f32[2048,1024]{1,0:T(8,128)}) %all-reduce.9.cloned.1.call-update) | async-done | bytes 8388624 | tf_op jit(solution)/shard_map/psum | solution.py:661
  652.4 11.9 %multiply_reduce_fusion.5 = (f32[2048]{0:T(1024)S(1)}, f32[2048]{0:T(1024)S(1)}, f32[2048,1024]{1,0:T(8,128)S(1)}) fusion(f32[1024]{0:T(1024)S(1)} %bitcast.221, f32[2048,1024]{1,0:T(8,128)} %copy-done.38, f32[2048,1024]{1,0:T(8,128)} %all-reduce.9.cloned.1.call-done, f32[2048,1024]{1,0:T(8,128)} %copy-done.39, f32[2048]{0:T(1024)S(1)} %broadcast_multiply_fusion.2, ...), kind=kLoop, calls=%fused_computation.94 | loop fusion | flops 23064576 | bytes 37797888 | tf_op jit(solution)/shard_map/reduce_sum | solution.py:33
  664.4 9.5 fusion.73
  678.2 3.3 reshape.258
  687.2 96.8 %while.27 = (s32[]{:T(128)}, bf16[2,1024,4,64]{1,3,2,0:T(8,128)(2,1)}, bf16[2,1024,4,64]{1,3,2,0:T(8,128)(2,1)}, bf16[2,1024,4,64]{1,3,2,0:T(8,128)(2,1)}, bf16[...) while((s32[]{:T(128)}, ...), condition=%wide.region_17.18_spmd, body=%wide.region_15.17_spmd.sunk | while | flops 2736517120 | bytes 215156176 | solution.py:669
  688.7 9.3 fusion.131
  698.1 8.8 fusion.134
  706.9 15.1 %multiply_reduce_fusion.8 = (f32[4,1024]{1,0:T(4,128)}, f32[4,1024,1024]{1,2,0:T(8,128)}) fusion(f32[4,1024,1024]{1,2,0:T(8,128)} %fusion.131, f32[4,1024]{1,0:T(4,128)} %copy-done.60, pred[1024,1024]{0,1:T(8,128)(4,1)S(1)} %broadcast_compare_fusion.5, bf16[2,1024,4,64]{1,3,2,0:T(8,128)(2,1)} %get-tuple-element.492, s32[]{:T(128)S(6)} %copy.156, ...), kind=kOutput, calls=%fused_computation.22.clone.1 | convolution fusion | flops 553644032 | bytes 35685376 | tf_op jit(solution)/shard_map/while/body/eval_jaxpr/qhd,khd->hqk/dot_general | solution.py:556
  722.1 8.2 multiply_convert_fusion.5
  737.0 9.3 fusion.131
  746.3 8.8 fusion.134
  755.2 15.1 %multiply_reduce_fusion.8 = (f32[4,1024]{1,0:T(4,128)}, f32[4,1024,1024]{1,2,0:T(8,128)}) fusion(f32[4,1024,1024]{1,2,0:T(8,128)} %fusion.131, f32[4,1024]{1,0:T(4,128)} %copy-done.60, pred[1024,1024]{0,1:T(8,128)(4,1)S(1)} %broadcast_compare_fusion.5, bf16[2,1024,4,64]{1,3,2,0:T(8,128)(2,1)} %get-tuple-element.492, s32[]{:T(128)S(6)} %copy.156, ...), kind=kOutput, calls=%fused_computation.22.clone.1 | convolution fusion | flops 553644032 | bytes 35685376 | tf_op jit(solution)/shard_map/while/body/eval_jaxpr/qhd,khd->hqk/dot_general | solution.py:556
  770.4 8.2 multiply_convert_fusion.5
  793.2 4.5 reshape.259
  800.0 4.0 copy.126
  804.0 4.3 reshape.260
  811.7 6.9 bitcast_convert_fusion
  818.6 3.6 convert_reduce_fusion.1
  822.2 12.9 %bitcast_add_fusion.down_ref.refs_3_ = f32[1024,1024]{1,0:T(8,128)} fusion(f32[1,1024,1024]{2,1,0:T(8,128)} %param.42, bf16[2048,1024]{1,0:T(8,128)(2,1)} %copy-done.59, bf16[2048,1024]{1,0:T(8,128)(2,1)} %copy-done.48), kind=kOutput, calls=%fused_computation.95 | convolution fusion | flops 4296015872 | bytes 16777216 | tf_op jit(solution)/shard_map/dot_general | solution.py:45
  835.2 6.4 bitcast_add_fusion.1.in_ref.refs_2_
  846.3 6.2 fusion.82
  854.9 3.4 fusion.64.qkv_ref.refs_0_
  859.2 4.4 convolution_add_fusion.out_ref.refs_1_
  863.7 4.1 left_factors.1
  871.9 5.4 dynamic-slice_reduce_fusion
  877.9 16.7 %bases.1 = (f32[8,1024]{1,0:T(8,128)}, f32[8,256]{1,0:T(8,128)}, f32[8,1024]{1,0:T(8,128)}, f32[8,1024]{1,0:T(8,128)}, f32[8,1024]{1,0:T(8,128)}) custom-call(f32[8,1024]{1,0:T(8,128)} %copy-done.27, f32[8,256]{1,0:T(8,128)} %copy-done.37, f32[8,1024]{1,0:T(8,128)} %copy-done.28, f32[8,1024]{1,0:T(8,128)} %copy-done.29, f32[8,1024]{1,0:T(8,128)} %concatenate.3.small_ref), custom_call_target="tpu_custom_call" | custom-call | tf_op jit(solution)/shard_map/bases/pallas_call | solution.py:393
  911.3 13.3 %right_sums.1 = (f32[3,8,256]{2,1,0:T(8,128)}, f32[8,1024]{1,0:T(8,128)}, f32[8,1024]{1,0:T(8,128)}, f32[8,1024]{1,0:T(8,128)}) custom-call(f32[3,8,256]{2,1,0:T(8,128)} %copy-done.35, f32[8,1024]{1,0:T(8,128)} %copy-done.30, f32[8,1024]{1,0:T(8,128)} %copy-done.31, f32[8,1024]{1,0:T(8,128)} %copy-done.32), custom_call_target="tpu_custom_call" | custom-call | tf_op jit(solution)/shard_map/right_sums/pallas_call | solution.py:440
  933.8 27.3 %update.1 = (f32[3,1024,256]{2,1,0:T(8,128)}, f32[256,1024]{1,0:T(8,128)}, f32[1024,1024]{1,0:T(8,128)}, f32[1024,1024]{1,0:T(8,128)}, f32[3,1024,256]{2,1,0:T(8...) custom-call(f32[3,1024,256]{2,1,0:T(8,128)} %copy-done.2, ...), custom_call_target="tpu_custom_call" | custom-call | tf_op jit(solution)/shard_map/update/pallas_call | solution.py:521
  (307 shorter events, 122.2 us)
Async XLA Ops:
  7.2 255.4 %all-reduce.5.cloned.1.call-start = ((), (), s32[]{:S(2)}) async-start(), calls=%async_computation.1 | async-start | bytes 16777216 | tf_op jit(solution)/shard_map/psum | solution.py:633
  31.4 14.4 %copy-start.65 = (s32[2,1024]{1,0:T(2,128)S(1)}, s32[2,1024]{1,0:T(2,128)}, u32[]{:S(2)}) copy-start(s32[2,1024]{1,0:T(2,128)} %param.30) | copy-start | bytes 24580
  45.8 56.5 %copy-start.10 = (bf16[256,1024]{1,0:T(8,128)(2,1)S(1)}, bf16[256,1024]{1,0:T(8,128)(2,1)}, u32[]{:S(2)}) copy-start(bf16[256,1024]{1,0:T(8,128)(2,1)} %refs_9_.1) | copy-start | bytes 1572868
  106.9 353.9 %all-reduce.7.cloned.1.call-start = ((), (), s32[]{:S(2)}) async-start(), calls=%async_computation.2 | async-start | bytes 16777216 | tf_op jit(solution)/shard_map/psum | solution.py:646
  107.6 353.3 %copy-start.74 = (f32[1,1024]{1,0:T(1,128)}, f32[1,1024]{1,0:T(1,128)S(1)}, u32[]{:S(2)}) copy-start(f32[1,1024]{1,0:T(1,128)S(1)} %get-tuple-element.318) | copy-start | bytes 12292
  107.6 544.8 %copy-start.67 = (f32[1,1024]{1,0:T(1,128)}, f32[1,1024]{1,0:T(1,128)S(1)}, u32[]{:S(2)}) copy-start(f32[1,1024]{1,0:T(1,128)S(1)} %get-tuple-element.316) | copy-start | bytes 12292
  107.6 556.7 %copy-start.71 = (f32[1,1024]{1,0:T(1,128)}, f32[1,1024]{1,0:T(1,128)S(1)}, u32[]{:S(2)}) copy-start(f32[1,1024]{1,0:T(1,128)S(1)} %get-tuple-element.319) | copy-start | bytes 12292
  274.3 24.7 %copy-start.38 = (f32[2048,1024]{1,0:T(8,128)}, f32[2048,1024]{1,0:T(8,128)S(1)}, u32[]{:S(2)}) copy-start(f32[2048,1024]{1,0:T(8,128)S(1)} %subtract_multiply_fusion.3) | copy-start | bytes 25165828
  274.4 26.6 %copy-start.62 = (bf16[1024,1024]{1,0:T(8,128)(2,1)S(1)}, bf16[1024,1024]{1,0:T(8,128)(2,1)}, u32[]{:S(2)}) copy-start(bf16[1024,1024]{1,0:T(8,128)(2,1)} %refs_11_.1) | copy-start | bytes 6291460
  307.7 344.7 %all-reduce.9.cloned.1.call-start = ((), (), s32[]{:S(2)}) async-start(), calls=%async_computation.3 | async-start | bytes 16777216 | tf_op jit(solution)/shard_map/psum | solution.py:661
  476.5 13.8 %copy-start.48 = (bf16[2048,1024]{1,0:T(8,128)(2,1)}, bf16[2048,1024]{1,0:T(8,128)(2,1)S(1)}, u32[]{:S(2)}) copy-start(bf16[2048,1024]{1,0:T(8,128)(2,1)S(1)} %fusion.72) | copy-start | bytes 12582916
  499.2 372.6 %reduce-scatter.2.cloned.1.call-start = ((), (), s32[]{:S(2)}) async-start(), calls=%async_computation.4 | async-start | bytes 5242880 | tf_op jit(solution)/shard_map/reduce_scatter | solution.py:688
  664.3 9.6 copy-start.46
  664.4 11.5 %copy-start.11 = (bf16[256,1024]{1,0:T(8,128)(2,1)S(1)}, bf16[256,1024]{1,0:T(8,128)(2,1)}, u32[]{:S(2)}) copy-start(bf16[256,1024]{1,0:T(8,128)(2,1)} %refs_9_.1) | copy-start | bytes 1572868
  675.9 11.3 %copy-start.41 = (bf16[2,1024,4,64]{1,3,2,0:T(8,128)(2,1)S(1)}, bf16[2,1024,4,64]{1,3,2,0:T(8,128)(2,1)}, u32[]{:S(2)}) copy-start(bf16[2,1024,4,64]{1,3,2,0:T(8,128)(2,1)} %copy-done.40) | copy-start | bytes 3145732
  675.9 11.3 %copy-start.66 = (s32[2,1024]{1,0:T(2,128)S(1)}, s32[2,1024]{1,0:T(2,128)}, u32[]{:S(2)}) copy-start(s32[2,1024]{1,0:T(2,128)} %param.30) | copy-start | bytes 24580
  688.1 10.0 %copy-start.60 = (f32[4,1024]{1,0:T(4,128)}, f32[4,1024]{1,0:T(4,128)S(1)}, u32[]{:S(2)}) copy-start(f32[4,1024]{1,0:T(4,128)S(1)} %dynamic-slice_bitcast_fusion.2) | copy-start | bytes 49156 | tf_op jit(solution)/shard_map/while
  698.0 24.0 %slice-start = ((s8[16777216]{0:T(1024)(128)(4,1)}), s8[4194304]{0:T(1024)(128)(4,1)S(1)}, s32[]{:S(2)}) async-start(s8[16777216]{0:T(1024)(128)(4,1)} %bitcast.200), calls=%async_computation.5 | async-start | bytes 8388608 | tf_op jit(solution)/shard_map/while
  698.0 24.0 %slice-start.1 = ((s8[16777216]{0:T(1024)(128)(4,1)}), s8[4194304]{0:T(1024)(128)(4,1)S(1)}, s32[]{:S(2)}) async-start(s8[16777216]{0:T(1024)(128)(4,1)} %bitcast.200), calls=%async_computation.6 | async-start | bytes 8388608 | tf_op jit(solution)/shard_map/while
  706.9 15.2 %slice-start.2 = ((s8[16777216]{0:T(1024)(128)(4,1)}), s8[4194304]{0:T(1024)(128)(4,1)S(1)}, s32[]{:S(2)}) async-start(s8[16777216]{0:T(1024)(128)(4,1)} %bitcast.200), calls=%async_computation.7 | async-start | bytes 8388608 | tf_op jit(solution)/shard_map/while
  706.9 15.2 %slice-start.3 = ((s8[16777216]{0:T(1024)(128)(4,1)}), s8[4194304]{0:T(1024)(128)(4,1)S(1)}, s32[]{:S(2)}) async-start(s8[16777216]{0:T(1024)(128)(4,1)} %bitcast.200), calls=%async_computation.8 | async-start | bytes 8388608 | tf_op jit(solution)/shard_map/while
  736.4 10.0 %copy-start.60 = (f32[4,1024]{1,0:T(4,128)}, f32[4,1024]{1,0:T(4,128)S(1)}, u32[]{:S(2)}) copy-start(f32[4,1024]{1,0:T(4,128)S(1)} %dynamic-slice_bitcast_fusion.2) | copy-start | bytes 49156 | tf_op jit(solution)/shard_map/while
  737.0 9.3 copy-start.49
  746.3 24.0 %slice-start = ((s8[16777216]{0:T(1024)(128)(4,1)}), s8[4194304]{0:T(1024)(128)(4,1)S(1)}, s32[]{:S(2)}) async-start(s8[16777216]{0:T(1024)(128)(4,1)} %bitcast.200), calls=%async_computation.5 | async-start | bytes 8388608 | tf_op jit(solution)/shard_map/while
  746.3 24.0 %slice-start.1 = ((s8[16777216]{0:T(1024)(128)(4,1)}), s8[4194304]{0:T(1024)(128)(4,1)S(1)}, s32[]{:S(2)}) async-start(s8[16777216]{0:T(1024)(128)(4,1)} %bitcast.200), calls=%async_computation.6 | async-start | bytes 8388608 | tf_op jit(solution)/shard_map/while
  755.2 15.2 %slice-start.2 = ((s8[16777216]{0:T(1024)(128)(4,1)}), s8[4194304]{0:T(1024)(128)(4,1)S(1)}, s32[]{:S(2)}) async-start(s8[16777216]{0:T(1024)(128)(4,1)} %bitcast.200), calls=%async_computation.7 | async-start | bytes 8388608 | tf_op jit(solution)/shard_map/while
  755.2 15.2 %slice-start.3 = ((s8[16777216]{0:T(1024)(128)(4,1)}), s8[4194304]{0:T(1024)(128)(4,1)S(1)}, s32[]{:S(2)}) async-start(s8[16777216]{0:T(1024)(128)(4,1)} %bitcast.200), calls=%async_computation.8 | async-start | bytes 8388608 | tf_op jit(solution)/shard_map/while
  793.2 17.4 %copy-start.54 = (bf16[2048,1,256]{2,0,1:T(8,128)(2,1)S(1)}, bf16[2048,1,256]{2,0,1:T(8,128)(2,1)}, u32[]{:S(2)}) copy-start(bf16[2048,1,256]{2,0,1:T(8,128)(2,1)} %reshape.261) | copy-start | bytes 3145732
  793.2 18.4 %copy-start.8 = (bf16[1024,3,256]{2,0,1:T(8,128)(2,1)S(1)}, bf16[1024,3,256]{2,0,1:T(8,128)(2,1)}, u32[]{:S(2)}) copy-start(bf16[1024,3,256]{2,0,1:T(8,128)(2,1)} %param.31) | copy-start | bytes 4718596
  818.6 16.5 %slice-start.4 = ((s8[8388608]{0:T(1024)(128)(4,1)}), s8[4194304]{0:T(1024)(128)(4,1)S(1)}, s32[]{:S(2)}) async-start(s8[8388608]{0:T(1024)(128)(4,1)} %bitcast.202), calls=%async_computation.9 | async-start | bytes 8388608
  822.2 12.9 %slice-start.5 = ((s8[8388608]{0:T(1024)(128)(4,1)}), s8[4194304]{0:T(1024)(128)(4,1)S(1)}, s32[]{:S(2)}) async-start(s8[8388608]{0:T(1024)(128)(4,1)} %bitcast.202), calls=%async_computation.10 | async-start | bytes 8388608
  822.2 12.9 %copy-start.72 = (f32[1,1024]{1,0:T(1,128)S(1)}, f32[1,1024]{1,0:T(1,128)}, u32[]{:S(2)}) copy-start(f32[1,1024]{1,0:T(1,128)} %copy-done.71) | copy-start | bytes 12292
  822.2 12.9 %copy-start.75 = (f32[1,1024]{1,0:T(1,128)S(1)}, f32[1,1024]{1,0:T(1,128)}, u32[]{:S(2)}) copy-start(f32[1,1024]{1,0:T(1,128)} %copy-done.74) | copy-start | bytes 12292
  822.2 12.9 %copy-start.86 = (f32[1,1024,1024]{2,1,0:T(8,128)S(1)}, f32[1,1024,1024]{2,1,0:T(8,128)}, u32[]{:S(2)}) copy-start(f32[1,1024,1024]{2,1,0:T(8,128)} %param.41) | copy-start | bytes 12582916
  822.2 12.9 %copy-start.89 = (bf16[2048,1024]{1,0:T(8,128)(2,1)S(1)}, bf16[2048,1024]{1,0:T(8,128)(2,1)}, u32[]{:S(2)}) copy-start(bf16[2048,1024]{1,0:T(8,128)(2,1)} %copy-done.88) | copy-start | bytes 12582916
  859.2 38.4 %copy-start.2 = (f32[3,1024,256]{2,1,0:T(8,128)}, f32[3,1024,256]{2,1,0:T(8,128)S(1)}, u32[]{:S(2)}) copy-start(f32[3,1024,256]{2,1,0:T(8,128)S(1)} %fusion.64.qkv_ref.refs_0_) | copy-start | bytes 9437188
  870.3 26.0 %copy-start.70 = (f32[6,1024]{1,0:T(8,128)S(1)}, f32[6,1024]{1,0:T(8,128)}, u32[]{:S(2)}) copy-start(f32[6,1024]{1,0:T(8,128)} %param.37) | copy-start | bytes 73732
  870.3 26.0 %copy-start.73 = (f32[6,1024]{1,0:T(8,128)S(1)}, f32[6,1024]{1,0:T(8,128)}, u32[]{:S(2)}) copy-start(f32[6,1024]{1,0:T(8,128)} %param.53) | copy-start | bytes 73732
  877.3 47.4 %copy-start.79 = (f32[2,256]{1,0:T(2,128)S(1)}, f32[2,256]{1,0:T(2,128)}, u32[]{:S(2)}) copy-start(f32[2,256]{1,0:T(2,128)} %param.32) | copy-start | bytes 6148
  877.3 47.4 %copy-start.85 = (f32[2,256]{1,0:T(2,128)S(1)}, f32[2,256]{1,0:T(2,128)}, u32[]{:S(2)}) copy-start(f32[2,256]{1,0:T(2,128)} %param.48) | copy-start | bytes 6148
  877.3 48.0 %copy-start.82 = (f32[1024]{0:T(1024)S(1)}, f32[1024]{0:T(1024)}, u32[]{:S(2)}) copy-start(f32[1024]{0:T(1024)} %param.35) | copy-start | bytes 12292
  877.3 48.0 %copy-start.83 = (f32[1024]{0:T(1024)S(1)}, f32[1024]{0:T(1024)}, u32[]{:S(2)}) copy-start(f32[1024]{0:T(1024)} %param.51) | copy-start | bytes 12292
  894.7 31.2 %copy-start.15 = (f32[8,1024]{1,0:T(8,128)S(1)}, f32[8,1024]{1,0:T(8,128)}, u32[]{:S(2)}) copy-start(f32[8,1024]{1,0:T(8,128)} %get-tuple-element.165.bq_ref.refs_12_) | copy-start | bytes 98308
  894.7 31.2 %copy-start.17 = (f32[8,1024]{1,0:T(8,128)S(1)}, f32[8,1024]{1,0:T(8,128)}, u32[]{:S(2)}) copy-start(f32[8,1024]{1,0:T(8,128)} %get-tuple-element.167.bi_ref.refs_14_) | copy-start | bytes 98308
  894.7 31.2 %copy-start.19 = (f32[8,1024]{1,0:T(8,128)S(1)}, f32[8,1024]{1,0:T(8,128)}, u32[]{:S(2)}) copy-start(f32[8,1024]{1,0:T(8,128)} %get-tuple-element.168.bd_ref.refs_15_) | copy-start | bytes 98308
  894.7 31.2 %copy-start.34 = (f32[8,256]{1,0:T(8,128)S(1)}, f32[8,256]{1,0:T(8,128)}, u32[]{:S(2)}) copy-start(f32[8,256]{1,0:T(8,128)} %get-tuple-element.166.bo_ref.refs_13_) | copy-start | bytes 24580
  896.2 64.8 %copy-start.76 = (f32[1,1024]{1,0:T(1,128)}, f32[1,1024]{1,0:T(1,128)S(1)}, u32[]{:S(2)}) copy-start(f32[1,1024]{1,0:T(1,128)S(1)} %slice.57) | copy-start | bytes 12292
  896.2 64.8 %copy-start.80 = (f32[2,256]{1,0:T(2,128)}, f32[2,256]{1,0:T(2,128)S(1)}, u32[]{:S(2)}) copy-start(f32[2,256]{1,0:T(2,128)S(1)} %reshape_squeeze.3) | copy-start | bytes 6148
  (64 other events, 233.3 us)
Sparse Core Ops, SparseCore 0:
  107.0 155.5 all-reduce.4
  307.8 153.0 all-reduce.6
  499.3 152.9 all-reduce.8
  818.7 44.6 reduce-scatter.1

commit v2 on v1

--- a/solution.py
+++ b/solution.py
@@ -572,6 +572,686 @@
         grad_query.astype(jnp.bfloat16),
         grad_key.astype(jnp.bfloat16),
         grad_value.astype(jnp.bfloat16),
+    )
+
+
+def stacked_heads(pair, lane_is_low):
+    zero = jnp.zeros_like(pair)
+    return jnp.concatenate(
+        [jnp.where(lane_is_low, pair, zero), jnp.where(lane_is_low, zero, pair)], axis=0
+    )
+
+
+def own_blocks(both):
+    rows = both.shape[1] // 2
+    return jnp.concatenate([both[:DH, :rows], both[DH:, rows:]], axis=0).T
+
+
+def mask_bias(seg_key_ref, seg_query_ref):
+    same = seg_key_ref[...] == seg_query_ref[...]
+    bias = jnp.where(same, 0.0, MASKED)
+    return jnp.concatenate([bias, bias], axis=1)
+
+
+def attend_kernel(place_ref, q_ref, k_ref, v_ref, seg_key_ref, seg_query_ref, mixed_ref, log_ref,
+                  value_t):
+    @pl.when(pl.program_id(0) == 0)
+    def _():
+        value_t[...] = v_ref[...].T
+
+    pairs = q_ref.shape[1] // LANES
+    lane_is_low = lax.broadcasted_iota(jnp.int32, (1, LANES), 1) < DH
+    bias = mask_bias(seg_key_ref, seg_query_ref)
+    for pair in range(pairs):
+        lanes = slice(pair * LANES, (pair + 1) * LANES)
+        queries = stacked_heads(q_ref[:, lanes], lane_is_low)
+        scores = dot_nt(k_ref[:, lanes], queries) + bias
+        highest = jnp.max(scores, axis=0, keepdims=True)
+        powers = jnp.exp(scores - highest)
+        denominator = jnp.sum(powers, axis=0, keepdims=True)
+        weights = (powers * (1.0 / denominator)).astype(jnp.bfloat16)
+        mixed_ref[:, lanes] = own_blocks(dot_nn(value_t[lanes], weights)).astype(jnp.bfloat16)
+        log_total = highest + jnp.log(denominator)
+        log_ref[2 * pair : 2 * pair + 1] = log_total[:, :LANES]
+        log_ref[2 * pair + 1 : 2 * pair + 2] = log_total[:, LANES:]
+
+
+def attend(projected, seg_keys, seg_queries, place):
+    length = seg_keys.shape[1]
+    slab = projected.shape[2]
+    blocks = length // LANES
+    grid_spec = pltpu.PrefetchScalarGridSpec(
+        num_scalar_prefetch=1,
+        grid=(blocks,),
+        in_specs=[
+            pl.BlockSpec((None, LANES, slab), lambda i, at: (0, at[0] * blocks + i, 0)),
+            pl.BlockSpec((None, length, slab), lambda i, at: (1, at[0], 0)),
+            pl.BlockSpec((None, length, slab), lambda i, at: (2, at[0], 0)),
+            pl.BlockSpec((None, length, LANES), lambda i, at: (at[0], 0, 0)),
+            pl.BlockSpec((None, 1, LANES), lambda i, at: (at[0], 0, i)),
+        ],
+        out_specs=[
+            pl.BlockSpec((LANES, slab), lambda i, at: (i, 0)),
+            pl.BlockSpec((slab // DH, LANES), lambda i, at: (0, i)),
+        ],
+        scratch_shapes=[pltpu.VMEM((slab, length), jnp.bfloat16)],
+    )
+    return pl.pallas_call(
+        attend_kernel,
+        grid_spec=grid_spec,
+        out_shape=[
+            jax.ShapeDtypeStruct((length, slab), jnp.bfloat16),
+            jax.ShapeDtypeStruct((slab // DH, length), jnp.float32),
+        ],
+        compiler_params=pltpu.CompilerParams(vmem_limit_bytes=32 << 20),
+        cost_estimate=pl.CostEstimate(
+            flops=16 * length * length * slab, bytes_accessed=8 * length * slab,
+            transcendentals=length * length * slab // DH,
+        ),
+        name="attend",
+    )(place.reshape(1), projected, projected, projected, seg_keys, seg_queries)
+
+
+def attend_back_kernel(place_ref, q_ref, k_ref, v_ref, seg_key_ref, seg_query_ref, gm_ref, log_ref,
+                       old_ref, grad_ref, sums_ref, key_t, grad_key, grad_value):
+    del old_ref
+    step = pl.program_id(0)
+
+    @pl.when(step == 0)
+    def _():
+        key_t[...] = k_ref[...].T
+        grad_key[...] = jnp.zeros_like(grad_key)
+        grad_value[...] = jnp.zeros_like(grad_value)
+
+    pairs = q_ref.shape[1] // LANES
+    lane_is_low = lax.broadcasted_iota(jnp.int32, (1, LANES), 1) < DH
+    bias = mask_bias(seg_key_ref, seg_query_ref)
+    head_scale = 1.0 / math.sqrt(DH)
+    here = pl.ds(pl.multiple_of(step * LANES, LANES), LANES)
+    for pair in range(pairs):
+        lanes = slice(pair * LANES, (pair + 1) * LANES)
+        queries = stacked_heads(q_ref[:, lanes], lane_is_low)
+        grads = stacked_heads(gm_ref[:, lanes], lane_is_low)
+        log_total = jnp.concatenate(
+            [log_ref[2 * pair : 2 * pair + 1], log_ref[2 * pair + 1 : 2 * pair + 2]], axis=1
+        )
+        probs = jnp.exp(dot_nt(k_ref[:, lanes], queries) + (bias - log_total))
+        grad_probs = dot_nt(v_ref[:, lanes], grads)
+        centre = jnp.sum(probs * grad_probs, axis=0, keepdims=True)
+        grad_scores = (probs * (grad_probs - centre)).astype(jnp.bfloat16)
+        grad_value[:, lanes] += dot_nn(probs.astype(jnp.bfloat16), grads)
+        grad_key[:, lanes] += dot_nn(grad_scores, queries)
+        grad_query = own_blocks(dot_nn(key_t[lanes], grad_scores)).astype(jnp.bfloat16)
+        grad_ref[0, here, lanes] = (grad_query.astype(jnp.float32) * head_scale).astype(
+            jnp.bfloat16
+        )
+
+    @pl.when(step == pl.num_programs(0) - 1)
+    def _():
+        grad_ref[1] = grad_key[...].astype(jnp.bfloat16)
+        low_value = grad_value[...].astype(jnp.bfloat16)
+        grad_ref[2] = low_value
+        sums_ref[0:1] = jnp.sum(grad_ref[0].astype(jnp.float32), axis=0, keepdims=True)
+        sums_ref[1:2] = jnp.sum(low_value.astype(jnp.float32), axis=0, keepdims=True)
+
+
+def attend_back(projected, seg_keys, seg_queries, grad_halves, log_total, old, place, core):
+    length = seg_keys.shape[1]
+    slab = projected.shape[2]
+    blocks = length // LANES
+    half = blocks // 2
+    grid_spec = pltpu.PrefetchScalarGridSpec(
+        num_scalar_prefetch=1,
+        grid=(blocks,),
+        in_specs=[
+            pl.BlockSpec((None, LANES, slab), lambda i, at: (0, at[0] * blocks + i, 0)),
+            pl.BlockSpec((None, length, slab), lambda i, at: (1, at[0], 0)),
+            pl.BlockSpec((None, length, slab), lambda i, at: (2, at[0], 0)),
+            pl.BlockSpec((None, length, LANES), lambda i, at: (at[0], 0, 0)),
+            pl.BlockSpec((None, 1, LANES), lambda i, at: (at[0], 0, i)),
+            pl.BlockSpec(
+                (None, LANES, slab), lambda i, at: (lax.rem(i // half + at[1], 2), lax.rem(i, half), 0)
+            ),
+            pl.BlockSpec((slab // DH, LANES), lambda i, at: (0, i)),
+            pl.BlockSpec(memory_space=pl.ANY),
+        ],
+        out_specs=[
+            pl.BlockSpec((3, length, slab), lambda i, at: (0, at[0], 0)),
+            pl.BlockSpec((2, slab), lambda i, at: (0, 0)),
+        ],
+        scratch_shapes=[
+            pltpu.VMEM((slab, length), jnp.bfloat16),
+            pltpu.VMEM((length, slab), jnp.float32),
+            pltpu.VMEM((length, slab), jnp.float32),
+        ],
+    )
+    return pl.pallas_call(
+        attend_back_kernel,
+        grid_spec=grid_spec,
+        out_shape=[
+            jax.ShapeDtypeStruct(projected.shape, jnp.bfloat16),
+            jax.ShapeDtypeStruct((2, slab), jnp.float32),
+        ],
+        input_output_aliases={8: 0},
+        compiler_params=pltpu.CompilerParams(vmem_limit_bytes=40 << 20),
+        cost_estimate=pl.CostEstimate(
+            flops=40 * length * length * slab, bytes_accessed=16 * length * slab,
+            transcendentals=length * length * slab // DH,
+        ),
+        name="attend_back",
+    )(jnp.stack([place, core]), projected, projected, projected, seg_keys, seg_queries, grad_halves,
+      log_total, old)
+
+
+def row_mean(values):
+    return jnp.mean(values, axis=-1, keepdims=True)
+
+
+def ffn_kernel(mixed_own, mixed_one, mixed_two, mixed_three, tokens, cotangent, out_own, out_one,
+               out_two, out_three, in_own, in_near, in_far, down_own, down_near, down_far,
+               bias_ref, vec_ref,
+               result_ref, low_out, active_out, branch_out, hidden_out, norm_out, attn_out,
+               mixed_out, unit_ref, sums_ref,
+               w_out, w_in, w_down, tok, cot, first, normed, inverse, low, slope, active, part,
+               other, other_two, acc, wide, branch, hidden, result, grad_h1, attn, mixed,
+               load_sem, store_sem, send_sem, recv_sem):
+    dp_place = lax.axis_index("dp")
+    tensor_place = lax.axis_index("tensor")
+    core = lax.rem(tensor_place, 2)
+    sibling = (dp_place, tensor_place + 1 - 2 * core)
+    side = lax.rem(dp_place, 2)
+    share, width = tok.shape
+    slab = in_own.shape[1]
+    own_rows = pl.ds(pl.multiple_of(tensor_place * share, LANES), share)
+    near_rows = pl.ds(pl.multiple_of(side * (width // 2), LANES), width // 2)
+    far_rows = pl.ds(pl.multiple_of((1 - side) * (width // 2), LANES), width // 2)
+    near_units = pl.ds(pl.multiple_of(slab + side * (slab // 2), LANES), slab // 2)
+    far_units = pl.ds(pl.multiple_of(slab + (1 - side) * (slab // 2), LANES), slab // 2)
+
+    loads = [
+        (out_own, w_out.at[0]), (out_one, w_out.at[1]), (out_two, w_out.at[2]),
+        (out_three, w_out.at[3]), (tokens.at[own_rows], tok),
+        (in_own, w_in.at[0]), (in_near, w_in.at[1, near_rows]), (in_far, w_in.at[1, far_rows]),
+        (down_own, w_down.at[pl.ds(0, slab)]), (down_near, w_down.at[near_units]),
+        (down_far, w_down.at[far_units]), (cotangent.at[own_rows], cot),
+    ]
+    loads = [
+        pltpu.make_async_copy(source, target, load_sem.at[number])
+        for number, (source, target) in enumerate(loads)
+    ]
+    for load in loads:
+        load.start()
+    stores = []
+
+    def store(source, target):
+        copy = pltpu.make_async_copy(source, target, store_sem.at[len(stores)])
+        copy.start()
+        stores.append(copy)
+
+    def send(number, source, target):
+        return pltpu.make_async_remote_copy(
+            src_ref=source,
+            dst_ref=target,
+            send_sem=send_sem.at[number],
+            recv_sem=recv_sem.at[number],
+            device_id=sibling,
+            device_id_type=MESH,
+        )
+
+    barrier = pltpu.get_barrier_semaphore()
+    pl.semaphore_signal(barrier, inc=1, device_id=sibling, device_id_type=MESH)
+    pl.semaphore_wait(barrier, 1)
+    sums_ref[...] = jnp.zeros_like(sums_ref)
+    unit_ref[...] = jnp.zeros_like(unit_ref)
+    pieces = (mixed_own, mixed_one, mixed_two, mixed_three)
+    for load in loads[:5]:
+        load.wait()
+    big = 256
+    small = 64
+
+    def attn_rows(step, carry):
+        rows = pl.ds(pl.multiple_of(step * big, big), big)
+        total = dot_nn(pieces[0][rows], w_out[0])
+        for piece in range(1, 4):
+            total += dot_nn(pieces[piece][rows], w_out[piece])
+        acc[rows] = total
+        return carry
+
+    def first_rows(step, carry):
+        rows = pl.ds(pl.multiple_of(step * small, small), small)
+        values = tok[rows].astype(jnp.float32) + (acc[rows] + vec_ref[0:1])
+        centred = values - row_mean(values)
+        scale = lax.rsqrt(row_mean(centred * centred) + EPS_NORM)
+        unit = centred * scale
+        normed[rows] = unit
+        inverse[rows] = scale
+        shifted = unit * vec_ref[2:3] + vec_ref[3:4]
+        first[rows] = shifted
+        low[0, rows] = shifted.astype(jnp.bfloat16)
+        return carry
+
+    lax.fori_loop(0, share // big, attn_rows, 0)
+    lax.fori_loop(0, share // small, first_rows, 0)
+    low_send = send(0, low.at[0], low.at[1])
+    low_send.start()
+    for load in loads[5:8]:
+        load.wait()
+    chunk = 256
+    half_chunks = slab // chunk
+
+    def hidden_of(slot):
+        def units(step, carry):
+            part_of = step // half_chunks
+            inner = pl.ds(pl.multiple_of(lax.rem(step, half_chunks) * chunk, chunk), chunk)
+            outer = pl.ds(pl.multiple_of(step * chunk, chunk), chunk)
+            values = dot_nn(low[slot], w_in[part_of, :, inner]) + bias_ref[:, outer]
+            share_of = 0.5 * (1.0 + lax.erf(values * math.sqrt(0.5)))
+            density = jnp.exp(-0.5 * values * values) * (1.0 / math.sqrt(2.0 * math.pi))
+            active[slot, :, outer] = (values * share_of).astype(jnp.bfloat16)
+            slope[slot, :, outer] = share_of + values * density
+            return carry
+
+        lax.fori_loop(0, 2 * half_chunks, units, 0)
+
+    def branch_of(slot, target):
+        def columns(step, carry):
+            at = pl.ds(pl.multiple_of(step * chunk, chunk), chunk)
+            target[:, at] = dot_nn(active[slot], w_down[:, at])
+            return carry
+
+        lax.fori_loop(0, width // chunk, columns, 0)
+
+    hidden_of(0)
+    low_send.wait_recv()
+    hidden_of(1)
+    store(low, low_out)
+    store(active, active_out)
+    for load in loads[8:]:
+        load.wait()
+    branch_of(1, part)
+    part_send = send(1, part, other)
+    part_send.start()
+    branch_of(0, acc)
+    part_send.wait_recv()
+
+    def second_rows(step, carry):
+        rows = pl.ds(pl.multiple_of(step * small, small), small)
+        values = first[rows] + (acc[rows] + other[rows]) + vec_ref[1:2]
+        centred = values - row_mean(values)
+        scale = lax.rsqrt(row_mean(centred * centred) + EPS_NORM)
+        unit = centred * scale
+        result[rows] = (unit * vec_ref[4:5] + vec_ref[5:6]).astype(jnp.bfloat16)
+        upper = cot[rows].astype(jnp.float32)
+        scaled = upper * vec_ref[4:5]
+        grad = scale * (scaled - row_mean(scaled) - unit * row_mean(scaled * unit))
+        wide[rows] = grad
+        grad_low = grad.astype(jnp.bfloat16)
+        branch[0, rows] = grad_low
+        sums_ref[1:2] += jnp.sum(grad_low.astype(jnp.float32), axis=0, keepdims=True)
+        sums_ref[4:5] += jnp.sum(upper * unit, axis=0, keepdims=True)
+        sums_ref[5:6] += jnp.sum(upper, axis=0, keepdims=True)
+        return carry
+
+    lax.fori_loop(0, share // small, second_rows, 0)
+    branch_send = send(2, branch.at[0], branch.at[1])
+    branch_send.start()
+    store(result, result_ref)
+
+    def grad_hidden_of(slot):
+        def units(step, carry):
+            outer = pl.ds(pl.multiple_of(step * chunk, chunk), chunk)
+            grad = dot_nt(branch[slot], w_down[outer]) * slope[slot, :, outer]
+            grad_low = grad.astype(jnp.bfloat16)
+            hidden[slot, :, outer] = grad_low
+            unit_ref[:, outer] += jnp.sum(grad_low.astype(jnp.float32), axis=0, keepdims=True)
+            return carry
+
+        lax.fori_loop(0, 2 * half_chunks, units, 0)
+
+    def grad_first_of(slot, target):
+        def columns(step, carry):
+            at = pl.ds(pl.multiple_of(step * chunk, chunk), chunk)
+            target[:, at] = dot_nt(hidden[slot, :, :slab], w_in[0, at]) + dot_nt(
+                hidden[slot, :, slab:], w_in[1, at]
+            )
+            return carry
+
+        lax.fori_loop(0, width // chunk, columns, 0)
+
+    grad_hidden_of(0)
+    branch_send.wait_recv()
+    store(branch, branch_out)
+    grad_hidden_of(1)
+    store(hidden, hidden_out)
+    part_send.wait_send()
+    grad_first_of(1, part)
+    first_send = send(3, part, other_two)
+    first_send.start()
+    grad_first_of(0, acc)
+    first_send.wait_recv()
+
+    def back_rows(step, carry):
+        rows = pl.ds(pl.multiple_of(step * small, small), small)
+        grad = acc[rows] + other_two[rows] + wide[rows]
+        unit = normed[rows]
+        scaled = grad * vec_ref[2:3]
+        back = inverse[rows] * (scaled - row_mean(scaled) - unit * row_mean(scaled * unit))
+        grad_h1[rows] = back
+        back_low = back.astype(jnp.bfloat16)
+        attn[rows] = back_low
+        sums_ref[0:1] += jnp.sum(back_low.astype(jnp.float32), axis=0, keepdims=True)
+        sums_ref[2:3] += jnp.sum(grad * unit, axis=0, keepdims=True)
+        sums_ref[3:4] += jnp.sum(grad, axis=0, keepdims=True)
+        return carry
+
+    lax.fori_loop(0, share // small, back_rows, 0)
+    store(grad_h1, norm_out)
+    store(attn, attn_out)
+
+    def mixed_rows(step, carry):
+        rows = pl.ds(pl.multiple_of(step * big, big), big)
+        for piece in range(4):
+            mixed[piece, rows] = dot_nt(attn[rows], w_out[piece]).astype(jnp.bfloat16)
+        return carry
+
+    lax.fori_loop(0, share // big, mixed_rows, 0)
+    store(mixed, mixed_out)
+    low_send.wait_send()
+    branch_send.wait_send()
+    first_send.wait_send()
+    for copy in stores:
+        copy.wait()
+
+
+def ffn(pieces, tokens, cotangent, w_out, w_in, w_down, bias, vectors):
+    share, piece_width = pieces[0].shape
+    width = tokens.shape[1]
+    slab = w_in[0].shape[1]
+    units = 2 * slab
+    low_type, full_type = jnp.bfloat16, jnp.float32
+    vmem = pl.BlockSpec(memory_space=pltpu.VMEM)
+    anywhere = pl.BlockSpec(memory_space=pl.ANY)
+    shapes = [
+        jax.ShapeDtypeStruct((share, width), low_type),
+        jax.ShapeDtypeStruct((2, share, width), low_type),
+        jax.ShapeDtypeStruct((2, share, units), low_type),
+        jax.ShapeDtypeStruct((2, share, width), low_type),
+        jax.ShapeDtypeStruct((2, share, units), low_type),
+        jax.ShapeDtypeStruct((share, width), full_type),
+        jax.ShapeDtypeStruct((share, width), low_type),
+        jax.ShapeDtypeStruct((4, share, piece_width), low_type),
+        jax.ShapeDtypeStruct((1, units), full_type),
+        jax.ShapeDtypeStruct((6, width), full_type),
+    ]
+    return pl.pallas_call(
+        ffn_kernel,
+        in_specs=[vmem] * 4 + [anywhere] * 12 + [vmem] * 2,
+        out_specs=[anywhere] * 8 + [vmem] * 2,
+        out_shape=shapes,
+        scratch_shapes=[
+            pltpu.VMEM((4, piece_width, width), low_type),
+            pltpu.VMEM((2, width, slab), low_type),
+            pltpu.VMEM((units, width), low_type),
+            pltpu.VMEM((share, width), low_type),
+            pltpu.VMEM((share, width), low_type),
+            pltpu.VMEM((share, width), full_type),
+            pltpu.VMEM((share, width), full_type),
+            pltpu.VMEM((share, 1), full_type),
+            pltpu.VMEM((2, share, width), low_type),
+            pltpu.VMEM((2, share, units), full_type),
+            pltpu.VMEM((2, share, units), low_type),
+            pltpu.VMEM((share, width), full_type),
+            pltpu.VMEM((share, width), full_type),
+            pltpu.VMEM((share, width), full_type),
+            pltpu.VMEM((share, width), full_type),
+            pltpu.VMEM((share, width), full_type),
+            pltpu.VMEM((2, share, width), low_type),
+            pltpu.VMEM((2, share, units), low_type),
+            pltpu.VMEM((share, width), low_type),
+            pltpu.VMEM((share, width), full_type),
+            pltpu.VMEM((share, width), low_type),
+            pltpu.VMEM((4, share, piece_width), low_type),
+            pltpu.SemaphoreType.DMA((12,)),
+            pltpu.SemaphoreType.DMA((8,)),
+            pltpu.SemaphoreType.DMA((4,)),
+            pltpu.SemaphoreType.DMA((4,)),
+        ],
+        compiler_params=pltpu.CompilerParams(
+            collective_id=3, has_side_effects=True, vmem_limit_bytes=60 << 20
+        ),
+        cost_estimate=pl.CostEstimate(
+            flops=2 * share * width * (8 * units + 8 * piece_width),
+            bytes_accessed=60 * share * width, transcendentals=4 * share * units,
+        ),
+        name="ffn",
+    )(*pieces, tokens, cotangent, *w_out, *w_in, *w_down, bias, vectors)
+
+
+def layer_general(tokens, segments, w_qkv, head_bias, w_out, w_in, unit_bias, w_down, vectors,
+                  cotangent):
+    token_count, model_width = tokens.shape
+    seq_count, length = segments.shape
+    head_slab = w_qkv.shape[2]
+    head_count = head_slab // DH
+    tensor_size = lax.axis_size("tensor")
+    share_rows = token_count // tensor_size
+    tensor_place = lax.axis_index("tensor")
+    row_start = tensor_place * share_rows
+    head_scale = 1.0 / math.sqrt(DH)
+
+    def own_rows(values):
+        return lax.dynamic_slice_in_dim(values, row_start, share_rows, 0)
+
+    flat_qkv = w_qkv.reshape(model_width, 3 * head_slab)
+    projected = jnp.dot(tokens, flat_qkv, preferred_element_type=jnp.float32).reshape(
+        token_count, 3, head_slab
+    )
+    head_shape = (seq_count, length, head_count, DH)
+    queries = (
+        ((projected[:, 0] + head_bias[0]) * head_scale).astype(jnp.bfloat16).reshape(head_shape)
+    )
+    key_heads = projected[:, 1].astype(jnp.bfloat16).reshape(head_shape)
+    value_heads = (projected[:, 2] + head_bias[1]).astype(jnp.bfloat16).reshape(head_shape)
+    mixed_heads, log_total = lax.map(attend_forward, (queries, key_heads, value_heads, segments))
+    mixed_flat = mixed_heads.reshape(token_count, head_slab)
+    attn_out = (
+        lax.psum(jnp.dot(mixed_flat, w_out, preferred_element_type=jnp.float32), "tensor")
+        + vectors[0]
+    )
+    first_norm, first_normed, first_inverse = norm_forward(
+        tokens.astype(jnp.float32) + attn_out, vectors[2], vectors[3]
+    )
+    first_low = first_norm.astype(jnp.bfloat16)
+    hidden = jnp.dot(first_low, w_in, preferred_element_type=jnp.float32) + unit_bias
+    active, gelu_back = jax.vjp(partial(jax.nn.gelu, approximate=False), hidden)
+    active_low = active.astype(jnp.bfloat16)
+    grad_out_share = own_rows(cotangent).astype(jnp.float32)
+    summed_input = (
+        first_norm
+        + lax.psum(jnp.dot(active_low, w_down, preferred_element_type=jnp.float32), "tensor")
+        + vectors[1]
+    )
+    second_norm, second_normed, second_inverse = norm_forward(summed_input, vectors[4], vectors[5])
+    layer_out = own_rows(second_norm).astype(jnp.bfloat16)
+    grad_sum = norm_backward(
+        cotangent.astype(jnp.float32), second_normed, second_inverse, vectors[4]
+    )
+    grad_branch = grad_sum.astype(jnp.bfloat16)
+    second_share = own_rows(second_normed)
+    grad_w_down = trans_times(active_low, grad_branch)
+    grad_active = times_trans(grad_branch, w_down)
+    grad_hidden = gelu_back(grad_active)[0].astype(jnp.bfloat16)
+    grad_w_in = trans_times(first_low, grad_hidden)
+    grad_units = jnp.sum(grad_hidden.astype(jnp.float32), axis=0)
+    grad_first = lax.psum(times_trans(grad_hidden, w_in), "tensor") + grad_sum
+    grad_h1 = norm_backward(grad_first, first_normed, first_inverse, vectors[2])
+    grad_attn = grad_h1.astype(jnp.bfloat16)
+    grad_first_share = own_rows(grad_first)
+    first_normed_share = own_rows(first_normed)
+    grad_h1_share = own_rows(grad_h1)
+    grad_w_out = trans_times(mixed_flat, grad_attn)
+    grad_mixed = times_trans(grad_attn, w_out).astype(jnp.bfloat16).reshape(head_shape)
+    grad_query, grad_key, grad_value = lax.map(
+        attend_backward, (queries, key_heads, value_heads, segments, grad_mixed, log_total)
+    )
+    grad_query = (
+        grad_query.reshape(token_count, head_slab).astype(jnp.float32) * head_scale
+    ).astype(jnp.bfloat16)
+    grad_key = grad_key.reshape(token_count, head_slab)
+    grad_value = grad_value.reshape(token_count, head_slab)
+    grad_projected = jnp.stack([grad_query, grad_key, grad_value], axis=1).reshape(
+        token_count, 3 * head_slab
+    )
+    grad_w_qkv = trans_times(tokens, grad_projected)
+    grad_heads = jnp.stack(
+        [
+            jnp.sum(grad_query.astype(jnp.float32), axis=0),
+            jnp.sum(grad_value.astype(jnp.float32), axis=0),
+        ]
+    )
+    grad_tokens = (
+        lax.psum_scatter(
+            times_trans(grad_projected, flat_qkv).astype(jnp.bfloat16),
+            "tensor",
+            scatter_dimension=0,
+            tiled=True,
+        ).astype(jnp.float32)
+        + grad_h1_share
+    )
+    local_vectors = jnp.stack(
+        [
+            jnp.sum(own_rows(grad_attn).astype(jnp.float32), axis=0),
+            jnp.sum(own_rows(grad_branch).astype(jnp.float32), axis=0),
+            jnp.sum(grad_first_share * first_normed_share, axis=0),
+            jnp.sum(grad_first_share, axis=0),
+            jnp.sum(grad_out_share * second_share, axis=0),
+            jnp.sum(grad_out_share, axis=0),
+        ]
+    )
+    return (
+        layer_out,
+        grad_tokens,
+        (
+            grad_w_qkv.reshape(model_width, 3, head_slab).transpose(1, 0, 2),
+            grad_w_out,
+            grad_w_in,
+            grad_w_down,
+        ),
+        local_vectors,
+        grad_heads,
+        grad_units,
+    )
+
+
+def layer_split(tokens, segments, w_qkv, head_bias, w_out, w_in, unit_bias, w_down, vectors,
+                cotangent):
+    token_count, model_width = tokens.shape
+    seq_count, length = segments.shape
+    head_slab = w_qkv.shape[2]
+    unit_slab = w_in.shape[1]
+    tensor_size = lax.axis_size("tensor")
+    replicas = lax.axis_size("dp")
+    share = token_count // tensor_size
+    tensor_place = lax.axis_index("tensor")
+    core = lax.rem(tensor_place, 2)
+    seq = tensor_place // 2
+    side = lax.rem(lax.axis_index("dp"), 2)
+    head_scale = 1.0 / math.sqrt(DH)
+
+    def to(values, step):
+        return lax.ppermute(
+            values, "tensor", [(place, place ^ step) for place in range(tensor_size)]
+        )
+
+    def across(values):
+        return lax.ppermute(values, "dp", [(place, place ^ 1) for place in range(replicas)])
+
+    def rows_at(values, number, size):
+        return lax.dynamic_slice_in_dim(values, number * size, size, 0)
+
+    in_near = to(rows_at(w_in, side, model_width // 2), 2)
+    out_two = to(w_out, 2)
+    down_near = to(rows_at(w_down, side, unit_slab // 2), 2)
+    in_far = across(in_near)
+    down_far = across(down_near)
+    bias_two = to(unit_bias, 2)
+    out_one, out_three = to(jnp.stack([w_out, out_two]), 1)
+
+    planes = w_qkv.transpose(1, 0, 2)
+    shift = jnp.stack([head_bias[0], jnp.zeros_like(head_bias[0]), head_bias[1]])
+    scale = jnp.array([head_scale, 1.0, 1.0], jnp.float32)
+    projected = jnp.einsum("td,gdn->gtn", tokens, planes, preferred_element_type=jnp.float32)
+    projected = ((projected + shift[:, None]) * scale[:, None, None]).astype(jnp.bfloat16)
+    seg_keys = jnp.broadcast_to(segments[:, :, None], (seq_count, length, LANES))
+    seg_queries = segments[:, None, :]
+    mixed_far, log_far = attend(projected, seg_keys, seg_queries, 1 - seq)
+    piece_two = to(rows_at(mixed_far, core, share), 2)
+    piece_three = to(rows_at(mixed_far, 1 - core, share), 3)
+    mixed_near, log_near = attend(projected, seg_keys, seg_queries, seq)
+    piece_one = to(rows_at(mixed_near, 1 - core, share), 1)
+    pieces = (rows_at(mixed_near, core, share), piece_one, piece_two, piece_three)
+
+    (layer_out, low, active, grad_branch, grad_hidden, grad_h1, grad_attn, grad_mixed, units, sums
+     ) = ffn(
+        pieces,
+        tokens,
+        cotangent,
+        (w_out, out_one, out_two, out_three),
+        (w_in, in_near, in_far),
+        (w_down, down_near, down_far),
+        jnp.concatenate([unit_bias, bias_two])[None],
+        vectors,
+    )
+    low = low.reshape(2 * share, model_width)
+    active = active.reshape(2 * share, 2 * unit_slab)
+    grad_branch = grad_branch.reshape(2 * share, model_width)
+    grad_hidden = grad_hidden.reshape(2 * share, 2 * unit_slab)
+    mixed_one = to(grad_mixed[1], 1)
+    mixed_two = to(grad_mixed[2], 2)
+    mixed_three = to(grad_mixed[3], 3)
+    down_two = to(trans_times(active[:, unit_slab:], grad_branch).astype(jnp.bfloat16), 2)
+    in_two = to(trans_times(low, grad_hidden[:, unit_slab:]).astype(jnp.bfloat16), 2)
+    outs = [trans_times(piece, grad_attn) for piece in pieces]
+    back_one, back_three = to(jnp.stack([outs[1], outs[3]]), 1)
+    out_back = to((outs[2] + back_three).astype(jnp.bfloat16), 2)
+    unit_two = to(units[0, unit_slab:], 2)
+
+    grad_projected = jnp.zeros_like(projected)
+    grad_projected, heads_near = attend_back(
+        projected, seg_keys, seg_queries, jnp.stack([grad_mixed[0], mixed_one]), log_near,
+        grad_projected, seq, core,
+    )
+    grad_projected, heads_far = attend_back(
+        projected, seg_keys, seg_queries, jnp.stack([mixed_two, mixed_three]), log_far,
+        grad_projected, 1 - seq, core,
+    )
+    token_part = jnp.einsum(
+        "gtn,gdn->td", grad_projected, planes, preferred_element_type=jnp.float32
+    ).astype(jnp.bfloat16)
+    other_one = to(
+        jnp.stack([rows_at(token_part, 2 * at + 1 - core, share) for at in (seq, 1 - seq)]), 1
+    ).astype(jnp.float32)
+    across_part = rows_at(token_part, 2 * (1 - seq) + core, share).astype(jnp.float32)
+    from_two = to((across_part + other_one[1]).astype(jnp.bfloat16), 2)
+    grad_tokens = (
+        rows_at(token_part, 2 * seq + core, share).astype(jnp.float32)
+        + other_one[0]
+        + from_two.astype(jnp.float32)
+        + grad_h1
+    )
+    grad_w_qkv = jnp.einsum(
+        "td,gtn->gdn", tokens, grad_projected, preferred_element_type=jnp.float32
+    )
+    grad_w_down = trans_times(active[:, :unit_slab], grad_branch) + down_two.astype(jnp.float32)
+    grad_w_in = trans_times(low, grad_hidden[:, :unit_slab]) + in_two.astype(jnp.float32)
+    grad_w_out = outs[0] + back_one + out_back.astype(jnp.float32)
+    return (
+        layer_out,
+        grad_tokens,
+        (grad_w_qkv, grad_w_out, grad_w_in, grad_w_down),
+        sums,
+        heads_near + heads_far,
+        units[0, :unit_slab] + unit_two,
     )
 
 
@@ -603,106 +1283,16 @@
     mom_vectors,
 ):
     token_count, model_width = tokens.shape
-    seq_count, length = segments.shape
     head_slab = w_qkv.shape[2]
-    head_count = head_slab // DH
     unit_slab = w_in.shape[1]
     tensor_size = lax.axis_size("tensor")
     replicas = lax.axis_size("dp")
-    share_rows = token_count // tensor_size
-    tensor_place = lax.axis_index("tensor")
-    row_start = tensor_place * share_rows
-    head_scale = 1.0 / math.sqrt(DH)
-
-    def own_rows(values):
-        return lax.dynamic_slice_in_dim(values, row_start, share_rows, 0)
-
-    flat_qkv = w_qkv.reshape(model_width, 3 * head_slab)
-    projected = jnp.dot(tokens, flat_qkv, preferred_element_type=jnp.float32).reshape(
-        token_count, 3, head_slab
-    )
-    head_shape = (seq_count, length, head_count, DH)
-    queries = (
-        ((projected[:, 0] + head_bias[0]) * head_scale).astype(jnp.bfloat16).reshape(head_shape)
-    )
-    key_heads = projected[:, 1].astype(jnp.bfloat16).reshape(head_shape)
-    value_heads = (projected[:, 2] + head_bias[1]).astype(jnp.bfloat16).reshape(head_shape)
-    mixed_heads, log_total = lax.map(attend_forward, (queries, key_heads, value_heads, segments))
-    mixed_flat = mixed_heads.reshape(token_count, head_slab)
-    attn_out = (
-        lax.psum(jnp.dot(mixed_flat, w_out, preferred_element_type=jnp.float32), "tensor")
-        + vectors[0]
-    )
-    first_norm, first_normed, first_inverse = norm_forward(
-        tokens.astype(jnp.float32) + attn_out, vectors[2], vectors[3]
-    )
-    first_low = first_norm.astype(jnp.bfloat16)
-    hidden = jnp.dot(first_low, w_in, preferred_element_type=jnp.float32) + unit_bias
-    active, gelu_back = jax.vjp(partial(jax.nn.gelu, approximate=False), hidden)
-    active_low = active.astype(jnp.bfloat16)
-    grad_out_share = own_rows(cotangent).astype(jnp.float32)
-    summed_input = (
-        first_norm
-        + lax.psum(jnp.dot(active_low, w_down, preferred_element_type=jnp.float32), "tensor")
-        + vectors[1]
-    )
-    second_norm, second_normed, second_inverse = norm_forward(summed_input, vectors[4], vectors[5])
-    layer_out = own_rows(second_norm).astype(jnp.bfloat16)
-    grad_sum = norm_backward(
-        cotangent.astype(jnp.float32), second_normed, second_inverse, vectors[4]
-    )
-    grad_branch = grad_sum.astype(jnp.bfloat16)
-    second_share = own_rows(second_normed)
-    grad_w_down = trans_times(active_low, grad_branch)
-    grad_active = times_trans(grad_branch, w_down)
-    grad_hidden = gelu_back(grad_active)[0].astype(jnp.bfloat16)
-    grad_w_in = trans_times(first_low, grad_hidden)
-    grad_units = jnp.sum(grad_hidden.astype(jnp.float32), axis=0)
-    grad_first = lax.psum(times_trans(grad_hidden, w_in), "tensor") + grad_sum
-    grad_h1 = norm_backward(grad_first, first_normed, first_inverse, vectors[2])
-    grad_attn = grad_h1.astype(jnp.bfloat16)
-    grad_first_share = own_rows(grad_first)
-    first_normed_share = own_rows(first_normed)
-    grad_h1_share = own_rows(grad_h1)
-    grad_w_out = trans_times(mixed_flat, grad_attn)
-    grad_mixed = times_trans(grad_attn, w_out).astype(jnp.bfloat16).reshape(head_shape)
-    grad_query, grad_key, grad_value = lax.map(
-        attend_backward, (queries, key_heads, value_heads, segments, grad_mixed, log_total)
-    )
-    grad_query = (
-        grad_query.reshape(token_count, head_slab).astype(jnp.float32) * head_scale
-    ).astype(jnp.bfloat16)
-    grad_key = grad_key.reshape(token_count, head_slab)
-    grad_value = grad_value.reshape(token_count, head_slab)
-    grad_projected = jnp.stack([grad_query, grad_key, grad_value], axis=1).reshape(
-        token_count, 3 * head_slab
-    )
-    grad_w_qkv = trans_times(tokens, grad_projected)
-    grad_heads = jnp.stack(
-        [
-            jnp.sum(grad_query.astype(jnp.float32), axis=0),
-            jnp.sum(grad_value.astype(jnp.float32), axis=0),
-        ]
-    )
-    grad_tokens = (
-        lax.psum_scatter(
-            times_trans(grad_projected, flat_qkv).astype(jnp.bfloat16),
-            "tensor",
-            scatter_dimension=0,
-            tiled=True,
-        ).astype(jnp.float32)
-        + grad_h1_share
-    )
-    local_vectors = jnp.stack(
-        [
-            jnp.sum(own_rows(grad_attn).astype(jnp.float32), axis=0),
-            jnp.sum(own_rows(grad_branch).astype(jnp.float32), axis=0),
-            jnp.sum(grad_first_share * first_normed_share, axis=0),
-            jnp.sum(grad_first_share, axis=0),
-            jnp.sum(grad_out_share * second_share, axis=0),
-            jnp.sum(grad_out_share, axis=0),
-        ]
-    )
+    one_sequence_per_chip = 2 * segments.shape[0] == tensor_size and replicas % 2 == 0
+    layer = layer_split if one_sequence_per_chip else layer_general
+    layer_out, grad_tokens, grads, local_vectors, grad_heads, grad_units = layer(
+        tokens, segments, w_qkv, head_bias, w_out, w_in, unit_bias, w_down, vectors, cotangent
+    )
+    grad_w_qkv, grad_w_out, grad_w_in, grad_w_down = grads
     small = jnp.concatenate(
         [
             local_vectors,
@@ -712,9 +1302,7 @@
         axis=0,
     )
     planes = (1, 0, 2)
-    combined_qkv = grad_w_qkv.reshape(model_width, 3, head_slab).transpose(planes) + err_qkv[
-        0
-    ].transpose(planes)
+    combined_qkv = grad_w_qkv + err_qkv[0].transpose(planes)
     combined_out = grad_w_out + err_out[0]
     combined_in = grad_w_in + err_in[0]
     combined_down = grad_w_down + err_down[0]

time: 978 us -> 364 us (0.37)
  waiting for transfers between devices: 461 us -> 69.7 us
  matrix products: 210 us -> 38.3 us
  Pallas kernels: 64 us -> 174 us
  other arithmetic: 105 us -> 10.5 us
  local copies, waits for them, and re-layouts: 114 us -> 43.8 us
  starting transfers between devices: 0.16 us -> 20.5 us
  between operations: 15 us -> 1.66 us
    psum x3 -> x0, waiting for transfers between devices: 461 us -> none  [the longest x1 155 us: local(): lax.psum(jnp.dot(mixed_flat, w_out, preferred_element_type=jnp.float32),...]
    dot_general x22 -> x3, matrix products: 180 us -> 17.5 us  [the longest x1 7.35 us: layer_split(): jnp.einsum('td,gdn->gtn', tokens, planes, preferred_element_type=jnp.floa...]
    pallas_call x0 -> x5, Pallas kernels: none -> 108 us  [the longest x1 45.5 us: ffn(): pl.pallas_call(ffn_kernel, in_specs=[vmem] * 4 + [anywhere] * 12 + [vmem]...]
    ppermute x0 -> x20, waiting for transfers between devices: none -> 69.7 us  [the longest x18 69.7 us: to(): lax.ppermute(values, 'tensor', [(place, place ^ step) for place in range(...]
    reduce_sum x13 -> x0, other arithmetic: 62 us -> none  [the longest x2 17.6 us: attend_forward(): denominator = jnp.sum(powers, axis=-1, keepdims=True)]
    convert_element_type x6 -> x2, other arithmetic: 33.2 us -> 1.83 us  [the longest x1 1.38 us: layer_split(): from_two = to((across_part + other_one[1]).astype(jnp.bfloat16), 2)]
    ppermute x0 -> x20, starting transfers between devices: none -> 20.5 us  [the longest x18 16.8 us: to(): lax.ppermute(values, 'tensor', [(place, place ^ step) for place in range(...]
    another operation x12 -> x3, local copies, waits for them, and re-layouts: 22.3 us -> 2.49 us  [the longest x1 2.23 us: layer_split(): out_one, out_three = to(jnp.stack([w_out, out_two]), 1)]
  transfers between devices with their start and end apart: 4 -> 20, of which waited for: 3 -> 6; matrix products, arithmetic and copies ran while one was open for 5% -> 16% of each run, Pallas kernels for 0% -> 36%
where the time goes in v2:
time: 364 us; the launch traced here: 359 us
  Pallas kernels  174 us (48%)
  waiting for transfers between devices  69.7 us (19%)
  local copies, waits for them, and re-layouts  43.8 us (12%)
  matrix products  38.3 us (11%)
  starting transfers between devices  20.5 us (6%)
  other arithmetic  10.5 us (3%)
    ppermute x18, waiting for transfers between devices, to(): lax.ppermute(values, 'tensor', [(place, place ^ step) for place in range(...  69.7 us
    pallas_call x1, Pallas kernels, ffn(): pl.pallas_call(ffn_kernel, in_specs=[vmem] * 4 + [anywhere] * 12 + [vmem]...  45.5 us
    pallas_call x2, Pallas kernels, attend_back(): pl.pallas_call(attend_back_kernel, grid_spec=grid_spec, out_shape=[jax.Sh...  32 us
    unnamed x162, local copies, waits for them, and re-layouts  31.8 us
    pallas_call x2, Pallas kernels, attend(): pl.pallas_call(attend_kernel, grid_spec=grid_spec, out_shape=[jax.ShapeDt...  30.2 us
    pallas_call x1, Pallas kernels, update(): pl.pallas_call(partial(update_kernel, step_rate, out_steps), grid=(steps,...  28.7 us
    dot_general x8, matrix products, trans_times(): lax.dot_general(left_side, right_side, (((0,), (0,)), ((), ())), preferre...  20.8 us
    pallas_call x1, Pallas kernels, bases_of(): pl.pallas_call(partial(basis_kernel, replicas, tensor_size), in_specs=[vm...  17.7 us
  transfers between devices with their start and end apart: 20, of which 6 were waited for; matrix products, arithmetic and copies ran while one was open for 16% of the time, Pallas kernels for 36%

profile of v2, /device:TPU:0, one launch (start us, length us, event | category | flops | bytes accessed | tf_op | source)
XLA Modules:
  0.0 358.6 jit_solution(17770335126988828056)
XLA Ops:
  0.7 3.0 collective-permute-start.3
  3.7 2.3 constant_dynamic-slice_fusion.1
  6.1 2.3 constant_dynamic-slice_fusion
  8.4 1.9 collective-permute-start.7
  10.5 7.4 %fusion.4.q_ref.k_ref.v_ref = bf16[3,2048,256]{2,1,0:T(8,128)(2,1)} fusion(f32[3]{0:T(128)S(1)} %copy-done.77, f32[3,256]{1,0:T(4,128)S(1)} %pad_maximum_fusion.6, bf16[2048,1024]{1,0:T(8,128)(2,1)} %tokens.1, bf16[1024,3,256]{2,0,1:T(8,128)(2,1)S(1)} %copy-done.10), kind=kOutput, calls=%fused_computation.8 | convolution fusion | flops 3225944064 | bytes 8915980 | tf_op jit(solution)/shard_map/td,gdn->gtn/dot_general | solution.py:1183
  20.3 15.2 %attend.2 = (bf16[1024,256]{1,0:T(8,128)(2,1)S(1)}, f32[4,1024]{1,0:T(4,128)S(1)}) custom-call(s32[1]{0:T(128)} %bitcast.place_ref, bf16[3,2048,256]{2,1,0:T(8,128)(2,1)S(1)} %copy-done.37, bf16[3,2048,256]{2,1,0:T(8,128)(2,1)S(1)} %copy-done.37, bf16[3,2048,256]{2,1,0:T(8,128)(2,1)S(1)} %copy-done.37, s32[2,1024,128]{2,1,0:T(8,128)S(1)} %broadcast_in_dim.32.seg_key_ref, ...), custom_call_target="tpu_custom_call" | custom-call | flops 4294967296 | bytes 2097152 | tf_op jit(solution)/shard_map/attend/pallas_call | solution.py:639
  36.7 2.6 collective-permute-done.5.in_near
  39.3 2.0 collective-permute-start.6
  41.3 19.7 %collective-permute-done.7.down_near = bf16[512,1024]{1,0:T(8,128)(2,1)} collective-permute-done((bf16[512,1024]{1,0:T(8,128)(2,1)}, bf16[512,1024]{1,0:T(8,128)(2,1)}, u32[]{:S(2)}, u32[]{:S(2)}) %collective-permute-start.7) | collective-permute-done | bytes 1048608 | tf_op jit(solution)/shard_map/ppermute | solution.py:1162
  61.0 1.7 collective-permute-start.8
  62.8 1.9 copy-done.38
  64.6 15.0 %attend.3 = (bf16[1024,256]{1,0:T(8,128)(2,1)S(1)}, f32[4,1024]{1,0:T(4,128)S(1)}) custom-call(s32[1]{0:T(128)} %bitcast.4.place_ref, bf16[3,2048,256]{2,1,0:T(8,128)(2,1)S(1)} %copy-done.38, bf16[3,2048,256]{2,1,0:T(8,128)(2,1)S(1)} %copy-done.38, bf16[3,2048,256]{2,1,0:T(8,128)(2,1)S(1)} %copy-done.38, s32[2,1024,128]{2,1,0:T(8,128)S(1)} %broadcast_in_dim.32.seg_key_ref, ...), custom_call_target="tpu_custom_call" | custom-call | flops 4294967296 | bytes 2097152 | tf_op jit(solution)/shard_map/attend/pallas_call | solution.py:639
  80.5 1.6 collective-permute-start.1
  82.7 2.2 slice_bitcast_fusion.4
  85.0 4.4 %collective-permute-done.1.mixed_two = bf16[512,256]{1,0:T(8,128)(2,1)S(1)} collective-permute-done((bf16[512,256]{1,0:T(8,128)(2,1)}, bf16[512,256]{1,0:T(8,128)(2,1)S(1)}, u32[]{:S(2)}, u32[]{:S(2)}) %collective-permute-start.1) | collective-permute-done | bytes 262176 | tf_op jit(solution)/shard_map/ppermute | solution.py:1162
  89.3 3.1 collective-permute-done.2.mixed_three
  93.1 45.5 %ffn.1 = (bf16[512,1024]{1,0:T(8,128)(2,1)}, bf16[2,512,1024]{2,1,0:T(8,128)(2,1)}, bf16[2,512,2048]{2,1,0:T(8,128)(2,1)}, bf16[2,512,1024]{2,1,0:T(8,128)(2,1)}...) custom-call(bf16[512,256]{1,0:T(8,128)(2,1)} %get-tuple-element.151., ...), custom_call_target="tpu_custom_call" | custom-call | flops 19327352832 | bytes 31457280 | tf_op jit(solution)/shard_map/ffn/pallas_call | solution.py:986
  138.7 1.4 fusion.37
  140.0 1.9 collective-permute-start.11
  142.4 1.8 convolution_bitcast_fusion
  145.5 1.5 collective-permute-start.19
  147.1 3.7 %fusion.20 = bf16[1024,1024]{1,0:T(8,128)(2,1)} fusion(bf16[1024,1024]{1,0:T(8,128)(2,1)S(1)} %bitcast.148, bf16[1024,2048]{1,0:T(8,128)(2,1)S(1)} %bitcast.144), kind=kOutput, calls=%fused_computation.27 | convolution fusion | flops 2148532224 | bytes 6291456 | tf_op jit(solution)/shard_map/dot_general | solution.py:45
  150.8 3.7 %fusion.23 = bf16[1024,1024]{1,0:T(8,128)(2,1)} fusion(bf16[1024,1024]{1,0:T(8,128)(2,1)S(1)} %bitcast.145, bf16[1024,2048]{1,0:T(8,128)(2,1)S(1)} %bitcast.141), kind=kOutput, calls=%fused_computation.28 | convolution fusion | flops 2148532224 | bytes 6291456 | tf_op jit(solution)/shard_map/dot_general | solution.py:45
  154.5 1.5 collective-permute-start.17
  156.9 16.0 %attend_back.2 = (bf16[3,2048,256]{2,1,0:T(8,128)(2,1)S(1)}, f32[2,256]{1,0:T(2,128)S(1)}) custom-call(s32[2]{0:T(128)S(1)} %pad_add_fusion.1.place_ref, bf16[3,2048,256]{2,1,0:T(8,128)(2,1)S(1)} %copy-done.39, bf16[3,2048,256]{2,1,0:T(8,128)(2,1)S(1)} %copy-done.39, bf16[3,2048,256]{2,1,0:T(8,128)(2,1)S(1)} %copy-done.39, ...), custom_call_target="tpu_custom_call", output_to_operand_aliasing={{0}: (8, {})} | custom-call | flops 10737418240 | bytes 4194304 | tf_op jit(solution)/shard_map/attend_back/pallas_call | solution.py:728
  172.9 16.0 %attend_back.3 = (bf16[3,2048,256]{2,1,0:T(8,128)(2,1)S(1)}, f32[2,256]{1,0:T(2,128)S(1)}) custom-call(s32[2]{0:T(128)S(1)} %pad_add_fusion.place_ref, bf16[3,2048,256]{2,1,0:T(8,128)(2,1)S(1)} %copy-done.39, bf16[3,2048,256]{2,1,0:T(8,128)(2,1)S(1)} %copy-done.39, bf16[3,2048,256]{2,1,0:T(8,128)(2,1)S(1)} %copy-done.39, ...), custom_call_target="tpu_custom_call", output_to_operand_aliasing={{0}: (8, {})} | custom-call | flops 10737418240 | bytes 4194304 | tf_op jit(solution)/shard_map/attend_back/pallas_call | solution.py:728
  188.9 4.2 %bitcast_convert_fusion = bf16[2048,1024]{1,0:T(8,128)(2,1)S(1)} fusion(bf16[3,2048,256]{2,1,0:T(8,128)(2,1)S(1)} %get-tuple-element.89, bf16[1024,3,256]{2,0,1:T(8,128)(2,1)S(1)} %copy-done.10), kind=kOutput, calls=%fused_computation | convolution fusion | flops 3223322624 | bytes 8912896 | tf_op jit(solution)/shard_map/gtn,gdn->td/dot_general | solution.py:1228
  193.7 3.2 copy-done.68
  196.9 6.0 %bitcast_add_fusion.2.qkv_ref.refs_0_ = f32[3,1024,256]{2,1,0:T(8,128)S(1)} fusion(f32[1,1024,3,256]{3,1,2,0:T(8,128)} %param.36, bf16[3,2048,256]{2,1,0:T(8,128)(2,1)S(1)} %get-tuple-element.89, bf16[2048,1024]{1,0:T(8,128)(2,1)S(1)} %copy-done.68), kind=kOutput, calls=%fused_computation.9 | convolution fusion | flops 3222011904 | bytes 13631488 | tf_op jit(solution)/shard_map/td,gtn->gdn/dot_general | solution.py:1242
  204.1 1.6 collective-permute-start.16
  205.7 6.2 %bitcast_add_fusion.1.in_ref.refs_2_ = f32[1024,1024]{1,0:T(8,128)S(1)} fusion(f32[1,1024,1024]{2,1,0:T(8,128)S(1)} %copy-done.69, bf16[1024,1024]{1,0:T(8,128)(2,1)} %collective-permute-done.17, bf16[1024,1024]{1,0:T(8,128)(2,1)} %bitcast.147, bf16[1024,2048]{1,0:T(8,128)(2,1)} %bitcast.143), kind=kOutput, calls=%fused_computation.3 | convolution fusion | flops 2150629376 | bytes 14680064 | tf_op jit(solution)/shard_map/dot_general | solution.py:45
  211.9 36.3 %collective-permute-done.18 = bf16[1024,1024]{1,0:T(8,128)(2,1)} collective-permute-done((bf16[1024,1024]{1,0:T(8,128)(2,1)}, bf16[1024,1024]{1,0:T(8,128)(2,1)}, u32[]{:S(2)}, u32[]{:S(2)}) %collective-permute-start.18) | collective-permute-done | bytes 2097184 | tf_op jit(solution)/shard_map/ppermute | solution.py:1162
  248.2 4.0 %bitcast_add_fusion.down_ref.refs_3_ = f32[1024,1024]{1,0:T(8,128)S(1)} fusion(f32[1,1024,1024]{2,1,0:T(8,128)S(1)} %copy-done.70, bf16[1024,1024]{1,0:T(8,128)(2,1)} %collective-permute-done.18, bf16[1024,1024]{1,0:T(8,128)(2,1)S(1)} %bitcast.146, bf16[1024,2048]{1,0:T(8,128)(2,1)S(1)} %bitcast.142), kind=kOutput, calls=%fused_computation.2 | convolution fusion | flops 2150629376 | bytes 14680064 | tf_op jit(solution)/shard_map/dot_general | solution.py:45
  252.8 1.4 fusion.16
  254.2 1.6 collective-permute-start.14
  255.7 3.6 %collective-permute-done.16 = bf16[256,1024]{1,0:T(8,128)(2,1)S(1)} collective-permute-done((bf16[256,1024]{1,0:T(8,128)(2,1)S(1)}, bf16[256,1024]{1,0:T(8,128)(2,1)S(1)}, u32[]{:S(2)}, u32[]{:S(2)}) %collective-permute-start.16) | collective-permute-done | bytes 524320 | tf_op jit(solution)/shard_map/ppermute | solution.py:1162
  259.9 4.3 %left_factors.1 = (f32[8,1024]{1,0:T(8,128)S(1)}, f32[8,256]{1,0:T(8,128)S(1)}, f32[8,1024]{1,0:T(8,128)S(1)}, f32[8,1024]{1,0:T(8,128)S(1)}) custom-call(f32[3,1024,256]{2,1,0:T(8,128)S(1)} %bitcast_add_fusion.2.qkv_ref.refs_0_, f32[256,1024]{1,0:T(8,128)S(1)} %fusion.33.out_ref.refs_1_, f32[1024,1024]{1,0:T(8,128)S(1)} %bitcast_add_fusion.1.in_ref.refs_2_, ...), custom_call_target="tpu_custom_call" | custom-call | tf_op jit(solution)/shard_map/left_factors/pallas_call | solution.py:119
  266.7 17.7 %bases.1 = (f32[8,1024]{1,0:T(8,128)}, f32[8,256]{1,0:T(8,128)}, f32[8,1024]{1,0:T(8,128)}, f32[8,1024]{1,0:T(8,128)}, f32[8,1024]{1,0:T(8,128)}) custom-call(f32[8,1024]{1,0:T(8,128)} %copy-done.26, f32[8,256]{1,0:T(8,128)} %copy-done.36, f32[8,1024]{1,0:T(8,128)} %copy-done.27, f32[8,1024]{1,0:T(8,128)} %copy-done.28, f32[8,1024]{1,0:T(8,128)} %select_maximum_fusion.small_ref), custom_call_target="tpu_custom_call" | custom-call | tf_op jit(solution)/shard_map/bases/pallas_call | solution.py:393
  285.9 2.2 copy-done.1
  288.1 2.2 copy-done.3
  290.3 1.2 copy-done.6
  294.5 2.6 right_factors.1
  299.6 13.1 %right_sums.1 = (f32[3,8,256]{2,1,0:T(8,128)}, f32[8,1024]{1,0:T(8,128)}, f32[8,1024]{1,0:T(8,128)}, f32[8,1024]{1,0:T(8,128)}) custom-call(f32[3,8,256]{2,1,0:T(8,128)} %copy-done.34, f32[8,1024]{1,0:T(8,128)} %copy-done.29, f32[8,1024]{1,0:T(8,128)} %copy-done.30, f32[8,1024]{1,0:T(8,128)} %copy-done.31), custom_call_target="tpu_custom_call" | custom-call | tf_op jit(solution)/shard_map/right_sums/pallas_call | solution.py:440
  312.7 1.2 copy-done.7
  315.0 1.4 copy-done.11
  316.4 1.2 copy-done.12
  320.7 28.7 %update.1 = (f32[3,1024,256]{2,1,0:T(8,128)}, f32[256,1024]{1,0:T(8,128)}, f32[1024,1024]{1,0:T(8,128)}, f32[1024,1024]{1,0:T(8,128)}, f32[3,1024,256]{2,1,0:T(8...) custom-call(f32[3,1024,256]{2,1,0:T(8,128)} %copy-done.4, ...), custom_call_target="tpu_custom_call" | custom-call | tf_op jit(solution)/shard_map/update/pallas_call | solution.py:521
  351.3 3.7 %fusion.19 = f32[512,1024]{1,0:T(8,128)} fusion(f32[512,1024]{1,0:T(8,128)S(1)} %copy-done.46, f32[2,512,1024]{2,1,0:T(8,128)S(1)} %copy-done.42, bf16[512,1024]{1,0:T(8,128)(2,1)} %collective-permute-done.14, bf16[2048,1024]{1,0:T(8,128)(2,1)} %copy-done.43, s32[]{:T(128)S(6)} %select_n.33), kind=kLoop, calls=%fused_computation.24 | loop fusion | flops 2621440 | bytes 8388612 | tf_op jit(solution)/shard_map/add | solution.py:1237
  (209 shorter events, 30.3 us)
Async XLA Ops:
  0.7 9.8 %copy-start.77 = (f32[3]{0:T(128)S(1)}, f32[3]{0:T(128)}, u32[]{:S(2)}) copy-start(f32[3]{0:T(128)} %constant.49.clone) | copy-start | bytes 40
  0.7 9.6 %copy-start.63 = (f32[2,256]{1,0:T(2,128)S(1)}, f32[2,256]{1,0:T(2,128)}, u32[]{:S(2)}) copy-start(f32[2,256]{1,0:T(2,128)} %param.29) | copy-start | bytes 6148
  0.7 9.8 %copy-start.10 = (bf16[1024,3,256]{2,0,1:T(8,128)(2,1)S(1)}, bf16[1024,3,256]{2,0,1:T(8,128)(2,1)}, u32[]{:S(2)}) copy-start(bf16[1024,3,256]{2,0,1:T(8,128)(2,1)} %param.28) | copy-start | bytes 4718596
  0.7 17.1 %collective-permute-start.3 = (bf16[256,1024]{1,0:T(8,128)(2,1)}, bf16[256,1024]{1,0:T(8,128)(2,1)S(1)}, u32[]{:S(2)}, u32[]{:S(2)}) collective-permute-start(bf16[256,1024]{1,0:T(8,128)(2,1)} %refs_9_.1), channel_id=1, source_target_pairs={{0,2},{1,3},{2,0},{3,1},{4,6},{5,7},{6,4},{7,5},{8,10},{9,11},{10,... | collective-permute-start | bytes 1572872 | tf_op jit(solution)/shard_map/ppermute | solution.py:1162
  6.0 33.3 %collective-permute-start.5 = (bf16[512,1024]{1,0:T(8,128)(2,1)}, bf16[512,1024]{1,0:T(8,128)(2,1)}, u32[]{:S(2)}, u32[]{:S(2)}) collective-permute-start(bf16[512,1024]{1,0:T(8,128)(2,1)} %constant_dynamic-slice_fusion.1), channel_id=1, source_target_pairs={{0,2},{1,3},{2,0},{3,1},{4,6},{5,7},{6,4},{7,5},{8,10},{9,11},{10,... | collective-permute-start | bytes 3145736 | tf_op jit(solution)/shard_map/ppermute | solution.py:1162
  8.4 52.6 %collective-permute-start.7 = (bf16[512,1024]{1,0:T(8,128)(2,1)}, bf16[512,1024]{1,0:T(8,128)(2,1)}, u32[]{:S(2)}, u32[]{:S(2)}) collective-permute-start(bf16[512,1024]{1,0:T(8,128)(2,1)} %constant_dynamic-slice_fusion), channel_id=1, source_target_pairs={{0,2},{1,3},{2,0},{3,1},{4,6},{5,7},{6,4},{7,5},{8,10},{9,11},{10,... | collective-permute-start | bytes 3145736 | tf_op jit(solution)/shard_map/ppermute | solution.py:1162
  18.9 63.8 %collective-permute-start.4 = (bf16[2,256,1024]{2,1,0:T(8,128)(2,1)}, bf16[2,256,1024]{2,1,0:T(8,128)(2,1)}, u32[]{:S(2)}, u32[]{:S(2)}) collective-permute-start(bf16[2,256,1024]{2,1,0:T(8,128)(2,1)} %pad_maximum_fusion.2), channel_id=1, source_target_pairs={{0,1},{1,0},{2,3},{3,2},{4,5},{5,4},{6,7},{7,6},{8,9},{9,8},{10,11... | collective-permute-start | bytes 3145736 | tf_op jit(solution)/shard_map/ppermute | solution.py:1162
  20.3 15.9 %copy-start.62 = (f32[1024]{0:T(1024)S(1)}, f32[1024]{0:T(1024)}, u32[]{:S(2)}) copy-start(f32[1024]{0:T(1024)} %param.32) | copy-start | bytes 12292
  36.2 48.7 %collective-permute-start = (bf16[512,256]{1,0:T(8,128)(2,1)S(1)}, bf16[512,256]{1,0:T(8,128)(2,1)S(1)}, u32[]{:S(2)}, u32[]{:S(2)}) collective-permute-start(bf16[512,256]{1,0:T(8,128)(2,1)S(1)} %get-tuple-element.150), channel_id=1, source_target_pairs={{0,1},{1,0},{2,3},{3,2},{4,5},{5,4},{6,7},{7,6},{8,9},{9,8},{10,11... | collective-permute-start | bytes 786440 | tf_op jit(solution)/shard_map/ppermute | solution.py:1162
  36.2 44.3 %collective-permute-start.9 = (f32[1024]{0:T(1024)S(1)}, f32[1024]{0:T(1024)S(1)}, u32[]{:S(2)}, u32[]{:S(2)}) collective-permute-start(f32[1024]{0:T(1024)S(1)} %copy-done.62), channel_id=1, source_target_pairs={{0,2},{1,3},{2,0},{3,1},{4,6},{5,7},{6,4},{7,5},{8,10},{9,11},{10,... | collective-permute-start | bytes 12296 | tf_op jit(solution)/shard_map/ppermute | solution.py:1162
  39.3 53.1 %collective-permute-start.6 = (bf16[512,1024]{1,0:T(8,128)(2,1)}, bf16[512,1024]{1,0:T(8,128)(2,1)}, u32[]{:S(2)}, u32[]{:S(2)}) collective-permute-start(bf16[512,1024]{1,0:T(8,128)(2,1)} %collective-permute-done.5.in_near), channel_id=1, source_target_pairs={{0,4},{4,0},{8,12},{12,8},{16,20},{20,16},{24,28},{28,24},{1,5},{5... | collective-permute-start | bytes 3145736 | tf_op jit(solution)/shard_map/ppermute | solution.py:1167
  61.0 31.5 %collective-permute-start.8 = (bf16[512,1024]{1,0:T(8,128)(2,1)}, bf16[512,1024]{1,0:T(8,128)(2,1)}, u32[]{:S(2)}, u32[]{:S(2)}) collective-permute-start(bf16[512,1024]{1,0:T(8,128)(2,1)} %collective-permute-done.7.down_near), channel_id=1, source_target_pairs={{0,4},{4,0},{8,12},{12,8},{16,20},{20,16},{24,28},{28,24},{1,5},{5... | collective-permute-start | bytes 3145736 | tf_op jit(solution)/shard_map/ppermute | solution.py:1167
  80.5 8.8 %collective-permute-start.1 = (bf16[512,256]{1,0:T(8,128)(2,1)}, bf16[512,256]{1,0:T(8,128)(2,1)S(1)}, u32[]{:S(2)}, u32[]{:S(2)}) collective-permute-start(bf16[512,256]{1,0:T(8,128)(2,1)} %get-tuple-element.149), channel_id=1, source_target_pairs={{0,2},{1,3},{2,0},{3,1},{4,6},{5,7},{6,4},{7,5},{8,10},{9,11},{10,... | collective-permute-start | bytes 786440 | tf_op jit(solution)/shard_map/ppermute | solution.py:1162
  82.7 9.7 %collective-permute-start.2 = (bf16[512,256]{1,0:T(8,128)(2,1)}, bf16[512,256]{1,0:T(8,128)(2,1)S(1)}, u32[]{:S(2)}, u32[]{:S(2)}) collective-permute-start(bf16[512,256]{1,0:T(8,128)(2,1)} %get-tuple-element.148), channel_id=1, source_target_pairs={{0,3},{1,2},{2,1},{3,0},{4,7},{5,6},{6,5},{7,4},{8,11},{9,10},{10,... | collective-permute-start | bytes 786440 | tf_op jit(solution)/shard_map/ppermute | solution.py:1162
  140.0 16.0 %collective-permute-start.11 = (bf16[512,256]{1,0:T(8,128)(2,1)S(1)}, bf16[512,256]{1,0:T(8,128)(2,1)S(1)}, u32[]{:S(2)}, u32[]{:S(2)}) collective-permute-start(bf16[512,256]{1,0:T(8,128)(2,1)S(1)} %get-tuple-element.144), channel_id=1, source_target_pairs={{0,3},{1,2},{2,1},{3,0},{4,7},{5,6},{6,5},{7,4},{8,11},{9,10},{10,... | collective-permute-start | bytes 786440 | tf_op jit(solution)/shard_map/ppermute | solution.py:1162
  141.9 14.7 %collective-permute-start.10 = (bf16[512,256]{1,0:T(8,128)(2,1)S(1)}, bf16[512,256]{1,0:T(8,128)(2,1)S(1)}, u32[]{:S(2)}, u32[]{:S(2)}) collective-permute-start(bf16[512,256]{1,0:T(8,128)(2,1)S(1)} %get-tuple-element.145), channel_id=1, source_target_pairs={{0,2},{1,3},{2,0},{3,1},{4,6},{5,7},{6,4},{7,5},{8,10},{9,11},{10,... | collective-permute-start | bytes 786440 | tf_op jit(solution)/shard_map/ppermute | solution.py:1162
  142.4 14.2 %collective-permute-start.12 = (bf16[512,256]{1,0:T(8,128)(2,1)S(1)}, bf16[512,256]{1,0:T(8,128)(2,1)S(1)}, u32[]{:S(2)}, u32[]{:S(2)}) collective-permute-start(bf16[512,256]{1,0:T(8,128)(2,1)S(1)} %get-tuple-element.143), channel_id=1, source_target_pairs={{0,1},{1,0},{2,3},{3,2},{4,5},{5,4},{6,7},{7,6},{8,9},{9,8},{10,11... | collective-permute-start | bytes 786440 | tf_op jit(solution)/shard_map/ppermute | solution.py:1162
  144.9 58.6 %collective-permute-start.15 = (f32[2,256,1024]{2,1,0:T(8,128)S(1)}, f32[2,256,1024]{2,1,0:T(8,128)S(1)}, u32[]{:S(2)}, u32[]{:S(2)}) collective-permute-start(f32[2,256,1024]{2,1,0:T(8,128)S(1)} %pad_maximum_fusion.1), channel_id=1, source_target_pairs={{0,1},{1,0},{2,3},{3,2},{4,5},{5,4},{6,7},{7,6},{8,9},{9,8},{10,11... | collective-permute-start | bytes 6291464 | tf_op jit(solution)/shard_map/ppermute | solution.py:1162
  145.5 9.0 %collective-permute-start.19 = (f32[1024]{0:T(1024)S(1)}, f32[1024]{0:T(1024)S(1)}, u32[]{:S(2)}, u32[]{:S(2)}) collective-permute-start(f32[1024]{0:T(1024)S(1)} %bitcast.133), channel_id=1, source_target_pairs={{0,2},{1,3},{2,0},{3,1},{4,6},{5,7},{6,4},{7,5},{8,10},{9,11},{10,... | collective-permute-start | bytes 12296 | tf_op jit(solution)/shard_map/ppermute | solution.py:1162
  154.5 51.1 %collective-permute-start.17 = (bf16[1024,1024]{1,0:T(8,128)(2,1)}, bf16[1024,1024]{1,0:T(8,128)(2,1)}, u32[]{:S(2)}, u32[]{:S(2)}) collective-permute-start(bf16[1024,1024]{1,0:T(8,128)(2,1)} %fusion.20), channel_id=1, source_target_pairs={{0,2},{1,3},{2,0},{3,1},{4,6},{5,7},{6,4},{7,5},{8,10},{9,11},{10,... | collective-permute-start | bytes 6291464 | tf_op jit(solution)/shard_map/ppermute | solution.py:1162
  156.1 92.2 %collective-permute-start.18 = (bf16[1024,1024]{1,0:T(8,128)(2,1)}, bf16[1024,1024]{1,0:T(8,128)(2,1)}, u32[]{:S(2)}, u32[]{:S(2)}) collective-permute-start(bf16[1024,1024]{1,0:T(8,128)(2,1)} %fusion.23), channel_id=1, source_target_pairs={{0,2},{1,3},{2,0},{3,1},{4,6},{5,7},{6,4},{7,5},{8,10},{9,11},{10,... | collective-permute-start | bytes 6291464 | tf_op jit(solution)/shard_map/ppermute | solution.py:1162
  193.2 59.6 %copy-start.43 = (bf16[2048,1024]{1,0:T(8,128)(2,1)}, bf16[2048,1024]{1,0:T(8,128)(2,1)S(1)}, u32[]{:S(2)}) copy-start(bf16[2048,1024]{1,0:T(8,128)(2,1)S(1)} %bitcast_convert_fusion) | copy-start | bytes 12582916
  193.6 9.3 %copy-start.58 = (f32[6,1024]{1,0:T(8,128)S(1)}, f32[6,1024]{1,0:T(8,128)}, u32[]{:S(2)}) copy-start(f32[6,1024]{1,0:T(8,128)} %get-tuple-element.100) | copy-start | bytes 73732
  193.6 10.0 %copy-start.55 = (bf16[512,256]{1,0:T(8,128)(2,1)S(1)}, bf16[512,256]{1,0:T(8,128)(2,1)}, u32[]{:S(2)}) copy-start(bf16[512,256]{1,0:T(8,128)(2,1)} %copy-done.54) | copy-start | bytes 786436
  193.6 12.1 %copy-start.69 = (f32[1,1024,1024]{2,1,0:T(8,128)S(1)}, f32[1,1024,1024]{2,1,0:T(8,128)}, u32[]{:S(2)}) copy-start(f32[1,1024,1024]{2,1,0:T(8,128)} %param.38) | copy-start | bytes 12582916
  193.6 58.6 %collective-permute-start.13 = (bf16[2,512,1024]{2,1,0:T(8,128)(2,1)S(1)}, bf16[2,512,1024]{2,1,0:T(8,128)(2,1)S(1)}, u32[]{:S(2)}, u32[]{:S(2)}) collective-permute-start(bf16[2,512,1024]{2,1,0:T(8,128)(2,1)S(1)} %pad_maximum_fusion), channel_id=1, source_target_pairs={{0,1},{1,0},{2,3},{3,2},{4,5},{5,4},{6,7},{7,6},{8,9},{9,8},{10,11... | collective-permute-start | bytes 6291464 | tf_op jit(solution)/shard_map/ppermute | solution.py:1162
  202.8 83.1 %copy-start.4 = (f32[3,1024,256]{2,1,0:T(8,128)}, f32[3,1024,256]{2,1,0:T(8,128)S(1)}, u32[]{:S(2)}) copy-start(f32[3,1024,256]{2,1,0:T(8,128)S(1)} %bitcast_add_fusion.2.qkv_ref.refs_0_) | copy-start | bytes 9437188
  203.6 8.3 %copy-start.44 = (f32[2,256,1024]{2,1,0:T(8,128)}, f32[2,256,1024]{2,1,0:T(8,128)S(1)}, u32[]{:S(2)}) copy-start(f32[2,256,1024]{2,1,0:T(8,128)S(1)} %collective-permute-done.15) | copy-start | bytes 6291460
  204.1 44.2 %copy-start.70 = (f32[1,1024,1024]{2,1,0:T(8,128)S(1)}, f32[1,1024,1024]{2,1,0:T(8,128)}, u32[]{:S(2)}) copy-start(f32[1,1024,1024]{2,1,0:T(8,128)} %param.39) | copy-start | bytes 12582916
  204.1 44.2 %copy-start.72 = (bf16[2,512,2048]{2,1,0:T(8,128)(2,1)S(1)}, bf16[2,512,2048]{2,1,0:T(8,128)(2,1)}, u32[]{:S(2)}) copy-start(bf16[2,512,2048]{2,1,0:T(8,128)(2,1)} %get-tuple-element.94) | copy-start | bytes 12582916
  204.1 44.1 %copy-start.75 = (bf16[2,512,1024]{2,1,0:T(8,128)(2,1)S(1)}, bf16[2,512,1024]{2,1,0:T(8,128)(2,1)}, u32[]{:S(2)}) copy-start(bf16[2,512,1024]{2,1,0:T(8,128)(2,1)} %get-tuple-element.95) | copy-start | bytes 6291460
  204.1 55.3 %collective-permute-start.16 = (bf16[256,1024]{1,0:T(8,128)(2,1)S(1)}, bf16[256,1024]{1,0:T(8,128)(2,1)S(1)}, u32[]{:S(2)}, u32[]{:S(2)}) collective-permute-start(bf16[256,1024]{1,0:T(8,128)(2,1)S(1)} %fusion.34), channel_id=1, source_target_pairs={{0,2},{1,3},{2,0},{3,1},{4,6},{5,7},{6,4},{7,5},{8,10},{9,11},{10,... | collective-permute-start | bytes 1572872 | tf_op jit(solution)/shard_map/ppermute | solution.py:1162
  211.9 48.0 %copy-start = (f32[1024,1024]{1,0:T(8,128)}, f32[1024,1024]{1,0:T(8,128)S(1)}, u32[]{:S(2)}) copy-start(f32[1024,1024]{1,0:T(8,128)S(1)} %bitcast_add_fusion.1.in_ref.refs_2_) | copy-start | bytes 12582916
  252.2 7.7 %copy-start.2 = (f32[1024,1024]{1,0:T(8,128)}, f32[1024,1024]{1,0:T(8,128)S(1)}, u32[]{:S(2)}) copy-start(f32[1024,1024]{1,0:T(8,128)S(1)} %bitcast_add_fusion.down_ref.refs_3_) | copy-start | bytes 12582916
  254.2 97.1 %collective-permute-start.14 = (bf16[512,1024]{1,0:T(8,128)(2,1)}, bf16[512,1024]{1,0:T(8,128)(2,1)}, u32[]{:S(2)}, u32[]{:S(2)}) collective-permute-start(bf16[512,1024]{1,0:T(8,128)(2,1)} %fusion.16), channel_id=1, source_target_pairs={{0,2},{1,3},{2,0},{3,1},{4,6},{5,7},{6,4},{7,5},{8,10},{9,11},{10,... | collective-permute-start | bytes 3145736 | tf_op jit(solution)/shard_map/ppermute | solution.py:1162
  285.2 64.9 %copy-start.61 = (f32[1,1024]{1,0:T(1,128)}, f32[1,1024]{1,0:T(1,128)S(1)}, u32[]{:S(2)}) copy-start(f32[1,1024]{1,0:T(1,128)S(1)} %slice.66) | copy-start | bytes 12292
  285.9 63.5 %copy-start.64 = (f32[2,256]{1,0:T(2,128)}, f32[2,256]{1,0:T(2,128)S(1)}, u32[]{:S(2)}) copy-start(f32[2,256]{1,0:T(2,128)S(1)} %reshape_squeeze.3) | copy-start | bytes 6148
  294.5 18.2 %copy-start.14 = (f32[8,1024]{1,0:T(8,128)S(1)}, f32[8,1024]{1,0:T(8,128)}, u32[]{:S(2)}) copy-start(f32[8,1024]{1,0:T(8,128)} %get-tuple-element.104.bq_ref.refs_12_) | copy-start | bytes 98308
  294.5 18.2 %copy-start.16 = (f32[8,1024]{1,0:T(8,128)S(1)}, f32[8,1024]{1,0:T(8,128)}, u32[]{:S(2)}) copy-start(f32[8,1024]{1,0:T(8,128)} %get-tuple-element.106.bi_ref.refs_14_) | copy-start | bytes 98308
  294.5 18.2 %copy-start.18 = (f32[8,1024]{1,0:T(8,128)S(1)}, f32[8,1024]{1,0:T(8,128)}, u32[]{:S(2)}) copy-start(f32[8,1024]{1,0:T(8,128)} %get-tuple-element.107.bd_ref.refs_15_) | copy-start | bytes 98308
  294.5 18.2 %copy-start.33 = (f32[8,256]{1,0:T(8,128)S(1)}, f32[8,256]{1,0:T(8,128)}, u32[]{:S(2)}) copy-start(f32[8,256]{1,0:T(8,128)} %get-tuple-element.105.bo_ref.refs_13_) | copy-start | bytes 24580
  320.6 28.8 %copy-start.67 = (f32[2,256]{1,0:T(2,128)S(1)}, f32[2,256]{1,0:T(2,128)}, u32[]{:S(2)}) copy-start(f32[2,256]{1,0:T(2,128)} %param.45) | copy-start | bytes 6148
  320.7 29.4 %copy-start.66 = (f32[1024]{0:T(1024)S(1)}, f32[1024]{0:T(1024)}, u32[]{:S(2)}) copy-start(f32[1024]{0:T(1024)} %param.48) | copy-start | bytes 12292
  320.7 30.0 %copy-start.56 = (f32[8,1024]{1,0:T(8,128)S(1)}, f32[8,1024]{1,0:T(8,128)}, u32[]{:S(2)}) copy-start(f32[8,1024]{1,0:T(8,128)} %get-tuple-element.117) | copy-start | bytes 98308
  320.7 30.0 %copy-start.59 = (f32[6,1024]{1,0:T(8,128)S(1)}, f32[6,1024]{1,0:T(8,128)}, u32[]{:S(2)}) copy-start(f32[6,1024]{1,0:T(8,128)} %vec_ref.1) | copy-start | bytes 73732
  320.7 30.0 %copy-start.60 = (f32[6,1024]{1,0:T(8,128)S(1)}, f32[6,1024]{1,0:T(8,128)}, u32[]{:S(2)}) copy-start(f32[6,1024]{1,0:T(8,128)} %param.50) | copy-start | bytes 73732
  320.7 30.6 %copy-start.42 = (f32[2,512,1024]{2,1,0:T(8,128)S(1)}, f32[2,512,1024]{2,1,0:T(8,128)}, u32[]{:S(2)}) copy-start(f32[2,512,1024]{2,1,0:T(8,128)} %copy-done.41) | copy-start | bytes 12582916
  320.7 30.6 %copy-start.46 = (f32[512,1024]{1,0:T(8,128)S(1)}, f32[512,1024]{1,0:T(8,128)}, u32[]{:S(2)}) copy-start(f32[512,1024]{1,0:T(8,128)} %get-tuple-element.90) | copy-start | bytes 6291460
  (50 other events, 142.4 us)

commit v3 on v2

--- a/solution.py
+++ b/solution.py
@@ -11,6 +11,7 @@
 DH = 64
 LANES = 128
 MESH = pl.DeviceIdType.MESH
+VMEM_GRANT = 60 << 20
 
 
 PRECISE = lax.Precision.HIGHEST
@@ -85,221 +86,6 @@
     matrix_high, matrix_low = split_bf16(matrix)
     both = dot_nn(jnp.concatenate([basis_high, basis_low], axis=0), matrix_high)
     return both[:rank_size] + both[rank_size:] + dot_nn(basis_high, matrix_low)
-
-
-def lefts_kernel(qkv_ref, out_ref, in_ref, down_ref, fq_ref, fo_ref, fi_ref, fd_ref,
-                 lq_ref, lo_ref, li_ref, ld_ref):
-    lq_ref[...] = (
-        left_factor(fq_ref[0], qkv_ref[0])
-        + left_factor(fq_ref[1], qkv_ref[1])
-        + left_factor(fq_ref[2], qkv_ref[2])
-    )
-    li_ref[...] = left_factor(fi_ref[...], in_ref[...])
-    ld_ref[...] = left_factor(fd_ref[...], down_ref[...])
-
-    @pl.when(pl.program_id(0) == 0)
-    def _():
-        lo_ref[...] = left_factor(fo_ref[...], out_ref[...])
-
-
-def lefts_of(matrices, factors):
-    steps = 4
-    qkv, out, inw, down = matrices
-    rank_size = factors[1].shape[0]
-
-    def whole(array):
-        return pl.BlockSpec(array.shape, lambda i: (0,) * array.ndim)
-
-    def rows(array):
-        return pl.BlockSpec((array.shape[0] // steps, array.shape[1]), lambda i: (i, 0))
-
-    def lanes(size):
-        return pl.BlockSpec((rank_size, size // steps), lambda i: (0, i))
-
-    return pl.pallas_call(
-        lefts_kernel,
-        grid=(steps,),
-        in_specs=[
-            pl.BlockSpec((3, qkv.shape[1] // steps, qkv.shape[2]), lambda i: (0, i, 0)),
-            whole(out),
-            rows(inw),
-            rows(down),
-        ]
-        + [whole(factor) for factor in factors],
-        out_specs=[
-            lanes(qkv.shape[1]),
-            pl.BlockSpec((rank_size, out.shape[0]), lambda i: (0, 0)),
-            lanes(inw.shape[0]),
-            lanes(down.shape[0]),
-        ],
-        out_shape=[
-            jax.ShapeDtypeStruct((rank_size, size), jnp.float32)
-            for size in (qkv.shape[1], out.shape[0], inw.shape[0], down.shape[0])
-        ],
-        compiler_params=pltpu.CompilerParams(vmem_limit_bytes=40 << 20),
-        name="left_factors",
-    )(qkv, out, inw, down, *factors)
-
-
-def rights_kernel(qkv_ref, out_ref, in_ref, down_ref, bq_ref, bo_ref, bi_ref, bd_ref,
-                  rq_ref, ro_ref, ri_ref, rd_ref):
-    first = pl.program_id(0) == 0
-
-    @pl.when(first)
-    def _():
-        ro_ref[...] = right_factor(bo_ref[...], out_ref[...])
-        rq_ref[...] = jnp.zeros_like(rq_ref)
-        ri_ref[...] = jnp.zeros_like(ri_ref)
-        rd_ref[...] = jnp.zeros_like(rd_ref)
-
-    for part in range(3):
-        rq_ref[part] += right_factor(bq_ref[...], qkv_ref[part])
-    ri_ref[...] += right_factor(bi_ref[...], in_ref[...])
-    rd_ref[...] += right_factor(bd_ref[...], down_ref[...])
-
-
-def rights_of(matrices, bases):
-    steps = 4
-    qkv, out, inw, down = matrices
-    rank_size = bases[0].shape[0]
-
-    def whole(shape):
-        return pl.BlockSpec(shape, lambda i: (0,) * len(shape))
-
-    def rows(array):
-        return pl.BlockSpec((array.shape[0] // steps, array.shape[1]), lambda i: (i, 0))
-
-    def lanes(array):
-        return pl.BlockSpec((rank_size, array.shape[1] // steps), lambda i: (0, i))
-
-    shapes = [(3, rank_size, qkv.shape[2])] + [(rank_size, one.shape[1]) for one in (out, inw, down)]
-    return pl.pallas_call(
-        rights_kernel,
-        grid=(steps,),
-        in_specs=[
-            pl.BlockSpec((3, qkv.shape[1] // steps, qkv.shape[2]), lambda i: (0, i, 0)),
-            whole(out.shape),
-            rows(inw),
-            rows(down),
-            lanes(bases[0]),
-            whole(bases[1].shape),
-            lanes(bases[2]),
-            lanes(bases[3]),
-        ],
-        out_specs=[whole(shape) for shape in shapes],
-        out_shape=[jax.ShapeDtypeStruct(shape, jnp.float32) for shape in shapes],
-        compiler_params=pltpu.CompilerParams(vmem_limit_bytes=40 << 20),
-        name="right_factors",
-    )(qkv, out, inw, down, *bases)
-
-
-def peer_ids(replicas, place):
-    dp_place = lax.axis_index("dp")
-    tensor_place = lax.axis_index("tensor")
-    return dp_place, tensor_place
-
-
-def greet(replicas, tensor_size):
-    dp_place = lax.axis_index("dp")
-    tensor_place = lax.axis_index("tensor")
-    barrier = pltpu.get_barrier_semaphore()
-
-    def greet_dp(step, carry):
-        pl.semaphore_signal(
-            barrier,
-            inc=1,
-            device_id=(lax.rem(dp_place + step, replicas), tensor_place),
-            device_id_type=MESH,
-        )
-        return carry
-
-    def greet_tensor(step, carry):
-        pl.semaphore_signal(
-            barrier,
-            inc=1,
-            device_id=(dp_place, lax.rem(tensor_place + step, tensor_size)),
-            device_id_type=MESH,
-        )
-        return carry
-
-    lax.fori_loop(1, replicas, greet_dp, 0)
-    if tensor_size > 1:
-        lax.fori_loop(1, tensor_size, greet_tensor, 0)
-    pl.semaphore_wait(barrier, replicas - 1 + tensor_size - 1)
-
-
-def dp_sum(replicas, mine, wire, arrived, total, send_one, recv_one, send_two, recv_two):
-    dp_place = lax.axis_index("dp")
-    tensor_place = lax.axis_index("tensor")
-
-    def scatter_to(step):
-        peer = lax.rem(dp_place + step, replicas)
-        return pltpu.make_async_remote_copy(
-            src_ref=wire.at[peer],
-            dst_ref=arrived.at[dp_place],
-            send_sem=send_one.at[step],
-            recv_sem=recv_one.at[dp_place],
-            device_id=(peer, tensor_place),
-            device_id_type=MESH,
-        )
-
-    def scatter_from(step):
-        peer = lax.rem(dp_place + step, replicas)
-        return pltpu.make_async_remote_copy(
-            src_ref=wire.at[peer],
-            dst_ref=arrived.at[peer],
-            send_sem=send_one.at[step],
-            recv_sem=recv_one.at[peer],
-            device_id=(peer, tensor_place),
-            device_id_type=MESH,
-        )
-
-    def gather_to(step):
-        peer = lax.rem(dp_place + step, replicas)
-        return pltpu.make_async_remote_copy(
-            src_ref=total.at[dp_place],
-            dst_ref=total.at[dp_place],
-            send_sem=send_two.at[step],
-            recv_sem=recv_two.at[dp_place],
-            device_id=(peer, tensor_place),
-            device_id_type=MESH,
-        )
-
-    def gather_from(step):
-        peer = lax.rem(dp_place + step, replicas)
-        return pltpu.make_async_remote_copy(
-            src_ref=total.at[dp_place],
-            dst_ref=total.at[peer],
-            send_sem=send_two.at[step],
-            recv_sem=recv_two.at[peer],
-            device_id=(peer, tensor_place),
-            device_id_type=MESH,
-        )
-
-    def start_scatter(step, carry):
-        scatter_to(step).start()
-        return carry
-
-    def add_arrived(step, carry):
-        scatter_from(step).wait_recv()
-        peer = lax.rem(dp_place + step, replicas)
-        return carry + arrived[peer].astype(jnp.float32)
-
-    def start_gather(step, carry):
-        gather_to(step).start()
-        return carry
-
-    def finish(step, carry):
-        scatter_to(step).wait_send()
-        gather_to(step).wait_send()
-        gather_from(step).wait_recv()
-        return carry
-
-    wire[...] = mine[...].astype(wire.dtype)
-    lax.fori_loop(1, replicas, start_scatter, 0)
-    total[dp_place] = lax.fori_loop(1, replicas, add_arrived, mine[dp_place])
-    lax.fori_loop(1, replicas, start_gather, 0)
-    lax.fori_loop(1, replicas, finish, 0)
 
 
 def place_tiles(target, offset, values):
@@ -334,44 +120,165 @@
     return rows
 
 
-def basis_kernel(replicas, tensor_size, lq_ref, lo_ref, li_ref, ld_ref, small_ref,
-                 bq_ref, bo_ref, bi_ref, bd_ref, sum_ref,
-                 mine, wire, arrived, total, small_slots,
-                 send_one, recv_one, send_two, recv_two, send_three, recv_three):
+def dp_exchange(replicas, mine, wire, arrived, total, sems, meanwhile=None):
+    send_one, recv_one, send_two, recv_two = sems
     dp_place = lax.axis_index("dp")
     tensor_place = lax.axis_index("tensor")
+
+    def peer_of(step):
+        return lax.rem(dp_place + step, replicas)
+
+    def scatter(step, slot):
+        return pltpu.make_async_remote_copy(
+            src_ref=wire.at[peer_of(step)],
+            dst_ref=arrived.at[slot],
+            send_sem=send_one.at[step],
+            recv_sem=recv_one.at[slot],
+            device_id=(peer_of(step), tensor_place),
+            device_id_type=MESH,
+        )
+
+    def gather(step, slot):
+        return pltpu.make_async_remote_copy(
+            src_ref=total.at[dp_place],
+            dst_ref=total.at[slot],
+            send_sem=send_two.at[step],
+            recv_sem=recv_two.at[slot],
+            device_id=(peer_of(step), tensor_place),
+            device_id_type=MESH,
+        )
+
+    def start_scatter(step, carry):
+        scatter(step, dp_place).start()
+        return carry
+
+    def add_arrived(step, carry):
+        scatter(step, peer_of(step)).wait_recv()
+        return carry + arrived[peer_of(step)].astype(jnp.float32)
+
+    def start_gather(step, carry):
+        gather(step, dp_place).start()
+        return carry
+
+    def finish(step, carry):
+        gather(step, peer_of(step)).wait_recv()
+        return carry
+
+    wire[...] = mine[...].astype(wire.dtype)
+    lax.fori_loop(1, replicas, start_scatter, 0)
+    total[dp_place] = lax.fori_loop(1, replicas, add_arrived, mine[dp_place])
+    lax.fori_loop(1, replicas, start_gather, 0)
+    lax.fori_loop(1, replicas, finish, 0)
+
+    def drain(step, carry):
+        scatter(step, dp_place).wait_send()
+        gather(step, dp_place).wait_send()
+        return carry
+
+    return lambda: lax.fori_loop(1, replicas, drain, 0)
+
+
+def compress_kernel(replicas, tensor_size, qkv_ref, out_ref, in_ref, down_ref,
+                    fq_ref, fo_ref, fi_ref, fd_ref, small_ref,
+                    bq_ref, bo_ref, bi_ref, bd_ref, rq_ref, ro_ref, ri_ref, rd_ref, sum_ref,
+                    qkv, out, inw, down, mine, wire, arrived, total,
+                    mine_two, wire_two, arrived_two, total_two, small_slots,
+                    load_sem, *sems):
+    first_sems, second_sems, (send_small, recv_small) = sems[:4], sems[4:8], sems[8:]
+    dp_place = lax.axis_index("dp")
+    tensor_place = lax.axis_index("tensor")
+    loads = [
+        pltpu.make_async_copy(source, target, load_sem.at[number])
+        for number, (source, target) in enumerate(
+            [(qkv_ref, qkv), (out_ref, out), (down_ref, down), (in_ref, inw)]
+        )
+    ]
+    for load in loads:
+        load.start()
+    barrier = pltpu.get_barrier_semaphore()
+
+    def greet_dp(step, carry):
+        pl.semaphore_signal(
+            barrier,
+            inc=1,
+            device_id=(lax.rem(dp_place + step, replicas), tensor_place),
+            device_id_type=MESH,
+        )
+        return carry
+
+    def greet_tensor(step, carry):
+        pl.semaphore_signal(
+            barrier,
+            inc=1,
+            device_id=(dp_place, lax.rem(tensor_place + step, tensor_size)),
+            device_id_type=MESH,
+        )
+        return carry
+
+    lax.fori_loop(1, replicas, greet_dp, 0)
+    lax.fori_loop(1, tensor_size, greet_tensor, 0)
     mine[...] = jnp.zeros_like(mine)
-    greet(replicas, tensor_size)
-    lefts = (lq_ref, lo_ref, li_ref, ld_ref)
+    mine_two[...] = jnp.zeros_like(mine_two)
+    block = 2 * LANES
     offset = 0
-    for ref in lefts + (small_ref,):
-        offset = place_tiles(mine, offset, ref[...])
-    dp_sum(replicas, mine, wire, arrived, total, send_one, recv_one, send_two, recv_two)
+    loads[0].wait()
+    for start in range(0, qkv.shape[1], block):
+        rows = slice(start, start + block)
+        left = left_factor(fq_ref[0], qkv[0, rows])
+        for part in range(1, 3):
+            left += left_factor(fq_ref[part], qkv[part, rows])
+        offset = place_tiles(mine, offset, left)
+    for load, factor_ref, matrix in zip(loads[1:], (fo_ref, fd_ref, fi_ref), (out, down, inw)):
+        load.wait()
+        rows_of = min(block, matrix.shape[0])
+        for start in range(0, matrix.shape[0], rows_of):
+            left = left_factor(factor_ref[...], matrix[start : start + rows_of])
+            offset = place_tiles(mine, offset, left)
+    place_tiles(mine, offset, small_ref[...])
+    pl.semaphore_wait(barrier, replicas - 1 + tensor_size - 1)
+    drain_one = dp_exchange(replicas, mine, wire, arrived, total, first_sems)
 
     def slot_copy(step, slot):
         peer = lax.rem(tensor_place + step, tensor_size)
         return pltpu.make_async_remote_copy(
             src_ref=small_slots.at[tensor_place],
             dst_ref=small_slots.at[slot],
-            send_sem=send_three.at[step],
-            recv_sem=recv_three.at[slot],
+            send_sem=send_small.at[step],
+            recv_sem=recv_small.at[slot],
             device_id=(dp_place, peer),
             device_id_type=MESH,
         )
 
-    def start(step, carry):
+    def start_small(step, carry):
         slot_copy(step, tensor_place).start()
         return carry
 
-    small_at = sum(ref.shape[1] for ref in lefts) // LANES
-    own_small = take_tiles(total, small_at, small_ref.shape[1])
+    own_small = take_tiles(total, offset, small_ref.shape[1])
     small_slots[tensor_place] = own_small
-    lax.fori_loop(1, tensor_size, start, 0)
+    lax.fori_loop(1, tensor_size, start_small, 0)
     offset = 0
-    for ref, basis_ref in zip(lefts, (bq_ref, bo_ref, bi_ref, bd_ref)):
-        rows = take_tiles(total, offset, ref.shape[1]) * (1.0 / replicas)
+    offset_two = 0
+    for basis_ref in (bq_ref, bo_ref, bd_ref, bi_ref):
+        rows = take_tiles(total, offset, basis_ref.shape[1]) * (1.0 / replicas)
         basis_ref[...] = orthonormal_rows(rows)
-        offset += ref.shape[1] // LANES
+        offset += basis_ref.shape[1] // LANES
+    drain_one()
+    for part in range(3):
+        right = right_factor(bq_ref[:, :block], qkv[part, :block])
+        for start in range(block, qkv.shape[1], block):
+            rows = slice(start, start + block)
+            right += right_factor(bq_ref[:, rows], qkv[part, rows])
+        offset_two = place_tiles(mine_two, offset_two, right)
+    for basis_ref, matrix in zip((bo_ref, bd_ref, bi_ref), (out, down, inw)):
+        rows_of = min(block, matrix.shape[0])
+        right = right_factor(basis_ref[:, :rows_of], matrix[:rows_of])
+        for start in range(rows_of, matrix.shape[0], rows_of):
+            rows = slice(start, start + rows_of)
+            right += right_factor(basis_ref[:, rows], matrix[rows])
+        offset_two = place_tiles(mine_two, offset_two, right)
+    drain_two = dp_exchange(
+        replicas, mine_two, wire_two, arrived_two, total_two, second_sems
+    )
 
     def collect(step, carry):
         peer = lax.rem(tensor_place + step, tensor_size)
@@ -382,79 +289,49 @@
     everyone = lax.fori_loop(1, tensor_size, collect, own_small)
     row_number = lax.broadcasted_iota(jnp.int32, everyone.shape, 0)
     sum_ref[...] = jnp.where(row_number < 6, everyone, own_small) * (1.0 / replicas)
-
-
-def bases_of(lefts, small, replicas, tensor_size):
-    rank_size = small.shape[0]
-    lanes = sum(left.shape[1] for left in lefts) + small.shape[1]
-    width = -(-lanes // (LANES * replicas)) * LANES
-    shapes = [left.shape for left in lefts] + [small.shape]
-    vmem = pl.BlockSpec(memory_space=pltpu.VMEM)
-    return pl.pallas_call(
-        partial(basis_kernel, replicas, tensor_size),
-        in_specs=[vmem] * 5,
-        out_specs=[vmem] * 5,
-        out_shape=[jax.ShapeDtypeStruct(shape, jnp.float32) for shape in shapes],
-        scratch_shapes=[
-            pltpu.VMEM((replicas, rank_size, width), jnp.float32),
-            pltpu.VMEM((replicas, rank_size, width), jnp.bfloat16),
-            pltpu.VMEM((replicas, rank_size, width), jnp.bfloat16),
-            pltpu.VMEM((replicas, rank_size, width), jnp.float32),
-            pltpu.VMEM((tensor_size,) + small.shape, jnp.float32),
-            pltpu.SemaphoreType.DMA((replicas,)),
-            pltpu.SemaphoreType.DMA((replicas,)),
-            pltpu.SemaphoreType.DMA((replicas,)),
-            pltpu.SemaphoreType.DMA((replicas,)),
-            pltpu.SemaphoreType.DMA((tensor_size,)),
-            pltpu.SemaphoreType.DMA((tensor_size,)),
-        ],
-        compiler_params=pltpu.CompilerParams(collective_id=1, has_side_effects=True),
-        name="bases",
-    )(*lefts, small)
-
-
-def right_sum_kernel(replicas, rq_ref, ro_ref, ri_ref, rd_ref, sq_ref, so_ref, si_ref, sd_ref,
-                     mine, wire, arrived, total, send_one, recv_one, send_two, recv_two):
-    mine[...] = jnp.zeros_like(mine)
-    greet(replicas, 1)
     offset = 0
     for part in range(3):
-        offset = place_tiles(mine, offset, rq_ref[part])
-    for ref in (ro_ref, ri_ref, rd_ref):
-        offset = place_tiles(mine, offset, ref[...])
-    dp_sum(replicas, mine, wire, arrived, total, send_one, recv_one, send_two, recv_two)
-    offset = 0
-    for part in range(3):
-        sq_ref[part] = take_tiles(total, offset, sq_ref.shape[2]) * (1.0 / replicas)
-        offset += sq_ref.shape[2] // LANES
-    for ref in (so_ref, si_ref, sd_ref):
-        ref[...] = take_tiles(total, offset, ref.shape[1]) * (1.0 / replicas)
+        rq_ref[part] = take_tiles(total_two, offset, rq_ref.shape[2]) * (1.0 / replicas)
+        offset += rq_ref.shape[2] // LANES
+    for ref in (ro_ref, rd_ref, ri_ref):
+        ref[...] = take_tiles(total_two, offset, ref.shape[1]) * (1.0 / replicas)
         offset += ref.shape[1] // LANES
-
-
-def right_sums(rights, replicas):
-    rank_size = rights[1].shape[0]
-    lanes = 3 * rights[0].shape[2] + sum(right.shape[1] for right in rights[1:])
-    width = -(-lanes // (LANES * replicas)) * LANES
+    drain_two()
+
+
+def compress(matrices, factors, small, replicas, tensor_size):
+    qkv, out, inw, down = matrices
+    rank_size = small.shape[0]
+    sizes = (qkv.shape[1], out.shape[0], inw.shape[0], down.shape[0])
+    right_shapes = [(3, rank_size, qkv.shape[2])] + [(rank_size, one.shape[1]) for one in matrices[1:]]
+    lanes_one = sum(sizes) + small.shape[1]
+    lanes_two = 3 * qkv.shape[2] + sum(one.shape[1] for one in matrices[1:])
+    scratch = [pltpu.VMEM(one.shape, jnp.float32) for one in matrices]
+    for lanes in (lanes_one, lanes_two):
+        shape = (replicas, rank_size, -(-lanes // (LANES * replicas)) * LANES)
+        scratch += [
+            pltpu.VMEM(shape, jnp.float32),
+            pltpu.VMEM(shape, jnp.bfloat16),
+            pltpu.VMEM(shape, jnp.bfloat16),
+            pltpu.VMEM(shape, jnp.float32),
+        ]
+    scratch += [pltpu.VMEM((tensor_size,) + small.shape, jnp.float32), pltpu.SemaphoreType.DMA((4,))]
+    scratch += [pltpu.SemaphoreType.DMA((replicas,))] * 8
+    scratch += [pltpu.SemaphoreType.DMA((tensor_size,))] * 2
     vmem = pl.BlockSpec(memory_space=pltpu.VMEM)
-    return pl.pallas_call(
-        partial(right_sum_kernel, replicas),
-        in_specs=[vmem] * 4,
-        out_specs=[vmem] * 4,
-        out_shape=[jax.ShapeDtypeStruct(right.shape, jnp.float32) for right in rights],
-        scratch_shapes=[
-            pltpu.VMEM((replicas, rank_size, width), jnp.float32),
-            pltpu.VMEM((replicas, rank_size, width), jnp.bfloat16),
-            pltpu.VMEM((replicas, rank_size, width), jnp.bfloat16),
-            pltpu.VMEM((replicas, rank_size, width), jnp.float32),
-            pltpu.SemaphoreType.DMA((replicas,)),
-            pltpu.SemaphoreType.DMA((replicas,)),
-            pltpu.SemaphoreType.DMA((replicas,)),
-            pltpu.SemaphoreType.DMA((replicas,)),
-        ],
-        compiler_params=pltpu.CompilerParams(collective_id=2, has_side_effects=True),
-        name="right_sums",
-    )(*rights)
+    shapes = [(rank_size, size) for size in sizes] + right_shapes + [small.shape]
+    outputs = pl.pallas_call(
+        partial(compress_kernel, replicas, tensor_size),
+        in_specs=[pl.BlockSpec(memory_space=pl.ANY)] * 4 + [vmem] * 5,
+        out_specs=[vmem] * 9,
+        out_shape=[jax.ShapeDtypeStruct(shape, jnp.float32) for shape in shapes],
+        scratch_shapes=scratch,
+        compiler_params=pltpu.CompilerParams(
+            collective_id=1, has_side_effects=True, vmem_limit_bytes=VMEM_GRANT
+        ),
+        name="compress",
+    )(*matrices, *factors, small)
+    return outputs[:4], outputs[4:8], outputs[8]
 
 
 def outer_of(basis_rows, right):
@@ -524,7 +401,7 @@
         in_specs=specs() * 3 + [whole(one) for one in bases] + [whole(one) for one in rights],
         out_specs=specs() * 4,
         out_shape=shapes * 4,
-        compiler_params=pltpu.CompilerParams(vmem_limit_bytes=48 << 20),
+        compiler_params=pltpu.CompilerParams(vmem_limit_bytes=VMEM_GRANT),
         name="update",
     )(*matrices, *momenta, *weights, *bases, *rights)
     return outputs[0:4], outputs[4:8], outputs[8:12], outputs[12:16]
@@ -643,7 +520,7 @@
             jax.ShapeDtypeStruct((length, slab), jnp.bfloat16),
             jax.ShapeDtypeStruct((slab // DH, length), jnp.float32),
         ],
-        compiler_params=pltpu.CompilerParams(vmem_limit_bytes=32 << 20),
+        compiler_params=pltpu.CompilerParams(vmem_limit_bytes=VMEM_GRANT),
         cost_estimate=pl.CostEstimate(
             flops=16 * length * length * slab, bytes_accessed=8 * length * slab,
             transcendentals=length * length * slab // DH,
@@ -733,7 +610,7 @@
             jax.ShapeDtypeStruct((2, slab), jnp.float32),
         ],
         input_output_aliases={8: 0},
-        compiler_params=pltpu.CompilerParams(vmem_limit_bytes=40 << 20),
+        compiler_params=pltpu.CompilerParams(vmem_limit_bytes=VMEM_GRANT),
         cost_estimate=pl.CostEstimate(
             flops=40 * length * length * slab, bytes_accessed=16 * length * slab,
             transcendentals=length * length * slab // DH,
@@ -1017,7 +894,7 @@
             pltpu.SemaphoreType.DMA((4,)),
         ],
         compiler_params=pltpu.CompilerParams(
-            collective_id=3, has_side_effects=True, vmem_limit_bytes=60 << 20
+            collective_id=3, has_side_effects=True, vmem_limit_bytes=VMEM_GRANT
         ),
         cost_estimate=pl.CostEstimate(
             flops=2 * share * width * (8 * units + 8 * piece_width),
@@ -1307,9 +1184,13 @@
     combined_in = grad_w_in + err_in[0]
     combined_down = grad_w_down + err_down[0]
     matrices = (combined_qkv, combined_out, combined_in, combined_down)
-    lefts = lefts_of(matrices, (basis_qkv.transpose(planes), basis_out, basis_in, basis_down))
-    *bases, small_sum = bases_of(lefts, small, replicas, tensor_size)
-    rights = right_sums(rights_of(matrices, bases), replicas)
+    bases, rights, small_sum = compress(
+        matrices,
+        (basis_qkv.transpose(planes), basis_out, basis_in, basis_down),
+        small,
+        replicas,
+        tensor_size,
+    )
     step_rate = 0.3 * math.sqrt(replicas / token_count)
     grads, errors, moments, news = update(
         matrices,

time: 364 us -> 338 us (0.929)
  local copies, waits for them, and re-layouts: 43.8 us -> 22.8 us
  waiting for transfers between devices: 69.7 us -> 52.1 us
  matrix products: 38.3 us -> 44 us
  other arithmetic: 10.5 us -> 15.2 us
    unnamed x162 -> x96, local copies, waits for them, and re-layouts: 31.8 us -> 8.41 us
    ppermute x18, waiting for transfers between devices: 69.7 us -> 52.1 us  [to(): lax.ppermute(values, 'tensor', [(place, place ^ step) for place in range(...]
    pallas_call x4 -> x1, Pallas kernels: 37.7 us -> 30.6 us  [compress(): pl.pallas_call(partial(compress_kernel, replicas, tensor_size), in_specs=...]
    pallas_call x2, Pallas kernels: 32 us -> 38.4 us  [attend_back(): pl.pallas_call(attend_back_kernel, grid_spec=grid_spec, out_shape=[jax.Sh...]
    pallas_call x2, Pallas kernels: 30.2 us -> 34.8 us  [attend(): pl.pallas_call(attend_kernel, grid_spec=grid_spec, out_shape=[jax.ShapeDt...]
    dot_general x8, matrix products: 20.8 us -> 25.2 us  [trans_times(): lax.dot_general(left_side, right_side, (((0,), (0,)), ((), ())), preferre...]
  transfers between devices with their start and end apart: 20 -> 20, of which waited for: 6 -> 5; matrix products, arithmetic and copies ran while one was open for 16% -> 20% of each run, Pallas kernels for 36% -> 39%
where the time goes in v3:
time: 338 us; the launch traced here: 334 us
  Pallas kernels  177 us (52%)
  waiting for transfers between devices  52.1 us (15%)
  matrix products  44 us (13%)
  local copies, waits for them, and re-layouts  22.8 us (7%)
  starting transfers between devices  20.7 us (6%)
  other arithmetic  15.2 us (4%)
    ppermute x18, waiting for transfers between devices, to(): lax.ppermute(values, 'tensor', [(place, place ^ step) for place in range(...  52.1 us
    pallas_call x1, Pallas kernels, ffn(): pl.pallas_call(ffn_kernel, in_specs=[vmem] * 4 + [anywhere] * 12 + [vmem]...  45.7 us
    pallas_call x2, Pallas kernels, attend_back(): pl.pallas_call(attend_back_kernel, grid_spec=grid_spec, out_shape=[jax.Sh...  38.4 us
    pallas_call x2, Pallas kernels, attend(): pl.pallas_call(attend_kernel, grid_spec=grid_spec, out_shape=[jax.ShapeDt...  34.8 us
    pallas_call x1, Pallas kernels, compress(): pl.pallas_call(partial(compress_kernel, replicas, tensor_size), in_specs=...  30.6 us
    pallas_call x1, Pallas kernels, update(): pl.pallas_call(partial(update_kernel, step_rate, out_steps), grid=(steps,...  27.7 us
    dot_general x8, matrix products, trans_times(): lax.dot_general(left_side, right_side, (((0,), (0,)), ((), ())), preferre...  25.2 us
    ppermute x18, starting transfers between devices, to(): lax.ppermute(values, 'tensor', [(place, place ^ step) for place in range(...  17.5 us
  transfers between devices with their start and end apart: 20, of which 5 were waited for; matrix products, arithmetic and copies ran while one was open for 20% of the time, Pallas kernels for 39%

profile of v3, /device:TPU:0, one launch (start us, length us, event | category | flops | bytes accessed | tf_op | source)
XLA Modules:
  0.0 333.5 jit_solution(14487892781098462316)
XLA Ops:
  0.7 3.0 collective-permute-start.3
  3.7 2.3 constant_dynamic-slice_fusion.1
  6.1 1.3 constant_dynamic-slice_fusion
  7.4 2.0 collective-permute-start.7
  9.6 7.4 %fusion.4.q_ref.k_ref.v_ref = bf16[3,2048,256]{2,1,0:T(8,128)(2,1)} fusion(f32[3]{0:T(128)S(1)} %copy-done.44, f32[3,256]{1,0:T(4,128)S(1)} %pad_maximum_fusion.6, bf16[2048,1024]{1,0:T(8,128)(2,1)} %tokens.1, bf16[1024,3,256]{2,0,1:T(8,128)(2,1)S(1)} %copy-done.6), kind=kOutput, calls=%fused_computation.8 | convolution fusion | flops 3225944064 | bytes 8915980 | tf_op jit(solution)/shard_map/td,gdn->gtn/dot_general | solution.py:1060
  17.5 1.1 pad_maximum_fusion.2
  18.8 1.3 broadcast_in_dim.32.seg_key_ref
  20.1 17.5 %attend.2 = (bf16[1024,256]{1,0:T(8,128)(2,1)}, f32[4,1024]{1,0:T(4,128)}) custom-call(s32[1]{0:T(128)} %bitcast.place_ref, bf16[3,2048,256]{2,1,0:T(8,128)(2,1)} %fusion.4.q_ref.k_ref.v_ref, bf16[3,2048,256]{2,1,0:T(8,128)(2,1)} %fusion.4.q_ref.k_ref.v_ref, bf16[3,2048,256]{2,1,0:T(8,128)(2,1)} %fusion.4.q_ref.k_ref.v_ref, ...), custom_call_target="tpu_custom_call" | custom-call | flops 4294967296 | bytes 2097152 | tf_op jit(solution)/shard_map/attend/pallas_call | solution.py:516
  37.5 1.9 constant_dynamic-slice_fusion.4
  39.9 1.3 collective-permute-start.9
  41.2 1.5 collective-permute-start.6
  42.7 18.2 %collective-permute-done.7.down_near = bf16[512,1024]{1,0:T(8,128)(2,1)} collective-permute-done((bf16[512,1024]{1,0:T(8,128)(2,1)S(1)}, bf16[512,1024]{1,0:T(8,128)(2,1)}, u32[]{:S(2)}, u32[]{:S(2)}) %collective-permute-start.7) | collective-permute-done | bytes 1048608 | tf_op jit(solution)/shard_map/ppermute | solution.py:1039
  61.0 1.7 collective-permute-start.8
  63.3 17.3 %attend.3 = (bf16[1024,256]{1,0:T(8,128)(2,1)}, f32[4,1024]{1,0:T(4,128)}) custom-call(s32[1]{0:T(128)} %bitcast.4.place_ref, bf16[3,2048,256]{2,1,0:T(8,128)(2,1)} %fusion.4.q_ref.k_ref.v_ref, bf16[3,2048,256]{2,1,0:T(8,128)(2,1)} %fusion.4.q_ref.k_ref.v_ref, bf16[3,2048,256]{2,1,0:T(8,128)(2,1)} %fusion.4.q_ref.k_ref.v_ref, ...), custom_call_target="tpu_custom_call" | custom-call | flops 4294967296 | bytes 2097152 | tf_op jit(solution)/shard_map/attend/pallas_call | solution.py:516
  80.5 1.1 constant_dynamic-slice_fusion.2
  82.2 1.5 collective-permute-start.1
  84.3 1.0 slice_bitcast_fusion.4
  85.4 5.4 %collective-permute-done.1.mixed_two = bf16[512,256]{1,0:T(8,128)(2,1)S(1)} collective-permute-done((bf16[512,256]{1,0:T(8,128)(2,1)S(1)}, bf16[512,256]{1,0:T(8,128)(2,1)S(1)}, u32[]{:S(2)}, u32[]{:S(2)}) %collective-permute-start.1) | collective-permute-done | bytes 262176 | tf_op jit(solution)/shard_map/ppermute | solution.py:1039
  90.7 3.0 collective-permute-done.2.mixed_three
  94.4 45.7 %ffn.1 = (bf16[512,1024]{1,0:T(8,128)(2,1)}, bf16[2,512,1024]{2,1,0:T(8,128)(2,1)}, bf16[2,512,2048]{2,1,0:T(8,128)(2,1)}, bf16[2,512,1024]{2,1,0:T(8,128)(2,1)}...) custom-call(bf16[512,256]{1,0:T(8,128)(2,1)} %get-tuple-element.135., ...), custom_call_target="tpu_custom_call" | custom-call | flops 19327352832 | bytes 31457280 | tf_op jit(solution)/shard_map/ffn/pallas_call | solution.py:863
  140.2 1.4 fusion.37
  141.5 2.0 collective-permute-start.11
  144.0 1.8 convolution_bitcast_fusion
  146.3 1.5 pad_maximum_fusion.1
  148.3 1.5 collective-permute-start.19
  149.8 3.8 %fusion.20 = bf16[1024,1024]{1,0:T(8,128)(2,1)} fusion(bf16[1024,1024]{1,0:T(8,128)(2,1)S(1)} %bitcast.147, bf16[1024,2048]{1,0:T(8,128)(2,1)S(1)} %bitcast.142), kind=kOutput, calls=%fused_computation.27 | convolution fusion | flops 2148532224 | bytes 6291456 | tf_op jit(solution)/shard_map/dot_general | solution.py:46
  153.6 3.8 %fusion.23 = bf16[1024,1024]{1,0:T(8,128)(2,1)} fusion(bf16[1024,1024]{1,0:T(8,128)(2,1)S(1)} %bitcast.144, bf16[1024,2048]{1,0:T(8,128)(2,1)S(1)} %bitcast.140), kind=kOutput, calls=%fused_computation.28 | convolution fusion | flops 2148532224 | bytes 6291456 | tf_op jit(solution)/shard_map/dot_general | solution.py:46
  157.4 1.2 collective-permute-start.17
  158.5 0.9 collective-permute-start.18
  161.1 1.9 broadcast_in_dim.35.old_ref
  162.9 19.1 %attend_back.2 = (bf16[3,2048,256]{2,1,0:T(8,128)(2,1)}, f32[2,256]{1,0:T(2,128)}) custom-call(s32[2]{0:T(128)} %pad_add_fusion.1.place_ref, bf16[3,2048,256]{2,1,0:T(8,128)(2,1)} %fusion.4.q_ref.k_ref.v_ref, bf16[3,2048,256]{2,1,0:T(8,128)(2,1)} %fusion.4.q_ref.k_ref.v_ref, ...), custom_call_target="tpu_custom_call", output_to_operand_aliasing={{0}: (8, {})} | custom-call | flops 10737418240 | bytes 4194304 | tf_op jit(solution)/shard_map/attend_back/pallas_call | solution.py:605
  182.1 19.3 %attend_back.3 = (bf16[3,2048,256]{2,1,0:T(8,128)(2,1)}, f32[2,256]{1,0:T(2,128)}) custom-call(s32[2]{0:T(128)} %pad_add_fusion.place_ref, bf16[3,2048,256]{2,1,0:T(8,128)(2,1)} %fusion.4.q_ref.k_ref.v_ref, bf16[3,2048,256]{2,1,0:T(8,128)(2,1)} %fusion.4.q_ref.k_ref.v_ref, ...), custom_call_target="tpu_custom_call", output_to_operand_aliasing={{0}: (8, {})} | custom-call | flops 10737418240 | bytes 4194304 | tf_op jit(solution)/shard_map/attend_back/pallas_call | solution.py:605
  201.3 6.0 %bitcast_convert_fusion = bf16[2048,1024]{1,0:T(8,128)(2,1)S(1)} fusion(bf16[3,2048,256]{2,1,0:T(8,128)(2,1)} %get-tuple-element.81, bf16[1024,3,256]{2,0,1:T(8,128)(2,1)} %param.28), kind=kOutput, calls=%fused_computation | convolution fusion | flops 3223322624 | bytes 8912896 | tf_op jit(solution)/shard_map/gtn,gdn->td/dot_general | solution.py:1105
  207.9 3.1 copy-done.33
  211.0 1.0 copy-done.3
  212.0 5.5 %bitcast_add_fusion.2.qkv_ref.refs_0_ = f32[3,1024,256]{2,1,0:T(8,128)} fusion(f32[1,1024,3,256]{3,1,2,0:T(8,128)S(1)} %copy-done.36, bf16[3,2048,256]{2,1,0:T(8,128)(2,1)S(1)} %copy-done.3, bf16[2048,1024]{1,0:T(8,128)(2,1)S(1)} %copy-done.33), kind=kOutput, calls=%fused_computation.9 | convolution fusion | flops 3222011904 | bytes 13631488 | tf_op jit(solution)/shard_map/td,gtn->gdn/dot_general | solution.py:1119
  218.7 1.2 collective-permute-start.16
  219.9 7.5 %bitcast_add_fusion.1.in_ref.refs_2_ = f32[1024,1024]{1,0:T(8,128)} fusion(f32[1,1024,1024]{2,1,0:T(8,128)S(1)} %copy-done.34, bf16[1024,1024]{1,0:T(8,128)(2,1)} %collective-permute-done.17, bf16[1024,1024]{1,0:T(8,128)(2,1)} %bitcast.146, bf16[1024,2048]{1,0:T(8,128)(2,1)S(1)} %bitcast.143), kind=kOutput, calls=%fused_computation.3 | convolution fusion | flops 2150629376 | bytes 14680064 | tf_op jit(solution)/shard_map/dot_general | solution.py:46
  227.4 23.7 %collective-permute-done.18 = bf16[1024,1024]{1,0:T(8,128)(2,1)} collective-permute-done((bf16[1024,1024]{1,0:T(8,128)(2,1)}, bf16[1024,1024]{1,0:T(8,128)(2,1)}, u32[]{:S(2)}, u32[]{:S(2)}) %collective-permute-start.18) | collective-permute-done | bytes 2097184 | tf_op jit(solution)/shard_map/ppermute | solution.py:1039
  251.1 6.0 %bitcast_add_fusion.down_ref.refs_3_ = f32[1024,1024]{1,0:T(8,128)} fusion(f32[1,1024,1024]{2,1,0:T(8,128)S(1)} %copy-done.35, bf16[1024,1024]{1,0:T(8,128)(2,1)} %collective-permute-done.18, bf16[1024,1024]{1,0:T(8,128)(2,1)S(1)} %bitcast.145, bf16[1024,2048]{1,0:T(8,128)(2,1)S(1)} %bitcast.141), kind=kOutput, calls=%fused_computation.2 | convolution fusion | flops 2150629376 | bytes 14680064 | tf_op jit(solution)/shard_map/dot_general | solution.py:46
  257.8 1.3 fusion.16
  259.2 1.1 collective-permute-start.14
  260.3 1.8 collective-permute-done.16
  262.1 1.5 fusion.33.out_ref.refs_1_
  263.6 30.6 %compress.1 = (f32[8,1024]{1,0:T(8,128)}, f32[8,256]{1,0:T(8,128)}, f32[8,1024]{1,0:T(8,128)}, f32[8,1024]{1,0:T(8,128)}, f32[3,8,256]{2,1,0:T(8,128)}, /*index=...) custom-call(f32[3,1024,256]{2,1,0:T(8,128)} %bitcast_add_fusion.2.qkv_ref.refs_0_, ...), custom_call_target="tpu_custom_call" | custom-call | tf_op jit(solution)/shard_map/compress/pallas_call | solution.py:323
  295.8 27.7 %update.1 = (f32[3,1024,256]{2,1,0:T(8,128)}, f32[256,1024]{1,0:T(8,128)}, f32[1024,1024]{1,0:T(8,128)}, f32[1024,1024]{1,0:T(8,128)}, f32[3,1024,256]{2,1,0:T(8...) custom-call(f32[3,1024,256]{2,1,0:T(8,128)} %bitcast_add_fusion.2.qk, ...), custom_call_target="tpu_custom_call" | custom-call | tf_op jit(solution)/shard_map/update/pallas_call | solution.py:398
  325.4 4.4 %fusion.19 = f32[512,1024]{1,0:T(8,128)} fusion(f32[512,1024]{1,0:T(8,128)S(1)} %copy-done.5, f32[2,512,1024]{2,1,0:T(8,128)} %copy-done.1, bf16[512,1024]{1,0:T(8,128)(2,1)} %collective-permute-done.14, bf16[2048,1024]{1,0:T(8,128)(2,1)} %copy-done.2, s32[]{:T(128)S(6)} %select_n.33), kind=kLoop, calls=%fused_computation.24 | loop fusion | flops 2621440 | bytes 8388612 | tf_op jit(solution)/shard_map/add | solution.py:1114
  329.8 1.0 copy.75
  (140 shorter events, 15.3 us)
Async XLA Ops:
  0.7 8.9 %copy-start.44 = (f32[3]{0:T(128)S(1)}, f32[3]{0:T(128)}, u32[]{:S(2)}) copy-start(f32[3]{0:T(128)} %constant.49.clone) | copy-start | bytes 40
  0.7 8.7 %copy-start.26 = (f32[2,256]{1,0:T(2,128)S(1)}, f32[2,256]{1,0:T(2,128)}, u32[]{:S(2)}) copy-start(f32[2,256]{1,0:T(2,128)} %param.29) | copy-start | bytes 6148
  0.7 8.9 %copy-start.6 = (bf16[1024,3,256]{2,0,1:T(8,128)(2,1)S(1)}, bf16[1024,3,256]{2,0,1:T(8,128)(2,1)}, u32[]{:S(2)}) copy-start(bf16[1024,3,256]{2,0,1:T(8,128)(2,1)} %param.28) | copy-start | bytes 4718596
  0.7 16.8 %collective-permute-start.3 = (bf16[256,1024]{1,0:T(8,128)(2,1)}, bf16[256,1024]{1,0:T(8,128)(2,1)}, u32[]{:S(2)}, u32[]{:S(2)}) collective-permute-start(bf16[256,1024]{1,0:T(8,128)(2,1)} %refs_9_.1), channel_id=1, source_target_pairs={{0,2},{1,3},{2,0},{3,1},{4,6},{5,7},{6,4},{7,5},{8,10},{9,11},{10,... | collective-permute-start | bytes 1572872 | tf_op jit(solution)/shard_map/ppermute | solution.py:1039
  6.0 35.2 %collective-permute-start.5 = (bf16[512,1024]{1,0:T(8,128)(2,1)}, bf16[512,1024]{1,0:T(8,128)(2,1)}, u32[]{:S(2)}, u32[]{:S(2)}) collective-permute-start(bf16[512,1024]{1,0:T(8,128)(2,1)} %constant_dynamic-slice_fusion.1), channel_id=1, source_target_pairs={{0,2},{1,3},{2,0},{3,1},{4,6},{5,7},{6,4},{7,5},{8,10},{9,11},{10,... | collective-permute-start | bytes 3145736 | tf_op jit(solution)/shard_map/ppermute | solution.py:1039
  7.4 53.5 %collective-permute-start.7 = (bf16[512,1024]{1,0:T(8,128)(2,1)S(1)}, bf16[512,1024]{1,0:T(8,128)(2,1)}, u32[]{:S(2)}, u32[]{:S(2)}) collective-permute-start(bf16[512,1024]{1,0:T(8,128)(2,1)S(1)} %constant_dynamic-slice_fusion), channel_id=1, source_target_pairs={{0,2},{1,3},{2,0},{3,1},{4,6},{5,7},{6,4},{7,5},{8,10},{9,11},{10,... | collective-permute-start | bytes 3145736 | tf_op jit(solution)/shard_map/ppermute | solution.py:1039
  9.5 7.4 %copy-start.20 = (s32[2,1024]{1,0:T(2,128)S(1)}, s32[2,1024]{1,0:T(2,128)}, u32[]{:S(2)}) copy-start(s32[2,1024]{1,0:T(2,128)} %param.27) | copy-start | bytes 24580
  9.6 8.0 %copy-start.4 = (bf16[256,1024]{1,0:T(8,128)(2,1)S(1)}, bf16[256,1024]{1,0:T(8,128)(2,1)}, u32[]{:S(2)}) copy-start(bf16[256,1024]{1,0:T(8,128)(2,1)} %refs_9_.1) | copy-start | bytes 1572868
  18.7 65.6 %collective-permute-start.4 = (bf16[2,256,1024]{2,1,0:T(8,128)(2,1)S(1)}, bf16[2,256,1024]{2,1,0:T(8,128)(2,1)S(1)}, u32[]{:S(2)}, u32[]{:S(2)}) collective-permute-start(bf16[2,256,1024]{2,1,0:T(8,128)(2,1)S(1)} %pad_maximum_fusion.2), channel_id=1, source_target_pairs={{0,1},{1,0},{2,3},{3,2},{4,5},{5,4},{6,7},{7,6},{8,9},{9,8},{10,11... | collective-permute-start | bytes 3145736 | tf_op jit(solution)/shard_map/ppermute | solution.py:1039
  20.1 19.8 %copy-start.25 = (f32[1024]{0:T(1024)S(1)}, f32[1024]{0:T(1024)}, u32[]{:S(2)}) copy-start(f32[1024]{0:T(1024)} %param.32) | copy-start | bytes 12292
  39.4 46.0 %collective-permute-start = (bf16[512,256]{1,0:T(8,128)(2,1)}, bf16[512,256]{1,0:T(8,128)(2,1)S(1)}, u32[]{:S(2)}, u32[]{:S(2)}) collective-permute-start(bf16[512,256]{1,0:T(8,128)(2,1)} %get-tuple-element.134), channel_id=1, source_target_pairs={{0,1},{1,0},{2,3},{3,2},{4,5},{5,4},{6,7},{7,6},{8,9},{9,8},{10,11... | collective-permute-start | bytes 786440 | tf_op jit(solution)/shard_map/ppermute | solution.py:1039
  39.9 42.3 %collective-permute-start.9 = (f32[1024]{0:T(1024)S(1)}, f32[1024]{0:T(1024)S(1)}, u32[]{:S(2)}, u32[]{:S(2)}) collective-permute-start(f32[1024]{0:T(1024)S(1)} %copy-done.25), channel_id=1, source_target_pairs={{0,2},{1,3},{2,0},{3,1},{4,6},{5,7},{6,4},{7,5},{8,10},{9,11},{10,... | collective-permute-start | bytes 12296 | tf_op jit(solution)/shard_map/ppermute | solution.py:1039
  41.2 52.5 %collective-permute-start.6 = (bf16[512,1024]{1,0:T(8,128)(2,1)}, bf16[512,1024]{1,0:T(8,128)(2,1)}, u32[]{:S(2)}, u32[]{:S(2)}) collective-permute-start(bf16[512,1024]{1,0:T(8,128)(2,1)} %collective-permute-done.5.in_near), channel_id=1, source_target_pairs={{0,4},{4,0},{8,12},{12,8},{16,20},{20,16},{24,28},{28,24},{1,5},{5... | collective-permute-start | bytes 3145736 | tf_op jit(solution)/shard_map/ppermute | solution.py:1044
  61.0 32.7 %collective-permute-start.8 = (bf16[512,1024]{1,0:T(8,128)(2,1)}, bf16[512,1024]{1,0:T(8,128)(2,1)}, u32[]{:S(2)}, u32[]{:S(2)}) collective-permute-start(bf16[512,1024]{1,0:T(8,128)(2,1)} %collective-permute-done.7.down_near), channel_id=1, source_target_pairs={{0,4},{4,0},{8,12},{12,8},{16,20},{20,16},{24,28},{28,24},{1,5},{5... | collective-permute-start | bytes 3145736 | tf_op jit(solution)/shard_map/ppermute | solution.py:1044
  82.2 8.5 %collective-permute-start.1 = (bf16[512,256]{1,0:T(8,128)(2,1)S(1)}, bf16[512,256]{1,0:T(8,128)(2,1)S(1)}, u32[]{:S(2)}, u32[]{:S(2)}) collective-permute-start(bf16[512,256]{1,0:T(8,128)(2,1)S(1)} %get-tuple-element.133), channel_id=1, source_target_pairs={{0,2},{1,3},{2,0},{3,1},{4,6},{5,7},{6,4},{7,5},{8,10},{9,11},{10,... | collective-permute-start | bytes 786440 | tf_op jit(solution)/shard_map/ppermute | solution.py:1039
  84.3 9.4 %collective-permute-start.2 = (bf16[512,256]{1,0:T(8,128)(2,1)S(1)}, bf16[512,256]{1,0:T(8,128)(2,1)S(1)}, u32[]{:S(2)}, u32[]{:S(2)}) collective-permute-start(bf16[512,256]{1,0:T(8,128)(2,1)S(1)} %get-tuple-element.132), channel_id=1, source_target_pairs={{0,3},{1,2},{2,1},{3,0},{4,7},{5,6},{6,5},{7,4},{8,11},{9,10},{10,... | collective-permute-start | bytes 786440 | tf_op jit(solution)/shard_map/ppermute | solution.py:1039
  85.4 8.4 %copy-start.10 = (bf16[512,256]{1,0:T(8,128)(2,1)}, bf16[512,256]{1,0:T(8,128)(2,1)S(1)}, u32[]{:S(2)}) copy-start(bf16[512,256]{1,0:T(8,128)(2,1)S(1)} %collective-permute-done.mixed_one) | copy-start | bytes 786436
  141.5 17.0 %collective-permute-start.11 = (bf16[512,256]{1,0:T(8,128)(2,1)S(1)}, bf16[512,256]{1,0:T(8,128)(2,1)S(1)}, u32[]{:S(2)}, u32[]{:S(2)}) collective-permute-start(bf16[512,256]{1,0:T(8,128)(2,1)S(1)} %get-tuple-element.128), channel_id=1, source_target_pairs={{0,3},{1,2},{2,1},{3,0},{4,7},{5,6},{6,5},{7,4},{8,11},{9,10},{10,... | collective-permute-start | bytes 786440 | tf_op jit(solution)/shard_map/ppermute | solution.py:1039
  143.5 15.9 %collective-permute-start.10 = (bf16[512,256]{1,0:T(8,128)(2,1)S(1)}, bf16[512,256]{1,0:T(8,128)(2,1)S(1)}, u32[]{:S(2)}, u32[]{:S(2)}) collective-permute-start(bf16[512,256]{1,0:T(8,128)(2,1)S(1)} %get-tuple-element.129), channel_id=1, source_target_pairs={{0,2},{1,3},{2,0},{3,1},{4,6},{5,7},{6,4},{7,5},{8,10},{9,11},{10,... | collective-permute-start | bytes 786440 | tf_op jit(solution)/shard_map/ppermute | solution.py:1039
  144.0 16.2 %collective-permute-start.12 = (bf16[512,256]{1,0:T(8,128)(2,1)S(1)}, bf16[512,256]{1,0:T(8,128)(2,1)S(1)}, u32[]{:S(2)}, u32[]{:S(2)}) collective-permute-start(bf16[512,256]{1,0:T(8,128)(2,1)S(1)} %get-tuple-element.127), channel_id=1, source_target_pairs={{0,1},{1,0},{2,3},{3,2},{4,5},{5,4},{6,7},{7,6},{8,9},{9,8},{10,11... | collective-permute-start | bytes 786440 | tf_op jit(solution)/shard_map/ppermute | solution.py:1039
  147.8 70.4 %collective-permute-start.15 = (f32[2,256,1024]{2,1,0:T(8,128)}, f32[2,256,1024]{2,1,0:T(8,128)S(1)}, u32[]{:S(2)}, u32[]{:S(2)}) collective-permute-start(f32[2,256,1024]{2,1,0:T(8,128)} %pad_maximum_fusion.1), channel_id=1, source_target_pairs={{0,1},{1,0},{2,3},{3,2},{4,5},{5,4},{6,7},{7,6},{8,9},{9,8},{10,11... | collective-permute-start | bytes 6291464 | tf_op jit(solution)/shard_map/ppermute | solution.py:1039
  148.3 9.1 %collective-permute-start.19 = (f32[1024]{0:T(1024)S(1)}, f32[1024]{0:T(1024)S(1)}, u32[]{:S(2)}, u32[]{:S(2)}) collective-permute-start(f32[1024]{0:T(1024)S(1)} %bitcast.132), channel_id=1, source_target_pairs={{0,2},{1,3},{2,0},{3,1},{4,6},{5,7},{6,4},{7,5},{8,10},{9,11},{10,... | collective-permute-start | bytes 12296 | tf_op jit(solution)/shard_map/ppermute | solution.py:1039
  157.4 62.5 %collective-permute-start.17 = (bf16[1024,1024]{1,0:T(8,128)(2,1)}, bf16[1024,1024]{1,0:T(8,128)(2,1)}, u32[]{:S(2)}, u32[]{:S(2)}) collective-permute-start(bf16[1024,1024]{1,0:T(8,128)(2,1)} %fusion.20), channel_id=1, source_target_pairs={{0,2},{1,3},{2,0},{3,1},{4,6},{5,7},{6,4},{7,5},{8,10},{9,11},{10,... | collective-permute-start | bytes 6291464 | tf_op jit(solution)/shard_map/ppermute | solution.py:1039
  158.5 92.5 %collective-permute-start.18 = (bf16[1024,1024]{1,0:T(8,128)(2,1)}, bf16[1024,1024]{1,0:T(8,128)(2,1)}, u32[]{:S(2)}, u32[]{:S(2)}) collective-permute-start(bf16[1024,1024]{1,0:T(8,128)(2,1)} %fusion.23), channel_id=1, source_target_pairs={{0,2},{1,3},{2,0},{3,1},{4,6},{5,7},{6,4},{7,5},{8,10},{9,11},{10,... | collective-permute-start | bytes 6291464 | tf_op jit(solution)/shard_map/ppermute | solution.py:1039
  201.3 6.6 %copy-start.36 = (f32[1,1024,3,256]{3,1,2,0:T(8,128)S(1)}, f32[1,1024,3,256]{3,1,2,0:T(8,128)}, u32[]{:S(2)}) copy-start(f32[1,1024,3,256]{3,1,2,0:T(8,128)} %param.36) | copy-start | bytes 9437188
  207.3 50.5 %copy-start.2 = (bf16[2048,1024]{1,0:T(8,128)(2,1)}, bf16[2048,1024]{1,0:T(8,128)(2,1)S(1)}, u32[]{:S(2)}) copy-start(bf16[2048,1024]{1,0:T(8,128)(2,1)S(1)} %bitcast_convert_fusion) | copy-start | bytes 12582916
  207.7 9.8 %copy-start.31 = (f32[2,256]{1,0:T(2,128)S(1)}, f32[2,256]{1,0:T(2,128)}, u32[]{:S(2)}) copy-start(f32[2,256]{1,0:T(2,128)} %get-tuple-element.90) | copy-start | bytes 6148
  207.7 9.7 %copy-start.32 = (f32[2,256]{1,0:T(2,128)S(1)}, f32[2,256]{1,0:T(2,128)}, u32[]{:S(2)}) copy-start(f32[2,256]{1,0:T(2,128)} %get-tuple-element.91) | copy-start | bytes 6148
  207.8 9.8 %copy-start.21 = (f32[6,1024]{1,0:T(8,128)S(1)}, f32[6,1024]{1,0:T(8,128)}, u32[]{:S(2)}) copy-start(f32[6,1024]{1,0:T(8,128)} %get-tuple-element.88) | copy-start | bytes 73732
  207.8 10.4 %copy-start.14 = (bf16[512,256]{1,0:T(8,128)(2,1)S(1)}, bf16[512,256]{1,0:T(8,128)(2,1)}, u32[]{:S(2)}) copy-start(bf16[512,256]{1,0:T(8,128)(2,1)} %copy-done.13) | copy-start | bytes 786436
  207.8 12.1 %copy-start.34 = (f32[1,1024,1024]{2,1,0:T(8,128)S(1)}, f32[1,1024,1024]{2,1,0:T(8,128)}, u32[]{:S(2)}) copy-start(f32[1,1024,1024]{2,1,0:T(8,128)} %param.38) | copy-start | bytes 12582916
  207.8 12.1 %copy-start.40 = (bf16[2,512,2048]{2,1,0:T(8,128)(2,1)S(1)}, bf16[2,512,2048]{2,1,0:T(8,128)(2,1)}, u32[]{:S(2)}) copy-start(bf16[2,512,2048]{2,1,0:T(8,128)(2,1)} %get-tuple-element.85) | copy-start | bytes 12582916
  207.8 49.3 %collective-permute-start.13 = (bf16[2,512,1024]{2,1,0:T(8,128)(2,1)S(1)}, bf16[2,512,1024]{2,1,0:T(8,128)(2,1)S(1)}, u32[]{:S(2)}, u32[]{:S(2)}) collective-permute-start(bf16[2,512,1024]{2,1,0:T(8,128)(2,1)S(1)} %pad_maximum_fusion), channel_id=1, source_target_pairs={{0,1},{1,0},{2,3},{3,2},{4,5},{5,4},{6,7},{7,6},{8,9},{9,8},{10,11... | collective-permute-start | bytes 6291464 | tf_op jit(solution)/shard_map/ppermute | solution.py:1039
  218.6 32.5 %copy-start.35 = (f32[1,1024,1024]{2,1,0:T(8,128)S(1)}, f32[1,1024,1024]{2,1,0:T(8,128)}, u32[]{:S(2)}) copy-start(f32[1,1024,1024]{2,1,0:T(8,128)} %param.39) | copy-start | bytes 12582916
  218.6 32.5 %copy-start.38 = (bf16[2,512,2048]{2,1,0:T(8,128)(2,1)S(1)}, bf16[2,512,2048]{2,1,0:T(8,128)(2,1)}, u32[]{:S(2)}) copy-start(bf16[2,512,2048]{2,1,0:T(8,128)(2,1)} %get-tuple-element.86) | copy-start | bytes 12582916
  218.6 32.4 %copy-start.42 = (bf16[2,512,1024]{2,1,0:T(8,128)(2,1)S(1)}, bf16[2,512,1024]{2,1,0:T(8,128)(2,1)}, u32[]{:S(2)}) copy-start(bf16[2,512,1024]{2,1,0:T(8,128)(2,1)} %get-tuple-element.87) | copy-start | bytes 6291460
  218.7 43.5 %collective-permute-start.16 = (bf16[256,1024]{1,0:T(8,128)(2,1)S(1)}, bf16[256,1024]{1,0:T(8,128)(2,1)S(1)}, u32[]{:S(2)}, u32[]{:S(2)}) collective-permute-start(bf16[256,1024]{1,0:T(8,128)(2,1)S(1)} %fusion.34), channel_id=1, source_target_pairs={{0,2},{1,3},{2,0},{3,1},{4,6},{5,7},{6,4},{7,5},{8,10},{9,11},{10,... | collective-permute-start | bytes 1572872 | tf_op jit(solution)/shard_map/ppermute | solution.py:1039
  259.2 66.2 %collective-permute-start.14 = (bf16[512,1024]{1,0:T(8,128)(2,1)}, bf16[512,1024]{1,0:T(8,128)(2,1)}, u32[]{:S(2)}, u32[]{:S(2)}) collective-permute-start(bf16[512,1024]{1,0:T(8,128)(2,1)} %fusion.16), channel_id=1, source_target_pairs={{0,2},{1,3},{2,0},{3,1},{4,6},{5,7},{6,4},{7,5},{8,10},{9,11},{10,... | collective-permute-start | bytes 3145736 | tf_op jit(solution)/shard_map/ppermute | solution.py:1039
  295.0 29.2 %copy-start.24 = (f32[1,1024]{1,0:T(1,128)}, f32[1,1024]{1,0:T(1,128)S(1)}, u32[]{:S(2)}) copy-start(f32[1,1024]{1,0:T(1,128)S(1)} %slice.66) | copy-start | bytes 12292
  295.7 27.8 %copy-start.27 = (f32[2,256]{1,0:T(2,128)}, f32[2,256]{1,0:T(2,128)S(1)}, u32[]{:S(2)}) copy-start(f32[2,256]{1,0:T(2,128)S(1)} %reshape_squeeze.3) | copy-start | bytes 6148
  295.7 27.8 %copy-start.30 = (f32[2,256]{1,0:T(2,128)S(1)}, f32[2,256]{1,0:T(2,128)}, u32[]{:S(2)}) copy-start(f32[2,256]{1,0:T(2,128)} %param.45) | copy-start | bytes 6148
  295.7 28.4 %copy-start.29 = (f32[1024]{0:T(1024)S(1)}, f32[1024]{0:T(1024)}, u32[]{:S(2)}) copy-start(f32[1024]{0:T(1024)} %param.48) | copy-start | bytes 12292
  295.7 29.0 %copy-start.19 = (f32[8,1024]{1,0:T(8,128)S(1)}, f32[8,1024]{1,0:T(8,128)}, u32[]{:S(2)}) copy-start(f32[8,1024]{1,0:T(8,128)} %get-tuple-element.101) | copy-start | bytes 98308
  295.8 29.0 %copy-start.22 = (f32[6,1024]{1,0:T(8,128)S(1)}, f32[6,1024]{1,0:T(8,128)}, u32[]{:S(2)}) copy-start(f32[6,1024]{1,0:T(8,128)} %vec_ref.1) | copy-start | bytes 73732
  295.8 29.0 %copy-start.23 = (f32[6,1024]{1,0:T(8,128)S(1)}, f32[6,1024]{1,0:T(8,128)}, u32[]{:S(2)}) copy-start(f32[6,1024]{1,0:T(8,128)} %param.50) | copy-start | bytes 73732
  295.8 29.6 %copy-start.5 = (f32[512,1024]{1,0:T(8,128)S(1)}, f32[512,1024]{1,0:T(8,128)}, u32[]{:S(2)}) copy-start(f32[512,1024]{1,0:T(8,128)} %get-tuple-element.82) | copy-start | bytes 6291460
  325.4 6.6 %copy-start.16 = (f32[8,1024]{1,0:T(8,128)S(1)}, f32[8,1024]{1,0:T(8,128)}, u32[]{:S(2)}) copy-start(f32[8,1024]{1,0:T(8,128)} %get-tuple-element.186.refs_18_) | copy-start | bytes 98308
  325.4 7.2 %copy-start.15 = (f32[8,1024]{1,0:T(8,128)S(1)}, f32[8,1024]{1,0:T(8,128)}, u32[]{:S(2)}) copy-start(f32[8,1024]{1,0:T(8,128)} %get-tuple-element.187.refs_19_) | copy-start | bytes 98308
  (17 other events, 71.4 us)
